TPU v7x, 512 devices: a whole 4x8x8 slice. The times are simulated.
512 devices in a mesh: req: 8 (over y), seq: 8 (over x, core), tp: 8 (over z).
Axes of the slice: x: 4, y: 8, z: 8, core: 2. Of those that a mesh axis runs over, the one named last changes fastest.
Arguments:
- tokens: bfloat16 [2048, 1024], P(('req', 'seq', 'tp')), may hold values from -3 to 3
- w_qkv: bfloat16 [1024, 3, 1024], P(None, None, 'tp'), may hold values from -0.1875 to 0.1875
- w_out: bfloat16 [1024, 1024], P('tp'), may hold values from -0.75 to 0.75
- variate_bias: float32 [2, 16], P(None, 'tp'), may hold values from -2 to 2
- attn_gain: float32 [1024], replicated, may hold values from 0.25 to 1.75
- ffn_gain: float32 [1024], replicated, may hold values from 0.25 to 1.75
- gate_up: bfloat16 [1024, 64, 128], P(None, ('seq', 'tp')), may hold values from -0.1875 to 0.1875
- w_down: bfloat16 [64, 64, 1024], P(('seq', 'tp')), may hold values from -0.09375 to 0.09375
- cache_keys: bfloat16 [1536, 256, 1024], P(('req', 'seq'), None, 'tp'), may hold values from -360 to 360
- cache_values: bfloat16 [1536, 256, 1024], P(('req', 'seq'), None, 'tp'), may hold values from -6 to 6
- cache_variate: int32 [1536, 256], P(('req', 'seq')), may hold values from 0 to 3
- new_variate: int32 [512, 4], P('req'), may hold values from 0 to 3
- piece_slot: int32 [512, 64], P('req'), may hold values from -1 to 191, as said below
- cache_len: int32 [512], P('req'), may hold values from 1 to 16384, as said below
Outputs:
- layer_out: bfloat16 [2048, 1024], P(('req', 'seq', 'tp'))
Inputs may be any that keep to these rules, and one draw needn't show every extreme that they name: `cache_len`: in each aligned block of 64 requests exactly one request has the most cached positions. `piece_slot`: entry p of request r is the slot within its group that holds cache positions p * 256 to p * 256 + 255; it is -1 exactly when p * 256 >= cache_len[r]; no slot of a group holds two pieces; slots that hold no piece are never read.
All inputs are finite; a program needn't handle non-finite values.
Results may differ from a plain program's by a relative error of at most 0.022.
Values may be sent and summed in bfloat16 or wider, within the bound.
No kernel may reach another device: no remote copies, remote signals or barrier semaphores. Data moves between devices by JAX's collectives and lax.ppermute only.
A program may use at most 64 MiB of HBM per device.

v0:
```python
import math

import jax
import jax.numpy as jnp
from jax import lax
from jax.sharding import PartitionSpec as P

HD = 64


EPSILON = 1e-05
MASKED_SCORE = -1e30


def joined(value, axis, combine):
    everything = jax.tree.map(lambda part: lax.all_gather(part, axis), value)
    first = jax.tree.map(lambda part: part[0], everything)

    def step(k, so_far):
        return combine(so_far, jax.tree.map(lambda part: part[k], everything))

    return lax.fori_loop(1, lax.axis_size(axis), step, first)


def rms_scale(rows, gain):
    rows32 = rows.astype(jnp.float32)
    mean_sq = jnp.mean(rows32 * rows32, axis=-1, keepdims=True)
    return (rows32 * lax.rsqrt(mean_sq + EPSILON) * gain).astype(jnp.bfloat16)


def rotate(vectors, positions):
    half_size = vectors.shape[-1] // 2
    inv_freq = 10000.0 ** (-jnp.arange(half_size, dtype=jnp.float32) / half_size)
    angles = positions[:, None] * inv_freq[None, :]
    cosine = jnp.cos(angles)[:, None, :]
    sine_part = jnp.sin(angles)[:, None, :]
    earlier = vectors[..., :half_size]
    latter = vectors[..., half_size:]
    return jnp.concatenate(
        [earlier * cosine - latter * sine_part, latter * cosine + earlier * sine_part], axis=-1
    )


def row_positions(lengths, step_count):
    offsets = jnp.arange(step_count, dtype=jnp.int32)
    return (lengths[:, None] + offsets[None, :]).reshape(-1).astype(jnp.float32)


def split_heads(projected, positions, head_size):
    row_count = projected.shape[0]
    parts = projected.reshape(row_count, 3, -1, head_size)
    queries = rotate(parts[:, 0], positions).astype(jnp.bfloat16)
    keys_new = rotate(parts[:, 1], positions).astype(jnp.bfloat16)
    values_new = parts[:, 2].astype(jnp.bfloat16)
    return (queries, keys_new, values_new)


def cache_partials(
    queries,
    cache_keys,
    cache_values,
    cache_variate,
    new_variate,
    piece_slot,
    cache_len,
    variate_bias,
    score_scale,
):
    slot_count, piece_len, _ = cache_keys.shape
    requests, step_count, heads, head_size = queries.shape
    max_pieces = piece_slot.shape[1]
    slot_ids = lax.axis_index("seq") * slot_count + jnp.arange(slot_count, dtype=jnp.int32)
    matches = piece_slot[None, :, :] == slot_ids[:, None, None]
    owners = jnp.any(matches, axis=2)
    piece_index = jnp.sum(
        jnp.where(matches, jnp.arange(max_pieces, dtype=jnp.int32)[None, None, :], 0), axis=(1, 2)
    )
    owner_len = jnp.sum(jnp.where(owners, cache_len[None, :], 0), axis=1)
    positions_in = (
        piece_index[:, None] * piece_len + jnp.arange(piece_len, dtype=jnp.int32)[None, :]
    )
    is_valid = positions_in < owner_len[:, None]
    picker = owners.astype(jnp.bfloat16)
    slot_query = jnp.dot(
        picker, queries.reshape(requests, -1), preferred_element_type=jnp.float32
    ).astype(jnp.bfloat16)
    slot_query = slot_query.reshape(slot_count, step_count, heads, head_size)
    slot_variate = jnp.sum(jnp.where(owners[:, :, None], new_variate[None], 0), axis=1)
    same_var = slot_variate[:, :, None] == cache_variate[:, None, :]
    bias_terms = jnp.where(
        same_var[:, None],
        variate_bias[0][None, :, None, None],
        variate_bias[1][None, :, None, None],
    )
    key_rows = cache_keys.reshape(slot_count, piece_len, heads, head_size)
    value_rows = cache_values.reshape(slot_count, piece_len, heads, head_size)
    scores = (
        jnp.einsum("sthd,slhd->shtl", slot_query, key_rows, preferred_element_type=jnp.float32)
        * score_scale
        + bias_terms
    )
    scores = jnp.where(is_valid[:, None, None, :], scores, MASKED_SCORE)
    slot_top = jnp.max(scores, axis=3)
    weights = jnp.where(is_valid[:, None, None, :], jnp.exp(scores - slot_top[..., None]), 0.0)
    slot_total = jnp.sum(weights, axis=3)
    slot_out = jnp.einsum(
        "shtl,slhd->shtd",
        weights.astype(jnp.bfloat16),
        value_rows,
        preferred_element_type=jnp.float32,
    )
    top_cache = jnp.max(
        jnp.where(owners[:, :, None, None], slot_top[:, None], MASKED_SCORE), axis=0
    )
    top_at = jnp.sum(jnp.where(owners[:, :, None, None], top_cache[None], 0.0), axis=1)
    factor = jnp.exp(slot_top - top_at)
    owner_f = owners.astype(jnp.float32)
    cache_total = jnp.einsum(
        "sr,sht->rht", owner_f, slot_total * factor, precision=lax.Precision.HIGHEST
    )
    cache_out = jnp.einsum(
        "sr,shtd->rhtd", owner_f, slot_out * factor[..., None], precision=lax.Precision.HIGHEST
    )
    return (top_cache, cache_total, cache_out)


def merge_pair(earlier, latter):
    joint_top = jnp.maximum(earlier[0], latter[0])
    left_scale = jnp.exp(earlier[0] - joint_top)
    right_scale = jnp.exp(latter[0] - joint_top)
    joint_total = earlier[1] * left_scale + latter[1] * right_scale
    joint_out = earlier[2] * left_scale[..., None] + latter[2] * right_scale[..., None]
    return (joint_top, joint_total, joint_out)


def finish(
    top_cache,
    cache_total,
    cache_out,
    queries,
    keys_new,
    values_new,
    new_variate,
    variate_bias,
    score_scale,
):
    step_count = new_variate.shape[1]
    new_scores = (
        jnp.einsum("rthd,ruhd->rhtu", queries, keys_new, preferred_element_type=jnp.float32)
        * score_scale
    )
    same_var = new_variate[:, :, None] == new_variate[:, None, :]
    new_scores = new_scores + jnp.where(
        same_var[:, None],
        variate_bias[0][None, :, None, None],
        variate_bias[1][None, :, None, None],
    )
    step_ids = jnp.arange(step_count, dtype=jnp.int32)
    causal = step_ids[:, None] >= step_ids[None, :]
    new_scores = jnp.where(causal[None, None], new_scores, MASKED_SCORE)
    row_top = jnp.maximum(top_cache, jnp.max(new_scores, axis=3))
    new_weights = jnp.where(causal[None, None], jnp.exp(new_scores - row_top[..., None]), 0.0)
    carried = jnp.exp(top_cache - row_top)
    row_total = cache_total * carried + jnp.sum(new_weights, axis=3)
    mixed_out = cache_out * carried[..., None] + jnp.einsum(
        "rhtu,ruhd->rhtd",
        new_weights.astype(jnp.bfloat16),
        values_new,
        preferred_element_type=jnp.float32,
    )
    attended = mixed_out / row_total[..., None]
    requests, heads, _, head_size = attended.shape
    return (
        jnp.transpose(attended, (0, 2, 1, 3))
        .reshape(requests * step_count, heads * head_size)
        .astype(jnp.bfloat16)
    )


def make_expand(gate_blocks, unit_block, row_block):
    block_count = gate_blocks.shape[1]
    expanded = jnp.einsum("nd,dbu->nbu", row_block, gate_blocks, preferred_element_type=jnp.float32)
    gate_part = expanded[:, :, :unit_block]
    up_part = expanded[:, :, unit_block:]
    return (
        (jax.nn.silu(gate_part) * up_part)
        .astype(jnp.bfloat16)
        .reshape(row_block.shape[0], block_count * unit_block)
    )


def on_device(
    tokens,
    w_qkv,
    w_out,
    variate_bias,
    attn_gain,
    ffn_gain,
    gate_up,
    w_down,
    cache_keys,
    cache_values,
    cache_variate,
    new_variate,
    piece_slot,
    cache_len,
):
    row_count = tokens.shape[0]
    requests, step_count = new_variate.shape
    score_scale = 1.0 / math.sqrt(HD)
    normed = rms_scale(tokens, attn_gain)
    qkv_width = w_qkv.shape[2]
    flat_qkv = w_qkv.reshape(w_qkv.shape[0], 3 * qkv_width)
    projected = jnp.dot(
        lax.all_gather(normed, ("seq", "tp"), axis=0, tiled=True),
        flat_qkv,
        preferred_element_type=jnp.float32,
    )
    queries, keys_new, values_new = split_heads(projected, row_positions(cache_len, step_count), HD)
    shape_four = (requests, step_count, qkv_width // HD, HD)
    queries = queries.reshape(shape_four)
    keys_new = keys_new.reshape(shape_four)
    values_new = values_new.reshape(shape_four)
    top_cache, cache_total, cache_out = cache_partials(
        queries,
        cache_keys,
        cache_values,
        cache_variate,
        new_variate,
        piece_slot,
        cache_len,
        variate_bias,
        score_scale,
    )
    top_cache, cache_total, cache_out = joined(
        (top_cache, cache_total, cache_out), "seq", merge_pair
    )
    attended = finish(
        top_cache,
        cache_total,
        cache_out,
        queries,
        keys_new,
        values_new,
        new_variate,
        variate_bias,
        score_scale,
    )
    seq_base = lax.axis_index("seq") * (row_count * lax.axis_size("tp"))
    picked = lax.dynamic_slice_in_dim(attended, seq_base, row_count * lax.axis_size("tp"), 0)
    attn_rows_sum = lax.psum_scatter(
        jnp.dot(picked, w_out, preferred_element_type=jnp.float32).astype(jnp.bfloat16),
        "tp",
        scatter_dimension=0,
        tiled=True,
    ).astype(jnp.float32)
    mid = tokens.astype(jnp.float32) + attn_rows_sum
    normed_mid = rms_scale(mid, ffn_gain)
    unit_block = w_down.shape[1]
    model_width = w_down.shape[2]
    hidden = make_expand(
        gate_up, unit_block, lax.all_gather(normed_mid, ("seq", "tp"), axis=0, tiled=True)
    )
    flat_down = w_down.reshape(w_down.shape[0] * unit_block, model_width)
    picked = hidden
    ffn_rows_sum = lax.psum_scatter(
        jnp.dot(picked, flat_down, preferred_element_type=jnp.float32),
        ("seq", "tp"),
        scatter_dimension=0,
        tiled=True,
    )
    return (mid + ffn_rows_sum).astype(jnp.bfloat16)


def solution(mesh):
    in_specs = (
        P(("req", "seq", "tp"), None),
        P(None, None, "tp"),
        P("tp", None),
        P(None, "tp"),
        P(),
        P(),
        P(None, ("seq", "tp"), None),
        P(("seq", "tp"), None, None),
        P(("req", "seq"), None, "tp"),
        P(("req", "seq"), None, "tp"),
        P(("req", "seq"), None),
        P("req", None),
        P("req", None),
        P("req"),
    )
    out_specs = P(("req", "seq", "tp"), None)
    return jax.shard_map(
        on_device, mesh=mesh, in_specs=in_specs, out_specs=out_specs, check_vma=False
    )
```

profile of v0, /device:TPU:56, one launch (start us, length us, event | category | flops | bytes accessed | tf_op | source)
XLA Modules:
  0.0 462.5 jit_solution(17933760203444792327)
XLA Ops:
  6.6 1.4 fusion.9
  8.0 1.3 compare_reduce_fusion
  10.8 1.3 slice_bitcast_fusion.3
  12.8 1.3 select_reduce_fusion.3
  16.5 55.1 %all-gather.3 = bf16[64,4,1024]{2,1,0:T(4,128)(2,1)S(1)} all-gather(bf16[1,4,1024]{2,1,0:T(4,128)(2,1)S(1)} %fusion.39), channel_id=1, replica_groups=mesh['req'=8,'seq'=8,'tp'=8] {'seq','tp'}, dimensions={0}, use_global_device_ids=true | all-gather | bytes 532480 | tf_op jit(solution)/shard_map/all_gather | solution.py:215
  76.4 1.7 fusion.47
  78.3 1.2 fusion.20
  80.5 1.5 convolution_multiply_fusion.1
  82.0 1.0 fusion.22
  85.9 13.6 %all-gather = f32[512,2,4]{2,1,0:T(2,128)S(1)} all-gather(f32[64,2,4]{2,1,0:T(2,128)S(1)} %copy.150), channel_id=2, replica_groups=mesh['req'=8,'seq'=8,'tp'=8] {'seq'}, dimensions={0}, use_global_device_ids=true | all-gather | bytes 18432 | tf_op jit(solution)/shard_map/all_gather | solution.py:16
  99.8 13.7 %all-gather.1 = f32[512,2,4]{2,1,0:T(2,128)S(1)} all-gather(f32[64,2,4]{2,1,0:T(2,128)S(1)} %copy.153), channel_id=3, replica_groups=mesh['req'=8,'seq'=8,'tp'=8] {'seq'}, dimensions={0}, use_global_device_ids=true | all-gather | bytes 18432 | tf_op jit(solution)/shard_map/all_gather | solution.py:16
  115.1 14.4 %while.19 = (s32[]{:T(128)}, f32[64,2,4]{0,2,1:T(4,128)S(1)}, f32[64,2,4]{0,2,1:T(4,128)S(1)}, f32[64,2,4,64]{3,2,1,0:T(4,128)S(1)}, f32[8,64,2,4]{1,3,2,0:T(4,1...) while((s32[]{:T(128)}, f32[64,2,4]{0,2,1:T(4,128)S(1)}, ...), condition=%wide.region_10.11_spmd, body=%wide.region_9.10_spmd.sunk | while | flops 101381 | bytes 684175 | solution.py:22
  117.4 1.0 constant_dynamic-slice_fusion.2
  119.5 1.0 constant_dynamic-slice_fusion.2
  121.6 1.0 constant_dynamic-slice_fusion.2
  123.6 1.0 constant_dynamic-slice_fusion.2
  127.7 1.0 constant_dynamic-slice_fusion.2
  131.6 1.3 dynamic-slice
  133.5 73.3 %all-reduce.5.cloned.1.call-done = bf16[32,1024]{1,0:T(8,128)(2,1)} async-done(((bf16[32,1024]{1,0:T(8,128)(2,1)}), bf16[32,1024]{1,0:T(8,128)(2,1)}) %all-reduce.5.cloned.1.call-update) | async-done | bytes 65552
  208.5 48.0 %all-gather.4 = bf16[64,4,1024]{2,1,0:T(4,128)(2,1)S(1)} all-gather(bf16[1,4,1024]{2,1,0:T(4,128)(2,1)S(1)} %fusion.38), channel_id=1, replica_groups=mesh['req'=8,'seq'=8,'tp'=8] {'seq','tp'}, dimensions={0}, use_global_device_ids=true | all-gather | bytes 532480 | tf_op jit(solution)/shard_map/all_gather | solution.py:262
  257.0 1.4 fusion.13
  258.4 1.3 dynamic-slice.2
  260.3 194.4 %all-reduce.7.cloned.1.call-done = f32[256,1024]{1,0:T(8,128)} async-done(((f32[256,1024]{1,0:T(8,128)}), f32[256,1024]{1,0:T(8,128)}) %all-reduce.7.cloned.1.call-update) | async-done | bytes 1048592
  454.6 1.4 fusion.34
  (142 shorter events, 28.5 us)
Async XLA Ops:
  6.5 124.2 %copy-start = (bf16[128,1024]{1,0:T(8,128)(2,1)S(1)}, bf16[128,1024]{1,0:T(8,128)(2,1)}, u32[]{:S(2)}) copy-start(bf16[128,1024]{1,0:T(8,128)(2,1)} %param.18) | copy-start | bytes 786436
  6.5 65.1 %copy-start.4 = (bf16[1024,3,128]{2,0,1:T(8,128)(2,1)S(1)}, bf16[1024,3,128]{2,0,1:T(8,128)(2,1)}, u32[]{:S(2)}) copy-start(bf16[1024,3,128]{2,0,1:T(8,128)(2,1)} %param.17) | copy-start | bytes 2359300
  6.5 107.4 %all-gather.7.cloned.1.call-start = ((), (), s32[]{:S(2)}) async-start(), calls=%async_computation | async-start | bytes 2359296 | tf_op jit(solution)/shard_map/all_gather | solution.py:16
  72.0 2.6 copy-start.1
  72.4 0.8 copy-start.3
  74.5 0.7 copy-start.16
  74.6 0.7 copy-start.17
  74.6 0.8 copy-start.12
  75.3 4.4 copy-start.2
  75.4 2.6 copy-start.10
  79.7 0.7 copy-start.11
  80.5 4.1 copy-start.8
  80.5 4.2 copy-start.7
  83.1 123.8 %all-reduce.5.cloned.1.call-start = ((), (), s32[]{:S(2)}) async-start(), calls=%async_computation.1 | async-start | bytes 131072
  85.4 28.3 %copy-start.13 = (s32[64,4]{0,1:T(4,128)S(1)}, s32[64,4]{0,1:T(4,128)}, u32[]{:S(2)}) copy-start(s32[64,4]{0,1:T(4,128)} %param.27) | copy-start | bytes 3076
  85.5 28.3 %copy-start.14 = (f32[2]{0:T(128)S(1)}, f32[2]{0:T(128)}, u32[]{:S(2)}) copy-start(f32[2]{0:T(128)} %get-tuple-element.258) | copy-start | bytes 28
  130.1 76.8 %copy-start.6 = (bf16[4,1024]{1,0:T(4,128)(2,1)S(1)}, bf16[4,1024]{1,0:T(4,128)(2,1)}, u32[]{:S(2)}) copy-start(bf16[4,1024]{1,0:T(4,128)(2,1)} %param.16) | copy-start | bytes 24580
  130.1 77.6 %copy-start.15 = (f32[1024]{0:T(1024)S(1)}, f32[1024]{0:T(1024)}, u32[]{:S(2)}) copy-start(f32[1024]{0:T(1024)} %param.21) | copy-start | bytes 12292
  130.5 126.2 %copy-start.5 = (bf16[1024,1,128]{2,0,1:T(8,128)(2,1)S(1)}, bf16[1024,1,128]{2,0,1:T(8,128)(2,1)}, u32[]{:S(2)}) copy-start(bf16[1024,1,128]{2,0,1:T(8,128)(2,1)} %param.22) | copy-start | bytes 786436
  130.6 126.4 %copy-start.9 = (bf16[1,64,1024]{2,1,0:T(8,128)(2,1)S(1)}, bf16[1,64,1024]{2,1,0:T(8,128)(2,1)}, u32[]{:S(2)}) copy-start(bf16[1,64,1024]{2,1,0:T(8,128)(2,1)} %param.23) | copy-start | bytes 393220
  131.5 323.1 %all-reduce.7.cloned.1.call-start = ((), (), s32[]{:S(2)}) async-start(), calls=%async_computation.2 | async-start | bytes 2097152
Sparse Core Ops, SparseCore 0:
  83.2 27.2 all-gather.6
  131.7 75.1 all-reduce.4
  258.5 196.1 all-reduce.6
where the time goes:
time: 464 us; the launch traced here: 463 us
  waiting for transfers between devices  268 us (58%)
  blocking collectives  130 us (28%)
  local copies, waits for them, and re-layouts  20.9 us (5%)
  other arithmetic  20.4 us (4%)
  between operations  14.9 us (3%)
  matrix products  7.97 us (2%)
    unnamed x5, waiting for transfers between devices  268 us
    all_gather x1, blocking collectives, on_device(): lax.all_gather(normed, ('seq', 'tp'), axis=0, tiled=True)  55.1 us
    all_gather x1, blocking collectives, on_device(): lax.all_gather(normed_mid, ('seq', 'tp'), axis=0, tiled=True)  48 us
    all_gather x2, blocking collectives, joined(): everything = jax.tree.map(lambda part: lax.all_gather(part, axis), value)  27.3 us
  transfers between devices with their start and end apart: 3, of which 2 were waited for; matrix products, arithmetic and copies ran while one was open for 1% of the time, Pallas kernels for 0%

commit v1 on v0

v1 whole, which is shorter than its diff:
```python
import math

import jax
import jax.numpy as jnp
import numpy as np
from jax import lax
from jax.experimental import pallas as pl
from jax.experimental.pallas import tpu as pltpu
from jax.sharding import PartitionSpec as P

HD = 64
EPSILON = 1e-05
MASKED_SCORE = -1e30
FAR = -1e38
LANES = 128
INTERPRET = False


def exchange(pieces, axes):
    return lax.all_to_all(pieces, axes, 0, 0, tiled=True)


def copies(block, axes):
    return jnp.broadcast_to(block[None], (lax.axis_size(axes), *block.shape))


def swapped(blocks, partner):
    return lax.ppermute(blocks, "seq", list(enumerate(partner)))


def in_vmem(count):
    return [pl.BlockSpec(memory_space=pltpu.VMEM)] * count


def in_smem(count):
    return [pl.BlockSpec(memory_space=pltpu.SMEM)] * count


def stay_in_hbm(array):
    return array if INTERPRET else pltpu.with_memory_space_constraint(array, pltpu.HBM)


def kernel_call(body, out_shape, in_specs, name, moved, loads=(), small=(), scratch=()):
    many = isinstance(out_shape, (list, tuple))
    outs = len(out_shape) if many else 1
    held = [pltpu.VMEM(a.shape, a.dtype) for a in loads] + [
        pltpu.SMEM(a.shape, a.dtype) for a in small
    ]
    count, plain = len(held), len(in_specs)

    def run(*refs):
        ins, refs = refs[:plain], refs[plain:]
        sources, refs = refs[:count], refs[count:]
        results, refs = refs[:outs], refs[outs:]
        buffers, refs = refs[:count], refs[count:]
        sems, rest = refs[:count], refs[count:]
        moves = [pltpu.make_async_copy(*each) for each in zip(sources, buffers, sems)]
        for move in moves:
            move.start()

        def arrive(*which):
            for i in which or range(count):
                moves[i].wait()

        body(arrive, *ins, *buffers, *results, *rest)

    call = pl.pallas_call(
        run,
        out_shape=out_shape,
        in_specs=list(in_specs) + [pl.BlockSpec(memory_space=pltpu.HBM)] * count,
        out_specs=in_vmem(outs) if many else in_vmem(1)[0],
        scratch_shapes=held + [pltpu.SemaphoreType.DMA(())] * count + list(scratch),
        name=name,
        interpret=INTERPRET,
        compiler_params=pltpu.CompilerParams(vmem_limit_bytes=16 << 20),
        cost_estimate=pl.CostEstimate(flops=300 * moved, bytes_accessed=moved, transcendentals=0),
    )
    return lambda *ins: call(*ins, *[stay_in_hbm(a) for a in (*loads, *small)])


def iota(shape, dim):
    return lax.broadcasted_iota(jnp.int32, shape, dim)


def matmul(a, b):
    return jnp.dot(a, b, preferred_element_type=jnp.float32)


def matmul_t(a, b):
    return lax.dot_general(a, b, (((1,), (1,)), ((), ())), preferred_element_type=jnp.float32)


def scaled_rows(rows, gain):
    mean_sq = jnp.mean(rows * rows, axis=-1, keepdims=True)
    return (rows * lax.rsqrt(mean_sq + EPSILON) * gain).astype(jnp.bfloat16)


def stacked(ref):
    return jnp.concatenate([ref[i].astype(jnp.float32) for i in range(ref.shape[0])], axis=0)


def pack_body(arrive, gate_ref, down_ref, out_ref):
    arrive()
    depth = gate_ref.shape[0]
    units = down_ref.shape[0]
    out_ref[0, :depth] = gate_ref[...]
    for c in range(down_ref.shape[1] // LANES):
        at = depth + units * c
        out_ref[0, at : at + units] = down_ref[:, LANES * c : LANES * (c + 1)]


def join_body(arrive, first_ref, second_ref, after_ref, out_ref):
    count = first_ref.shape[0]
    out_ref[:count] = first_ref[...]
    out_ref[count:] = second_ref[...]


def joined(first, second, after):
    return kernel_call(
        join_body,
        jax.ShapeDtypeStruct((2 * first.shape[0], *first.shape[1:]), first.dtype),
        in_vmem(2) + [pl.BlockSpec(memory_space=pl.ANY)],
        "join",
        moved=4 << 20,
    )(first, second, after)


def project_body(arrive, token_ref, cos_ref, sin_ref, gain_ref, w_ref, q_ref, k_ref, v_ref):
    arrive(0)
    normed = scaled_rows(stacked(token_ref), gain_ref[...])
    cosine, sine = stacked(cos_ref), stacked(sin_ref)
    first_half = iota(cosine.shape, 1) % HD < HD // 2

    def rotate(part):
        partner = jnp.where(
            first_half,
            pltpu.roll(part, LANES - HD // 2, 1),
            pltpu.roll(part, HD // 2, 1),
        )
        return (part * cosine + partner * sine).astype(jnp.bfloat16)

    arrive(1)
    queries = rotate(matmul(normed, w_ref[0]))
    for i in range(q_ref.shape[0]):
        q_ref[i] = queries
    k_ref[...] = rotate(matmul(normed, w_ref[1]))
    v_ref[...] = matmul(normed, w_ref[2]).astype(jnp.bfloat16)


def fresh_part(steps, scale, packed, q_ref, k_ref, v_ref, bias_ref, out_ref, lse_ref):
    queries = q_ref[0]
    rows = queries.shape[0]
    packed = jnp.concatenate(
        [jnp.broadcast_to(packed[i : i + 1, :rows], (steps, rows)) for i in range(packed.shape[0])],
        axis=0,
    )
    low_lanes = iota((rows, LANES), 1) < HD
    split = [
        jnp.where(low_lanes, queries, jnp.zeros_like(queries)),
        jnp.where(low_lanes, jnp.zeros_like(queries), queries),
    ]
    row_id, col_id = iota((rows, rows), 0), iota((rows, rows), 1)
    allowed = (row_id // steps == col_id // steps) & (row_id % steps >= col_id % steps)
    same = (packed >> (2 * (row_id % steps))) & 3 == (packed >> (2 * (col_id % steps))) & 3
    outs, lses = [], []
    for head in range(2):
        scores = matmul_t(split[head], k_ref[...]) * scale
        scores = scores + jnp.where(same, bias_ref[0, head], bias_ref[1, head])
        scores = jnp.where(allowed, scores, MASKED_SCORE)
        top = jnp.max(scores, axis=1, keepdims=True)
        weights = jnp.where(allowed, jnp.exp(scores - top), 0.0)
        total = jnp.sum(weights, axis=1, keepdims=True)
        outs.append(matmul(weights.astype(jnp.bfloat16), v_ref[...]) / total)
        lses.append(top + jnp.log(total))
    out_ref[...] = jnp.where(low_lanes, outs[0], outs[1])
    lse_ref[...] = jnp.where(low_lanes, lses[0], lses[1])


def prepare_body(
    steps,
    slots,
    scale,
    arrive,
    seq_ref,
    q_ref,
    k_ref,
    v_ref,
    slot_ref,
    len_ref,
    variate_ref,
    cached_variate_ref,
    bias_ref,
    pick_ref,
    place_ref,
    same_ref,
    bias_mask_ref,
    fresh_ref,
    fresh_lse_ref,
    packed_ref,
):
    requests, pieces = slot_ref.shape
    piece_len = cached_variate_ref.shape[1]
    group = 2 * steps
    rows = slots * group
    arrive()
    table = slot_ref[...]
    packed_row = variate_ref[0:1, :]
    for t in range(1, steps):
        packed_row = packed_row + (variate_ref[t : t + 1, :] << (2 * t))
    columns = jnp.where(iota((8, requests), 0) == 0, packed_row, len_ref[...])
    columns = jnp.transpose(columns.astype(jnp.float32)).astype(jnp.int32)
    packed_variate, length = columns[:, 0:1], columns[:, 1:2]
    packed_ref[...] = jnp.broadcast_to(packed_variate, (requests, LANES))
    own = requests // (requests * steps // q_ref.shape[1])
    packed = packed_ref[pl.ds(pl.multiple_of(seq_ref[0] * own, own), own), :]
    fresh_part(steps, scale, packed, q_ref, k_ref, v_ref, bias_ref, fresh_ref, fresh_lse_ref)

    live = jnp.clip(length - piece_len * iota((requests, pieces), 1), 0, piece_len)
    code = (iota((requests, pieces), 0) << 17) + (packed_variate << 9) + live
    code = code.astype(jnp.float32)
    base = seq_ref[0] * slots
    found = []
    for s in range(slots):
        hit = jnp.where(table == base + s, code, -1.0)
        hit = jnp.max(jnp.max(hit, axis=0, keepdims=True), axis=1, keepdims=True)
        found.append(jnp.broadcast_to(hit, (group, LANES)))
    found = jnp.concatenate(found, axis=0)
    found_lane = jnp.transpose(found)[0:1, :].astype(jnp.int32)
    found = found[:, 0:1].astype(jnp.int32)
    owned = found >= 0
    owner = jnp.where(owned, found >> 17, -1)
    owner_lane = jnp.where(found_lane >= 0, found_lane >> 17, -1)
    row_in = iota((rows, 1), 0) % group
    step_row = row_in % steps
    lane_in = iota((1, rows), 1) % group

    wide = (rows, requests * steps)
    pick_ref[...] = jnp.where(
        iota(wide, 1) == jnp.where(owned, owner * steps + step_row, -1), 1.0, 0.0
    ).astype(jnp.bfloat16)
    tall = (requests * steps, rows)
    place_ref[...] = jnp.where(
        iota(tall, 0) == jnp.where(owner_lane >= 0, owner_lane * steps + lane_in % steps, -1),
        1.0,
        0.0,
    ).astype(jnp.bfloat16)
    same_ref[...] = jnp.where((owner == owner_lane) & (row_in == lane_in), 0.0, FAR)

    limit = jnp.where(owned, found & 511, 0)
    variate = (found >> (9 + 2 * step_row)) & 3
    first_head = row_in < steps
    same_bias = jnp.where(first_head, bias_ref[0, 0], bias_ref[0, 1])
    other_bias = jnp.where(first_head, bias_ref[1, 0], bias_ref[1, 1])
    cached = jnp.concatenate(
        [
            jnp.broadcast_to(cached_variate_ref[s : s + 1, :], (group, piece_len))
            for s in range(slots)
        ],
        axis=0,
    )
    biases = jnp.where(variate == cached, same_bias, other_bias)
    bias_mask_ref[...] = jnp.where(iota((rows, piece_len), 1) < limit, biases, MASKED_SCORE)


def two_terms(value):
    high = value.astype(jnp.bfloat16)
    return high, (value - high.astype(jnp.float32)).astype(jnp.bfloat16)


def cache_body(
    steps, scale, arrive, q_ref, pick_ref, place_ref, same_ref, bias_mask_ref, k_ref, v_ref, out_ref
):
    slots = k_ref.shape[0]
    group = 2 * steps
    rows = slots * group
    devices = out_ref.shape[0]
    span = out_ref.shape[1] // 2
    all_queries = jnp.concatenate([q_ref[i] for i in range(devices)], axis=0)
    picked = matmul(pick_ref[...], all_queries)
    row_head = iota((rows, LANES), 0) % group // steps
    head_match = row_head == iota((rows, LANES), 1) // HD
    picked = jnp.where(head_match, picked, 0.0)
    scores = jnp.concatenate(
        [
            matmul_t(picked[group * s : group * (s + 1)].astype(jnp.bfloat16), k_ref[s])
            for s in range(slots)
        ],
        axis=0,
    )
    bias_mask = bias_mask_ref[...]
    live = bias_mask > 0.5 * MASKED_SCORE
    scores = jnp.where(live, scores * scale + bias_mask, MASKED_SCORE)
    slot_top = jnp.max(scores, axis=1, keepdims=True)
    top_lane = jnp.transpose(jnp.broadcast_to(slot_top, (rows, LANES)))[0:1, :]
    row_top = jnp.max(top_lane + same_ref[...], axis=1, keepdims=True)
    weights = jnp.where(live, jnp.exp(scores - row_top), 0.0)
    total = jnp.sum(weights, axis=1, keepdims=True)
    arrive(0)
    mixed = jnp.concatenate(
        [
            matmul(weights[group * s : group * (s + 1)].astype(jnp.bfloat16), v_ref[s])
            for s in range(slots)
        ],
        axis=0,
    )
    both = jnp.concatenate(
        [jnp.where(head_match, mixed, 0.0), jnp.where(head_match, total, 0.0)], axis=1
    )
    high, low = two_terms(both)
    place = place_ref[...]
    summed = matmul(place, high) + matmul(place, low)
    out_sum, total_sum = summed[:, :LANES], summed[:, LANES:]
    lane_head = iota((1, rows), 1) % group // steps
    placed = place.astype(jnp.float32) > 0.5
    tops = [
        jnp.max(jnp.where(placed & (lane_head == h), top_lane, MASKED_SCORE), axis=1, keepdims=True)
        for h in range(2)
    ]
    low_lanes = iota(out_sum.shape, 1) < HD
    top = jnp.where(low_lanes, tops[0], tops[1])
    some = total_sum > 0.0
    safe_total = jnp.where(some, total_sum, 1.0)
    averaged = jnp.where(some, out_sum / safe_total, 0.0).astype(jnp.bfloat16)
    lse = jnp.where(some, top + jnp.log(safe_total), MASKED_SCORE)
    lse_high = lse.astype(jnp.bfloat16).astype(jnp.float32)
    rest = lse - lse_high
    lse_mid = rest.astype(jnp.bfloat16).astype(jnp.float32)
    place_in = iota(out_sum.shape, 1) % HD
    coded = jnp.where(
        place_in == 0,
        lse_high,
        jnp.where(place_in == 1, lse_mid, jnp.where(place_in == 2, rest - lse_mid, 0.0)),
    ).astype(jnp.bfloat16)
    for d in range(devices):
        out_ref[d, :span] = averaged[span * d : span * (d + 1)]
        out_ref[d, span:] = coded[span * d : span * (d + 1)]


def finish_body(arrive, part_ref, fresh_ref, fresh_lse_ref, w_ref, out_ref):
    devices = part_ref.shape[0]
    span = part_ref.shape[1] // 2
    source, lane = iota((LANES, LANES), 0), iota((LANES, LANES), 1)
    decode = jnp.where((source // HD == lane // HD) & (source % HD < 3), 1.0, 0.0)
    decode = decode.astype(jnp.bfloat16)
    lses = [matmul(part_ref[d, span:], decode) for d in range(devices)]
    top = fresh_lse_ref[...]
    for lse in lses:
        top = jnp.maximum(top, lse)
    weight = jnp.exp(fresh_lse_ref[...] - top)
    total = weight
    mixed = weight * fresh_ref[...]
    for d in range(devices):
        weight = jnp.exp(lses[d] - top)
        total = total + weight
        mixed = mixed + weight * part_ref[d, :span].astype(jnp.float32)
    attended = (mixed / total).astype(jnp.bfloat16)
    arrive()
    partial = matmul(attended, w_ref[...]).astype(jnp.bfloat16)
    for d in range(out_ref.shape[0]):
        out_ref[d] = partial


def feed(normed, w_ref):
    rows, width = normed.shape
    blocks = [w_ref.at[i] for i in range(w_ref.shape[0])]
    low_lanes = iota((rows, LANES), 1) < HD
    halves = []
    for s, block in enumerate(blocks):
        expanded = matmul(normed, block[:width])
        gate = expanded / (1.0 + jnp.exp(-expanded))
        part = gate * pltpu.roll(expanded, HD, 1)
        if s % 2 == 0:
            halves.append(part)
        else:
            halves[-1] = jnp.where(low_lanes, halves[-1], pltpu.roll(part, HD, 1))
    hidden = jnp.concatenate(halves, axis=1).astype(jnp.bfloat16)
    parts = []
    for c in range(width // LANES):
        at = width + HD * c
        weights = jnp.concatenate([block[at : at + HD] for block in blocks], axis=0)
        parts.append(matmul(hidden, weights))
    return parts


def feed_own_body(arrive, part_ref, token_ref, w_ref, gain_ref, out_ref, normed_ref, mid_ref):
    mid = part_ref[0].astype(jnp.float32)
    for d in range(1, part_ref.shape[0]):
        mid = mid + part_ref[d].astype(jnp.float32)
    mid = mid + stacked(token_ref)
    own = mid_ref.shape[1]
    for d in range(mid_ref.shape[0]):
        mid_ref[d] = mid[own * d : own * (d + 1)]
    arrive()
    normed = scaled_rows(mid, gain_ref[...])
    normed_ref[...] = normed
    for c, part in enumerate(feed(normed, w_ref)):
        out_ref[:, LANES * c : LANES * (c + 1)] = part


def feed_near_body(arrive, normed_ref, w_ref, part_ref, out_ref):
    own = out_ref.shape[1]
    for c, part in enumerate(feed(normed_ref[...], w_ref)):
        lanes = slice(LANES * c, LANES * (c + 1))
        part = part + part_ref[:, lanes]
        for d in range(out_ref.shape[0]):
            out_ref[d, :, lanes] = part[own * d : own * (d + 1)].astype(jnp.bfloat16)


def last_body(arrive, index_ref, part_ref, mid_ref, out_ref):
    total = mid_ref[index_ref[0]]
    summed = part_ref[0].astype(jnp.float32)
    for d in range(1, part_ref.shape[0]):
        summed = summed + part_ref[d].astype(jnp.float32)
    out_ref[...] = (total + summed).astype(jnp.bfloat16)


def rotation_tables(lengths, steps):
    half = HD // 2
    lane = np.arange(LANES)
    inv_freq = (10000.0 ** (-(lane % half) / half)).astype(np.float32)
    sign = np.where(lane % HD < half, -1.0, 1.0).astype(np.float32)
    offsets = jnp.arange(steps, dtype=jnp.int32)
    positions = (lengths[:, None, None] + offsets[None, :, None]).astype(jnp.float32)
    angles = positions * inv_freq
    return jnp.cos(angles), jnp.sin(angles) * sign


def on_device(
    tokens,
    w_qkv,
    w_out,
    variate_bias,
    attn_gain,
    ffn_gain,
    gate_up,
    w_down,
    cache_keys,
    cache_values,
    cache_variate,
    new_variate,
    piece_slot,
    cache_len,
):
    row_count, width = tokens.shape
    requests, steps = new_variate.shape
    slots, piece_len, lanes = cache_keys.shape
    seqs, tps = lax.axis_size("seq"), lax.axis_size("tp")
    rows = row_count * tps
    own_requests = rows // steps
    scale = 1.0 / math.sqrt(HD)
    bf16, f32 = jnp.bfloat16, jnp.float32
    shape = jax.ShapeDtypeStruct
    seq_at = lax.axis_index("seq")
    tp_at = lax.axis_index("tp").astype(jnp.int32).reshape(1)

    row_tokens = exchange(copies(tokens, "tp"), "tp")

    blocks, units = w_down.shape[:2]
    ffn_weights = kernel_call(
        pack_body,
        shape((1, width + units * width // lanes, lanes), bf16),
        [],
        "pack",
        moved=1 << 20,
        loads=[gate_up.reshape(width, lanes), w_down.reshape(units, width)],
    )()
    ffn_next = swapped(ffn_weights, [2, 3, 0, 1, 6, 7, 4, 5])

    own_len = lax.dynamic_slice_in_dim(cache_len, seq_at * own_requests, own_requests, 0)
    cosine, sine = rotation_tables(own_len, steps)
    queries, keys_new, values_new = kernel_call(
        project_body,
        [shape((seqs, rows, lanes), bf16), shape((rows, lanes), bf16), shape((rows, lanes), bf16)],
        in_vmem(3),
        "project",
        moved=1 << 20,
        loads=[attn_gain[None, :], w_qkv.transpose(1, 0, 2)],
    )(row_tokens, cosine, sine)
    all_queries = exchange(queries, "seq")

    slot_rows = 2 * steps * slots
    pick, place, same, bias_mask, fresh, fresh_lse = kernel_call(
        lambda *refs: prepare_body(steps, slots, scale, *refs),
        [
            shape((slot_rows, requests * steps), bf16),
            shape((requests * steps, slot_rows), bf16),
            shape((slot_rows, slot_rows), f32),
            shape((slot_rows, piece_len), f32),
            shape((rows, lanes), f32),
            shape((rows, lanes), f32),
        ],
        in_smem(1) + in_vmem(3),
        "prepare",
        moved=1 << 20,
        loads=[piece_slot, cache_len[None, :], new_variate.T, cache_variate],
        small=[variate_bias],
        scratch=[pltpu.VMEM((requests, lanes), jnp.int32)],
    )(seq_at.astype(jnp.int32).reshape(1), queries, keys_new, values_new)

    partial = kernel_call(
        lambda *refs: cache_body(steps, scale, *refs),
        shape((seqs, 2 * rows, lanes), bf16),
        in_vmem(6),
        "cache",
        moved=4 << 20,
        loads=[cache_values],
    )(all_queries, pick, place, same, bias_mask, cache_keys)
    ffn_weights = joined(ffn_weights, ffn_next, partial)
    partial = exchange(partial, "seq")

    ffn_far = swapped(ffn_weights, [6, 7, 4, 5, 2, 3, 0, 1])
    mid_parts = kernel_call(
        finish_body,
        shape((tps, rows, width), bf16),
        in_vmem(3),
        "finish",
        moved=30 << 20,
        loads=[w_out],
    )(partial, fresh, fresh_lse)
    ffn_weights = joined(ffn_weights, ffn_far, mid_parts)
    mid_parts = exchange(mid_parts, "tp")
    ffn_near = swapped(ffn_weights, [1, 0, 3, 2, 5, 4, 7, 6])
    ffn_sum, normed, mid = kernel_call(
        feed_own_body,
        [
            shape((rows, width), f32),
            shape((rows, width), bf16),
            shape((tps, row_count, width), f32),
        ],
        in_vmem(3),
        "feed_own",
        moved=30 << 20,
        loads=[ffn_gain[None, :]],
    )(mid_parts, row_tokens, ffn_weights)
    ffn_parts = kernel_call(
        feed_near_body,
        shape((tps, row_count, width), bf16),
        in_vmem(3),
        "feed_near",
        moved=4 << 20,
    )(normed, ffn_near, ffn_sum)
    ffn_parts = exchange(ffn_parts, "tp")
    return kernel_call(
        last_body, shape((row_count, width), bf16), in_smem(1) + in_vmem(2), "last", moved=1 << 17
    )(tp_at, ffn_parts, mid)


def solution(mesh):
    in_specs = (
        P(("req", "seq", "tp"), None),
        P(None, None, "tp"),
        P("tp", None),
        P(None, "tp"),
        P(),
        P(),
        P(None, ("seq", "tp"), None),
        P(("seq", "tp"), None, None),
        P(("req", "seq"), None, "tp"),
        P(("req", "seq"), None, "tp"),
        P(("req", "seq"), None),
        P("req", None),
        P("req", None),
        P("req"),
    )
    out_specs = P(("req", "seq", "tp"), None)
    return jax.shard_map(
        on_device, mesh=mesh, in_specs=in_specs, out_specs=out_specs, check_vma=False
    )
```

time: 464 us -> 87 us (0.19)
  waiting for transfers between devices: 268 us -> 27.8 us
  blocking collectives: 130 us -> 0 us
  starting transfers between devices: 0.09 us -> 37 us
  other arithmetic: 20.4 us -> 0.94 us
  local copies, waits for them, and re-layouts: 20.9 us -> 4.1 us
  Pallas kernels: 0 us -> 15.8 us
  between operations: 14.9 us -> 0.13 us
  matrix products: 7.97 us -> 0 us
    unnamed x5 -> x0, waiting for transfers between devices: 268 us -> none
    all_gather x4 -> x0, blocking collectives: 130 us -> none  [the longest x1 55.1 us: on_device(): lax.all_gather(normed, ('seq', 'tp'), axis=0, tiled=True)]
    all_to_all x0 -> x5, starting transfers between devices: none -> 26.7 us  [exchange(): return lax.all_to_all(pieces, axes, 0, 0, tiled=True)]
    all_to_all x0 -> x5, waiting for transfers between devices: none -> 17.7 us  [exchange(): return lax.all_to_all(pieces, axes, 0, 0, tiled=True)]
    pallas_call x0 -> x10, Pallas kernels: none -> 15.8 us  [kernel_call(): return lambda *ins: call(*ins, *[stay_in_hbm(a) for a in (*loads, *small)])]
    ppermute x0 -> x3, starting transfers between devices: none -> 10.4 us  [swapped(): return lax.ppermute(blocks, 'seq', list(enumerate(partner)))]
    ppermute x0 -> x3, waiting for transfers between devices: none -> 10.2 us  [swapped(): return lax.ppermute(blocks, 'seq', list(enumerate(partner)))]
    dot_general x10 -> x0, matrix products: 7.84 us -> none  [the longest x1 1.65 us: cache_partials(): jnp.einsum('sthd,slhd->shtl', slot_query, key_rows, preferred_element_typ...]
  transfers between devices with their start and end apart: 3 -> 8, of which waited for: 2 -> 6; matrix products, arithmetic and copies ran while one was open for 1% -> 2% of each run, Pallas kernels for 0% -> 15%
where the time goes in v1:
time: 87 us; the launch traced here: 85.9 us
  starting transfers between devices  37 us (43%)
  waiting for transfers between devices  27.8 us (32%)
  Pallas kernels  15.8 us (18%)
  local copies, waits for them, and re-layouts  4.1 us (5%)
  other arithmetic  0.94 us (1%)
    all_to_all x5, starting transfers between devices, exchange(): return lax.all_to_all(pieces, axes, 0, 0, tiled=True)  26.7 us
    all_to_all x5, waiting for transfers between devices, exchange(): return lax.all_to_all(pieces, axes, 0, 0, tiled=True)  17.7 us
    pallas_call x10, Pallas kernels, kernel_call(): return lambda *ins: call(*ins, *[stay_in_hbm(a) for a in (*loads, *small)])  15.8 us
    ppermute x3, starting transfers between devices, swapped(): return lax.ppermute(blocks, 'seq', list(enumerate(partner)))  10.4 us
    ppermute x3, waiting for transfers between devices, swapped(): return lax.ppermute(blocks, 'seq', list(enumerate(partner)))  10.2 us
    unnamed x6, local copies, waits for them, and re-layouts  2.02 us
  transfers between devices with their start and end apart: 8, of which 6 were waited for; matrix products, arithmetic and copies ran while one was open for 2% of the time, Pallas kernels for 15%

profile of v1, /device:TPU:56, one launch (start us, length us, event | category | flops | bytes accessed | tf_op | source)
XLA Modules:
  0.0 85.9 jit_solution(14840886355987876789)
XLA Ops:
  0.0 1.3 %broadcast_in_dim.8 = bf16[8,4,1024]{2,1,0:T(4,128)(2,1)} broadcast(bf16[4,1024]{1,0:T(4,128)(2,1)} %param.16), dimensions={1,2} | broadcast | bytes 73728 | tf_op jit(solution)/shard_map/broadcast_in_dim | solution.py:24
  1.3 10.3 %all-to-all-start = ((bf16[8,4,1024]{2,1,0:T(4,128)(2,1)}), bf16[8,4,1024]{2,1,0:T(4,128)(2,1)S(1)}, u32[]{:S(2)}, u32[]{:S(2)}) async-start(bf16[8,4,1024]{2,1,0:T(4,128)(2,1)} %broadcast_in_dim.8), calls=%async_computation | async-start | bytes 131072 | tf_op jit(solution)/shard_map/all_to_all | solution.py:20
  11.7 1.2 %pack.1.refs_0_ = bf16[1,1536,128]{2,1,0:T(8,128)(2,1)S(1)} custom-call(bf16[1024,128]{1,0:T(8,128)(2,1)} %bitcast.10, bf16[64,1024]{1,0:T(8,128)(2,1)} %bitcast.11), custom_call_target="tpu_custom_call" | custom-call | flops 314572800 | bytes 1048576 | tf_op jit(solution)/shard_map/pack/pallas_call | solution.py:78
  12.8 3.4 %collective-permute-start = (bf16[1,1536,128]{2,1,0:T(8,128)(2,1)S(1)}, bf16[1,1536,128]{2,1,0:T(8,128)(2,1)S(1)}, u32[]{:S(2)}, u32[]{:S(2)}) collective-permute-start(bf16[1,1536,128]{2,1,0:T(8,128)(2,1)S(1)} %pack.1.refs_0_), channel_id=1, source_target_pairs={{0,16},{8,24},{16,0},{24,8},{32,48},{40,56},{48,32},{56,40},{1,17}... | collective-permute-start | bytes 1179656 | tf_op jit(solution)/shard_map/ppermute | solution.py:28
  17.9 2.1 %all-to-all-done.refs_0_.refs_1_ = bf16[8,4,1024]{2,1,0:T(4,128)(2,1)S(1)} async-done(((bf16[8,4,1024]{2,1,0:T(4,128)(2,1)}), bf16[8,4,1024]{2,1,0:T(4,128)(2,1)S(1)}, u32[]{:S(2)}, u32[]{:S(2)}) %all-to-all-start) | async-done | bytes 65568 | tf_op jit(solution)/shard_map/all_to_all | solution.py:20
  20.0 2.0 %project.1 = (bf16[8,32,128]{2,1,0:T(8,128)(2,1)}, bf16[32,128]{1,0:T(8,128)(2,1)S(1)}, bf16[32,128]{1,0:T(8,128)(2,1)S(1)}) custom-call(bf16[8,4,1024]{2,1,0:T(4,128)(2,1)S(1)} %all-to-all-done.refs_0_.refs_1_, f32[8,4,128]{2,1,0:T(4,128)S(1)} %get-tuple-element.30.refs_1_, f32[8,4,128]{2,1,0:T(4,128)S(1)} %get-tuple-element.29.refs_2_, ...), custom_call_target="tpu_custom_call" | custom-call | flops 314572800 | bytes 1048576 | tf_op jit(solution)/shard_map/project/pallas_call | solution.py:78
  22.1 4.3 %all-to-all-start.1 = ((bf16[8,32,128]{2,1,0:T(8,128)(2,1)}), bf16[8,32,128]{2,1,0:T(8,128)(2,1)S(1)}, u32[]{:S(2)}, u32[]{:S(2)}) async-start(bf16[8,32,128]{2,1,0:T(8,128)(2,1)} %get-tuple-element.17.refs_1_), calls=%async_computation.1 | async-start | bytes 131072 | tf_op jit(solution)/shard_map/all_to_all | solution.py:20
  26.4 2.5 %prepare.1 = (bf16[192,256]{1,0:T(8,128)(2,1)S(1)}, bf16[256,192]{1,0:T(8,128)(2,1)S(1)}, f32[192,192]{1,0:T(8,128)S(1)}, f32[192,256]{1,0:T(8,128)S(1)}, f32[32,128]{1,0:T(8,128)S(1)}, /*index=5*/f32[32,128]{1,0:T(8,128)S(1)}) custom-call(s32[1]{0:T(128)} %bitcast.3.refs_0_, bf16[8,32,128]{2,1,0:T(8,128)(2,1)} %get-tuple-element.17.refs_1_, ...), custom_call_target="tpu_custom_call" | custom-call | flops 314572800 | bytes 1048576 | tf_op jit(solution)/shard_map/prepare/pallas_call | solution.py:78
  28.9 3.2 %all-to-all-done.1.refs_0_ = bf16[8,32,128]{2,1,0:T(8,128)(2,1)S(1)} async-done(((bf16[8,32,128]{2,1,0:T(8,128)(2,1)}), bf16[8,32,128]{2,1,0:T(8,128)(2,1)S(1)}, u32[]{:S(2)}, u32[]{:S(2)}) %all-to-all-start.1) | async-done | bytes 65568 | tf_op jit(solution)/shard_map/all_to_all | solution.py:20
  32.0 3.4 %cache.1.refs_2_ = bf16[8,64,128]{2,1,0:T(8,128)(2,1)} custom-call(bf16[8,32,128]{2,1,0:T(8,128)(2,1)S(1)} %all-to-all-done.1.refs_0_, bf16[192,256]{1,0:T(8,128)(2,1)S(1)} %get-tuple-element.20.refs_1_, bf16[256,192]{1,0:T(8,128)(2,1)S(1)} %get-tuple-element.21.refs_2_, f32[192,192]{1,0:T(8,128)S(1)} %get-tuple-element.22.refs_3_, ...), custom_call_target="tpu_custom_call" | custom-call | flops 1258291200 | bytes 4194304 | tf_op jit(solution)/shard_map/cache/pallas_call | solution.py:78
  35.5 3.4 %all-to-all-start.2 = ((bf16[8,64,128]{2,1,0:T(8,128)(2,1)}), bf16[8,64,128]{2,1,0:T(8,128)(2,1)S(1)}, u32[]{:S(2)}, u32[]{:S(2)}) async-start(bf16[8,64,128]{2,1,0:T(8,128)(2,1)} %cache.1.refs_2_), calls=%async_computation.2 | async-start | bytes 262144 | tf_op jit(solution)/shard_map/all_to_all | solution.py:20
  38.9 5.1 %collective-permute-start.1 = (bf16[2,1536,128]{2,1,0:T(8,128)(2,1)S(1)}, bf16[2,1536,128]{2,1,0:T(8,128)(2,1)S(1)}, u32[]{:S(2)}, u32[]{:S(2)}) collective-permute-start(bf16[2,1536,128]{2,1,0:T(8,128)(2,1)S(1)} %join.2.refs_0_), channel_id=1, source_target_pairs={{0,48},{8,56},{16,32},{24,40},{32,16},{40,24},{48,0},{56,8},{1,49}... | collective-permute-start | bytes 2359304 | tf_op jit(solution)/shard_map/ppermute | solution.py:28
  44.0 0.9 %all-to-all-done.2.refs_0_ = bf16[8,64,128]{2,1,0:T(8,128)(2,1)S(1)} async-done(((bf16[8,64,128]{2,1,0:T(8,128)(2,1)}), bf16[8,64,128]{2,1,0:T(8,128)(2,1)S(1)}, u32[]{:S(2)}, u32[]{:S(2)}) %all-to-all-start.2) | async-done | bytes 131104 | tf_op jit(solution)/shard_map/all_to_all | solution.py:20
  44.9 2.0 %finish.1.refs_2_ = bf16[8,32,1024]{2,1,0:T(8,128)(2,1)} custom-call(bf16[8,64,128]{2,1,0:T(8,128)(2,1)S(1)} %all-to-all-done.2.refs_0_, f32[32,128]{1,0:T(8,128)S(1)} %get-tuple-element.24.refs_1_, f32[32,128]{1,0:T(8,128)S(1)} %get-tuple-element.25.refs_2_, bf16[128,1024]{1,0:T(8,128)(2,1)} %refs_3_.1), custom_call_target="tpu_custom_call" | custom-call | flops 9437184000 | bytes 31457280 | tf_op jit(solution)/shard_map/finish/pallas_call | solution.py:78
  46.9 4.8 %all-to-all-start.3 = ((bf16[8,32,1024]{2,1,0:T(8,128)(2,1)}), bf16[8,32,1024]{2,1,0:T(8,128)(2,1)S(1)}, u32[]{:S(2)}, u32[]{:S(2)}) async-start(bf16[8,32,1024]{2,1,0:T(8,128)(2,1)} %finish.1.refs_2_), calls=%async_computation.3 | async-start | bytes 1048576 | tf_op jit(solution)/shard_map/all_to_all | solution.py:20
  51.7 10.1 %collective-permute-done.1.refs_1_ = bf16[2,1536,128]{2,1,0:T(8,128)(2,1)S(1)} collective-permute-done((bf16[2,1536,128]{2,1,0:T(8,128)(2,1)S(1)}, bf16[2,1536,128]{2,1,0:T(8,128)(2,1)S(1)}, u32[]{:S(2)}, u32[]{:S(2)}) %collective-permute-start.1) | collective-permute-done | bytes 786464 | tf_op jit(solution)/shard_map/ppermute | solution.py:28
  61.9 0.9 %copy-done.1 = bf16[2,1536,128]{2,1,0:T(8,128)(2,1)} copy-done((bf16[2,1536,128]{2,1,0:T(8,128)(2,1)}, bf16[2,1536,128]{2,1,0:T(8,128)(2,1)S(1)}, u32[]{:S(2)}) %copy-start.1) | copy-done | bytes 786456
  62.8 1.1 %copy-done.2 = bf16[2,1536,128]{2,1,0:T(8,128)(2,1)S(1)} copy-done((bf16[2,1536,128]{2,1,0:T(8,128)(2,1)S(1)}, bf16[2,1536,128]{2,1,0:T(8,128)(2,1)}, u32[]{:S(2)}) %copy-start.2) | copy-done | bytes 786456
  64.0 1.9 %collective-permute-start.2 = (bf16[4,1536,128]{2,1,0:T(8,128)(2,1)S(1)}, bf16[4,1536,128]{2,1,0:T(8,128)(2,1)}, u32[]{:S(2)}, u32[]{:S(2)}) collective-permute-start(bf16[4,1536,128]{2,1,0:T(8,128)(2,1)S(1)} %join.3.refs_2_), channel_id=1, source_target_pairs={{0,8},{8,0},{16,24},{24,16},{32,40},{40,32},{48,56},{56,48},{1,9},... | collective-permute-start | bytes 4718600 | tf_op jit(solution)/shard_map/ppermute | solution.py:28
  65.9 3.1 %all-to-all-done.3.refs_0_ = bf16[8,32,1024]{2,1,0:T(8,128)(2,1)S(1)} async-done(((bf16[8,32,1024]{2,1,0:T(8,128)(2,1)}), bf16[8,32,1024]{2,1,0:T(8,128)(2,1)S(1)}, u32[]{:S(2)}, u32[]{:S(2)}) %all-to-all-start.3) | async-done | bytes 524320 | tf_op jit(solution)/shard_map/all_to_all | solution.py:20
  69.0 1.4 %feed_own.1 = (f32[32,1024]{1,0:T(8,128)S(1)}, bf16[32,1024]{1,0:T(8,128)(2,1)S(1)}, f32[8,4,1024]{2,1,0:T(4,128)S(1)}) custom-call(bf16[8,32,1024]{2,1,0:T(8,128)(2,1)S(1)} %all-to-all-done.3.refs_0_, bf16[8,4,1024]{2,1,0:T(4,128)(2,1)S(1)} %all-to-all-done.refs_0_.refs_1_, bf16[4,1536,128]{2,1,0:T(8,128)(2,1)S(1)} %join.3.refs_2_, f32[1,1024]{1,0:T(1,128)} %bitcast.13), custom_call_target="tpu_custom_call" | custom-call | flops 9437184000 | bytes 31457280 | tf_op jit(solution)/shard_map/feed_own/pallas_call | solution.py:78
  70.4 2.6 %feed_near.1 = bf16[8,4,1024]{2,1,0:T(4,128)(2,1)} custom-call(bf16[32,1024]{1,0:T(8,128)(2,1)S(1)} %get-tuple-element.26.refs_0_, bf16[4,1536,128]{2,1,0:T(8,128)(2,1)} %collective-permute-done.2.refs_1_, f32[32,1024]{1,0:T(8,128)S(1)} %get-tuple-element.27.refs_2_), custom_call_target="tpu_custom_call" | custom-call | flops 1258291200 | bytes 4194304 | tf_op jit(solution)/shard_map/feed_near/pallas_call | solution.py:78
  73.1 3.8 %all-to-all-start.4 = ((bf16[8,4,1024]{2,1,0:T(4,128)(2,1)}), bf16[8,4,1024]{2,1,0:T(4,128)(2,1)S(1)}, u32[]{:S(2)}, u32[]{:S(2)}) async-start(bf16[8,4,1024]{2,1,0:T(4,128)(2,1)} %feed_near.1), calls=%async_computation.4 | async-start | bytes 131072 | tf_op jit(solution)/shard_map/all_to_all | solution.py:20
  76.9 8.4 %all-to-all-done.4.refs_1_ = bf16[8,4,1024]{2,1,0:T(4,128)(2,1)S(1)} async-done(((bf16[8,4,1024]{2,1,0:T(4,128)(2,1)}), bf16[8,4,1024]{2,1,0:T(4,128)(2,1)S(1)}, u32[]{:S(2)}, u32[]{:S(2)}) %all-to-all-start.4) | async-done | bytes 65568 | tf_op jit(solution)/shard_map/all_to_all | solution.py:20
  (12 shorter events, 2.5 us)
Async XLA Ops:
  1.3 18.7 %all-to-all-start = ((bf16[8,4,1024]{2,1,0:T(4,128)(2,1)}), bf16[8,4,1024]{2,1,0:T(4,128)(2,1)S(1)}, u32[]{:S(2)}, u32[]{:S(2)}) async-start(bf16[8,4,1024]{2,1,0:T(4,128)(2,1)} %broadcast_in_dim.8), calls=%async_computation | async-start | bytes 131072 | tf_op jit(solution)/shard_map/all_to_all | solution.py:20
  11.7 20.4 %copy-start = (bf16[24,256,128]{2,1,0:T(8,128)(2,1)S(1)}, bf16[24,256,128]{2,1,0:T(8,128)(2,1)}, u32[]{:S(2)}) copy-start(bf16[24,256,128]{2,1,0:T(8,128)(2,1)} %refs_5_.1) | copy-start | bytes 4718596
  12.8 26.0 %collective-permute-start = (bf16[1,1536,128]{2,1,0:T(8,128)(2,1)S(1)}, bf16[1,1536,128]{2,1,0:T(8,128)(2,1)S(1)}, u32[]{:S(2)}, u32[]{:S(2)}) collective-permute-start(bf16[1,1536,128]{2,1,0:T(8,128)(2,1)S(1)} %pack.1.refs_0_), channel_id=1, source_target_pairs={{0,16},{8,24},{16,0},{24,8},{32,48},{40,56},{48,32},{56,40},{1,17}... | collective-permute-start | bytes 1179656 | tf_op jit(solution)/shard_map/ppermute | solution.py:28
  22.1 9.9 %all-to-all-start.1 = ((bf16[8,32,128]{2,1,0:T(8,128)(2,1)}), bf16[8,32,128]{2,1,0:T(8,128)(2,1)S(1)}, u32[]{:S(2)}, u32[]{:S(2)}) async-start(bf16[8,32,128]{2,1,0:T(8,128)(2,1)} %get-tuple-element.17.refs_1_), calls=%async_computation.1 | async-start | bytes 131072 | tf_op jit(solution)/shard_map/all_to_all | solution.py:20
  35.5 9.4 %all-to-all-start.2 = ((bf16[8,64,128]{2,1,0:T(8,128)(2,1)}), bf16[8,64,128]{2,1,0:T(8,128)(2,1)S(1)}, u32[]{:S(2)}, u32[]{:S(2)}) async-start(bf16[8,64,128]{2,1,0:T(8,128)(2,1)} %cache.1.refs_2_), calls=%async_computation.2 | async-start | bytes 262144 | tf_op jit(solution)/shard_map/all_to_all | solution.py:20
  38.9 22.9 %collective-permute-start.1 = (bf16[2,1536,128]{2,1,0:T(8,128)(2,1)S(1)}, bf16[2,1536,128]{2,1,0:T(8,128)(2,1)S(1)}, u32[]{:S(2)}, u32[]{:S(2)}) collective-permute-start(bf16[2,1536,128]{2,1,0:T(8,128)(2,1)S(1)} %join.2.refs_0_), channel_id=1, source_target_pairs={{0,48},{8,56},{16,32},{24,40},{32,16},{40,24},{48,0},{56,8},{1,49}... | collective-permute-start | bytes 2359304 | tf_op jit(solution)/shard_map/ppermute | solution.py:28
  46.9 22.1 %all-to-all-start.3 = ((bf16[8,32,1024]{2,1,0:T(8,128)(2,1)}), bf16[8,32,1024]{2,1,0:T(8,128)(2,1)S(1)}, u32[]{:S(2)}, u32[]{:S(2)}) async-start(bf16[8,32,1024]{2,1,0:T(8,128)(2,1)} %finish.1.refs_2_), calls=%async_computation.3 | async-start | bytes 1048576 | tf_op jit(solution)/shard_map/all_to_all | solution.py:20
  61.9 0.9 %copy-start.1 = (bf16[2,1536,128]{2,1,0:T(8,128)(2,1)}, bf16[2,1536,128]{2,1,0:T(8,128)(2,1)S(1)}, u32[]{:S(2)}) copy-start(bf16[2,1536,128]{2,1,0:T(8,128)(2,1)S(1)} %collective-permute-done.1.refs_1_) | copy-start | bytes 2359300
  62.8 1.1 %copy-start.2 = (bf16[2,1536,128]{2,1,0:T(8,128)(2,1)S(1)}, bf16[2,1536,128]{2,1,0:T(8,128)(2,1)}, u32[]{:S(2)}) copy-start(bf16[2,1536,128]{2,1,0:T(8,128)(2,1)} %copy-done.1) | copy-start | bytes 2359300
  64.0 6.4 %collective-permute-start.2 = (bf16[4,1536,128]{2,1,0:T(8,128)(2,1)S(1)}, bf16[4,1536,128]{2,1,0:T(8,128)(2,1)}, u32[]{:S(2)}, u32[]{:S(2)}) collective-permute-start(bf16[4,1536,128]{2,1,0:T(8,128)(2,1)S(1)} %join.3.refs_2_), channel_id=1, source_target_pairs={{0,8},{8,0},{16,24},{24,16},{32,40},{40,32},{48,56},{56,48},{1,9},... | collective-permute-start | bytes 4718600 | tf_op jit(solution)/shard_map/ppermute | solution.py:28
  73.1 12.2 %all-to-all-start.4 = ((bf16[8,4,1024]{2,1,0:T(4,128)(2,1)}), bf16[8,4,1024]{2,1,0:T(4,128)(2,1)S(1)}, u32[]{:S(2)}, u32[]{:S(2)}) async-start(bf16[8,4,1024]{2,1,0:T(4,128)(2,1)} %feed_near.1), calls=%async_computation.4 | async-start | bytes 131072 | tf_op jit(solution)/shard_map/all_to_all | solution.py:20

commit v2 on v1

--- a/solution.py
+++ b/solution.py
@@ -20,10 +20,6 @@
     return lax.all_to_all(pieces, axes, 0, 0, tiled=True)
 
 
-def copies(block, axes):
-    return jnp.broadcast_to(block[None], (lax.axis_size(axes), *block.shape))
-
-
 def swapped(blocks, partner):
     return lax.ppermute(blocks, "seq", list(enumerate(partner)))
 
@@ -40,21 +36,40 @@
     return array if INTERPRET else pltpu.with_memory_space_constraint(array, pltpu.HBM)
 
 
-def kernel_call(body, out_shape, in_specs, name, moved, loads=(), small=(), scratch=()):
+class Part:
+    def __init__(self, array, start=0, size=None):
+        self.array, self.start = array, start
+        self.shape = (array.shape[0] if size is None else size, *array.shape[1:])
+        self.dtype = array.dtype
+
+    def of(self, ref):
+        return ref if self.shape == ref.shape else ref.at[pl.ds(self.start, self.shape[0])]
+
+
+def kernel_call(
+    body, out_shape, in_specs, name, moved, loads=(), small=(), carried=(), scratch=()
+):
+    loads, small, carried = (
+        [a if isinstance(a, Part) else Part(a) for a in arrays] for arrays in (loads, small, carried)
+    )
     many = isinstance(out_shape, (list, tuple))
-    outs = len(out_shape) if many else 1
+    shapes = list(out_shape) if many else [out_shape]
+    outs = len(shapes)
+    shapes = shapes + [jax.ShapeDtypeStruct(a.shape, a.dtype) for a in carried]
     held = [pltpu.VMEM(a.shape, a.dtype) for a in loads] + [
         pltpu.SMEM(a.shape, a.dtype) for a in small
     ]
-    count, plain = len(held), len(in_specs)
+    count, more, plain = len(held), len(carried), len(in_specs)
 
     def run(*refs):
         ins, refs = refs[:plain], refs[plain:]
-        sources, refs = refs[:count], refs[count:]
-        results, refs = refs[:outs], refs[outs:]
+        sources, refs = refs[: count + more], refs[count + more :]
+        results, refs = refs[: outs + more], refs[outs + more :]
         buffers, refs = refs[:count], refs[count:]
-        sems, rest = refs[:count], refs[count:]
-        moves = [pltpu.make_async_copy(*each) for each in zip(sources, buffers, sems)]
+        sems, rest = refs[: count + more], refs[count + more :]
+        targets = [*buffers, *results[outs:]]
+        sources = [a.of(ref) for a, ref in zip((*loads, *small, *carried), sources)]
+        moves = [pltpu.make_async_copy(*each) for each in zip(sources, targets, sems)]
         for move in moves:
             move.start()
 
@@ -62,20 +77,22 @@
             for i in which or range(count):
                 moves[i].wait()
 
-        body(arrive, *ins, *buffers, *results, *rest)
+        body(arrive, *ins, *buffers, *results[:outs], *rest)
+        for move in moves[count:]:
+            move.wait()
 
     call = pl.pallas_call(
         run,
-        out_shape=out_shape,
-        in_specs=list(in_specs) + [pl.BlockSpec(memory_space=pltpu.HBM)] * count,
-        out_specs=in_vmem(outs) if many else in_vmem(1)[0],
-        scratch_shapes=held + [pltpu.SemaphoreType.DMA(())] * count + list(scratch),
+        out_shape=shapes if many or more else shapes[0],
+        in_specs=list(in_specs) + [pl.BlockSpec(memory_space=pltpu.HBM)] * (count + more),
+        out_specs=in_vmem(outs + more) if many or more else in_vmem(1)[0],
+        scratch_shapes=held + [pltpu.SemaphoreType.DMA(())] * (count + more) + list(scratch),
         name=name,
         interpret=INTERPRET,
-        compiler_params=pltpu.CompilerParams(vmem_limit_bytes=16 << 20),
+        compiler_params=pltpu.CompilerParams(vmem_limit_bytes=8 << 20),
         cost_estimate=pl.CostEstimate(flops=300 * moved, bytes_accessed=moved, transcendentals=0),
     )
-    return lambda *ins: call(*ins, *[stay_in_hbm(a) for a in (*loads, *small)])
+    return lambda *ins: call(*ins, *[stay_in_hbm(a.array) for a in (*loads, *small, *carried)])
 
 
 def iota(shape, dim):
@@ -109,24 +126,27 @@
         out_ref[0, at : at + units] = down_ref[:, LANES * c : LANES * (c + 1)]
 
 
-def join_body(arrive, first_ref, second_ref, after_ref, out_ref):
+def join_body(_, first_ref, second_ref, after_ref, out_ref, sem):
     count = first_ref.shape[0]
+    move = pltpu.make_async_copy(second_ref, out_ref.at[pl.ds(count, count)], sem)
+    move.start()
     out_ref[:count] = first_ref[...]
-    out_ref[count:] = second_ref[...]
-
-
-def joined(first, second, after):
+    move.wait()
+
+
+def joined(first, second, after, carried=()):
     return kernel_call(
         join_body,
         jax.ShapeDtypeStruct((2 * first.shape[0], *first.shape[1:]), first.dtype),
-        in_vmem(2) + [pl.BlockSpec(memory_space=pl.ANY)],
+        in_vmem(1) + [pl.BlockSpec(memory_space=pltpu.HBM), pl.BlockSpec(memory_space=pl.ANY)],
         "join",
         moved=4 << 20,
-    )(first, second, after)
+        carried=carried,
+        scratch=[pltpu.SemaphoreType.DMA(())],
+    )(first, stay_in_hbm(second), after)
 
 
 def project_body(arrive, token_ref, cos_ref, sin_ref, gain_ref, w_ref, q_ref, k_ref, v_ref):
-    arrive(0)
     normed = scaled_rows(stacked(token_ref), gain_ref[...])
     cosine, sine = stacked(cos_ref), stacked(sin_ref)
     first_half = iota(cosine.shape, 1) % HD < HD // 2
@@ -139,7 +159,6 @@
         )
         return (part * cosine + partner * sine).astype(jnp.bfloat16)
 
-    arrive(1)
     queries = rotate(matmul(normed, w_ref[0]))
     for i in range(q_ref.shape[0]):
         q_ref[i] = queries
@@ -268,7 +287,18 @@
 
 
 def cache_body(
-    steps, scale, arrive, q_ref, pick_ref, place_ref, same_ref, bias_mask_ref, k_ref, v_ref, out_ref
+    steps,
+    scale,
+    arrive,
+    q_ref,
+    pick_ref,
+    place_ref,
+    same_ref,
+    bias_mask_ref,
+    k_ref,
+    early_v_ref,
+    late_v_ref,
+    out_ref,
 ):
     slots = k_ref.shape[0]
     group = 2 * steps
@@ -295,10 +325,11 @@
     row_top = jnp.max(top_lane + same_ref[...], axis=1, keepdims=True)
     weights = jnp.where(live, jnp.exp(scores - row_top), 0.0)
     total = jnp.sum(weights, axis=1, keepdims=True)
-    arrive(0)
+    arrive()
+    values = [r.at[i] for r in (early_v_ref, late_v_ref) for i in range(r.shape[0])]
     mixed = jnp.concatenate(
         [
-            matmul(weights[group * s : group * (s + 1)].astype(jnp.bfloat16), v_ref[s])
+            matmul(weights[group * s : group * (s + 1)].astype(jnp.bfloat16), values[s][...])
             for s in range(slots)
         ],
         axis=0,
@@ -354,35 +385,22 @@
         total = total + weight
         mixed = mixed + weight * part_ref[d, :span].astype(jnp.float32)
     attended = (mixed / total).astype(jnp.bfloat16)
-    arrive()
     partial = matmul(attended, w_ref[...]).astype(jnp.bfloat16)
     for d in range(out_ref.shape[0]):
         out_ref[d] = partial
 
 
-def feed(normed, w_ref):
-    rows, width = normed.shape
-    blocks = [w_ref.at[i] for i in range(w_ref.shape[0])]
-    low_lanes = iota((rows, LANES), 1) < HD
-    halves = []
-    for s, block in enumerate(blocks):
-        expanded = matmul(normed, block[:width])
-        gate = expanded / (1.0 + jnp.exp(-expanded))
-        part = gate * pltpu.roll(expanded, HD, 1)
-        if s % 2 == 0:
-            halves.append(part)
-        else:
-            halves[-1] = jnp.where(low_lanes, halves[-1], pltpu.roll(part, HD, 1))
-    hidden = jnp.concatenate(halves, axis=1).astype(jnp.bfloat16)
-    parts = []
-    for c in range(width // LANES):
-        at = width + HD * c
-        weights = jnp.concatenate([block[at : at + HD] for block in blocks], axis=0)
-        parts.append(matmul(hidden, weights))
-    return parts
-
-
-def feed_own_body(arrive, part_ref, token_ref, w_ref, gain_ref, out_ref, normed_ref, mid_ref):
+def gated(normed, blocks):
+    low_lanes = iota((normed.shape[0], LANES), 1) < HD
+    pair = jnp.concatenate([block[: normed.shape[1]] for block in blocks], axis=1)
+    expanded = matmul(normed, pair)
+    gates = expanded / (1.0 + jnp.exp(-expanded))
+    first = gates[:, :LANES] * pltpu.roll(expanded[:, :LANES], HD, 1)
+    second = pltpu.roll(gates[:, LANES:], HD, 1) * expanded[:, LANES:]
+    return jnp.where(low_lanes, first, second)
+
+
+def settle_body(_, part_ref, token_ref, gain_ref, normed_ref, mid_ref):
     mid = part_ref[0].astype(jnp.float32)
     for d in range(1, part_ref.shape[0]):
         mid = mid + part_ref[d].astype(jnp.float32)
@@ -390,20 +408,40 @@
     own = mid_ref.shape[1]
     for d in range(mid_ref.shape[0]):
         mid_ref[d] = mid[own * d : own * (d + 1)]
-    arrive()
-    normed = scaled_rows(mid, gain_ref[...])
-    normed_ref[...] = normed
-    for c, part in enumerate(feed(normed, w_ref)):
-        out_ref[:, LANES * c : LANES * (c + 1)] = part
-
-
-def feed_near_body(arrive, normed_ref, w_ref, part_ref, out_ref):
+    normed_ref[...] = scaled_rows(mid, gain_ref[...])
+
+
+def feed_body(_, normed_ref, own_w_ref, near_hbm_ref, out_ref, near_w_ref, sems):
+    count = near_w_ref.shape[0]
+    moves = [
+        pltpu.make_async_copy(near_hbm_ref.at[i], near_w_ref.at[i], sems.at[i])
+        for i in range(count)
+    ]
+    for move in moves:
+        move.start()
     own = out_ref.shape[1]
-    for c, part in enumerate(feed(normed_ref[...], w_ref)):
-        lanes = slice(LANES * c, LANES * (c + 1))
-        part = part + part_ref[:, lanes]
+    normed = normed_ref[...]
+    width = normed.shape[1]
+    blocks = [r.at[i] for r in (own_w_ref, near_w_ref) for i in range(count)]
+    halves = []
+    for s in range(0, 2 * count, 2):
+        if s >= count:
+            moves[s - count].wait()
+            moves[s - count + 1].wait()
+        halves.append(gated(normed, blocks[s : s + 2]))
+    hidden = jnp.concatenate(halves, axis=1).astype(jnp.bfloat16)
+    for c in range(0, width // LANES, 2):
+        at = width + HD * c
+        weights = jnp.concatenate(
+            [
+                jnp.concatenate([block[at : at + HD], block[at + HD : at + 2 * HD]], axis=1)
+                for block in blocks
+            ],
+            axis=0,
+        )
+        part = matmul(hidden, weights).astype(jnp.bfloat16)
         for d in range(out_ref.shape[0]):
-            out_ref[d, :, lanes] = part[own * d : own * (d + 1)].astype(jnp.bfloat16)
+            out_ref[d, :, LANES * c : LANES * (c + 2)] = part[own * d : own * (d + 1)]
 
 
 def last_body(arrive, index_ref, part_ref, mid_ref, out_ref):
@@ -453,16 +491,17 @@
     seq_at = lax.axis_index("seq")
     tp_at = lax.axis_index("tp").astype(jnp.int32).reshape(1)
 
-    row_tokens = exchange(copies(tokens, "tp"), "tp")
+    row_tokens = exchange(jnp.broadcast_to(tokens[None], (tps, *tokens.shape)), "tp")
 
     blocks, units = w_down.shape[:2]
-    ffn_weights = kernel_call(
+    ffn_weights, qkv_weights, qkv_gain = kernel_call(
         pack_body,
         shape((1, width + units * width // lanes, lanes), bf16),
         [],
         "pack",
         moved=1 << 20,
         loads=[gate_up.reshape(width, lanes), w_down.reshape(units, width)],
+        carried=[w_qkv.transpose(1, 0, 2), attn_gain[None, :]],
     )()
     ffn_next = swapped(ffn_weights, [2, 3, 0, 1, 6, 7, 4, 5])
 
@@ -471,15 +510,15 @@
     queries, keys_new, values_new = kernel_call(
         project_body,
         [shape((seqs, rows, lanes), bf16), shape((rows, lanes), bf16), shape((rows, lanes), bf16)],
-        in_vmem(3),
+        in_vmem(5),
         "project",
         moved=1 << 20,
-        loads=[attn_gain[None, :], w_qkv.transpose(1, 0, 2)],
-    )(row_tokens, cosine, sine)
+    )(row_tokens, cosine, sine, qkv_gain, qkv_weights)
     all_queries = exchange(queries, "seq")
 
     slot_rows = 2 * steps * slots
-    pick, place, same, bias_mask, fresh, fresh_lse = kernel_call(
+    early = slots // 3
+    pick, place, same, bias_mask, fresh, fresh_lse, held_values = kernel_call(
         lambda *refs: prepare_body(steps, slots, scale, *refs),
         [
             shape((slot_rows, requests * steps), bf16),
@@ -494,51 +533,52 @@
         moved=1 << 20,
         loads=[piece_slot, cache_len[None, :], new_variate.T, cache_variate],
         small=[variate_bias],
+        carried=[Part(cache_values, 0, early)],
         scratch=[pltpu.VMEM((requests, lanes), jnp.int32)],
     )(seq_at.astype(jnp.int32).reshape(1), queries, keys_new, values_new)
 
     partial = kernel_call(
         lambda *refs: cache_body(steps, scale, *refs),
         shape((seqs, 2 * rows, lanes), bf16),
-        in_vmem(6),
+        in_vmem(7),
         "cache",
         moved=4 << 20,
-        loads=[cache_values],
-    )(all_queries, pick, place, same, bias_mask, cache_keys)
-    ffn_weights = joined(ffn_weights, ffn_next, partial)
+        loads=[Part(cache_values, early, slots - early)],
+    )(all_queries, pick, place, same, bias_mask, cache_keys, held_values)
+    ffn_weights, out_weights, gain = joined(
+        ffn_weights, ffn_next, partial, [w_out, ffn_gain[None, :]]
+    )
     partial = exchange(partial, "seq")
 
     ffn_far = swapped(ffn_weights, [6, 7, 4, 5, 2, 3, 0, 1])
     mid_parts = kernel_call(
         finish_body,
         shape((tps, rows, width), bf16),
-        in_vmem(3),
+        in_vmem(4),
         "finish",
         moved=30 << 20,
-        loads=[w_out],
-    )(partial, fresh, fresh_lse)
+    )(partial, fresh, fresh_lse, out_weights)
     ffn_weights = joined(ffn_weights, ffn_far, mid_parts)
     mid_parts = exchange(mid_parts, "tp")
     ffn_near = swapped(ffn_weights, [1, 0, 3, 2, 5, 4, 7, 6])
-    ffn_sum, normed, mid = kernel_call(
-        feed_own_body,
-        [
-            shape((rows, width), f32),
-            shape((rows, width), bf16),
-            shape((tps, row_count, width), f32),
+    normed, mid = kernel_call(
+        settle_body,
+        [shape((rows, width), bf16), shape((tps, row_count, width), f32)],
+        in_vmem(3),
+        "settle",
+        moved=30 << 20,
+    )(mid_parts, row_tokens, gain)
+    ffn_parts = kernel_call(
+        feed_body,
+        shape((tps, row_count, width), bf16),
+        in_vmem(2) + [pl.BlockSpec(memory_space=pltpu.HBM)],
+        "feed",
+        moved=4 << 20,
+        scratch=[
+            pltpu.VMEM(ffn_near.shape, bf16),
+            pltpu.SemaphoreType.DMA((ffn_near.shape[0],)),
         ],
-        in_vmem(3),
-        "feed_own",
-        moved=30 << 20,
-        loads=[ffn_gain[None, :]],
-    )(mid_parts, row_tokens, ffn_weights)
-    ffn_parts = kernel_call(
-        feed_near_body,
-        shape((tps, row_count, width), bf16),
-        in_vmem(3),
-        "feed_near",
-        moved=4 << 20,
-    )(normed, ffn_near, ffn_sum)
+    )(normed, ffn_weights, stay_in_hbm(ffn_near))
     ffn_parts = exchange(ffn_parts, "tp")
     return kernel_call(
         last_body, shape((row_count, width), bf16), in_smem(1) + in_vmem(2), "last", moved=1 << 17

time: 87 us -> 86 us (0.989)
  local copies, waits for them, and re-layouts: 4.1 us -> 2.07 us
  starting transfers between devices: 37 us -> 38.7 us
  Pallas kernels: 15.8 us -> 14.7 us
    ppermute x3, waiting for transfers between devices: 10.2 us -> 12.2 us  [swapped(): return lax.ppermute(blocks, 'seq', list(enumerate(partner)))]
    unnamed x6 -> x2, local copies, waits for them, and re-layouts: 2.02 us -> 0.01 us
    all_to_all x5, starting transfers between devices: 26.7 us -> 28.2 us  [exchange(): return lax.all_to_all(pieces, axes, 0, 0, tiled=True)]
    all_to_all x5, waiting for transfers between devices: 17.7 us -> 16.1 us  [exchange(): return lax.all_to_all(pieces, axes, 0, 0, tiled=True)]
    pallas_call x10, Pallas kernels: 15.8 us -> 14.7 us  [kernel_call(): call(*ins, *[stay_in_hbm(a.array) for a in (*loads, *small, *carried)])]
  transfers between devices with their start and end apart: 8 -> 8, of which waited for: 6 -> 6; matrix products, arithmetic and copies ran while one was open for 2% -> 2% of each run, Pallas kernels for 15% -> 13%
where the time goes in v2:
time: 86 us; the launch traced here: 85 us
  starting transfers between devices  38.7 us (45%)
  waiting for transfers between devices  28.3 us (33%)
  Pallas kernels  14.7 us (17%)
  local copies, waits for them, and re-layouts  2.07 us (2%)
  other arithmetic  0.94 us (1%)
    all_to_all x5, starting transfers between devices, exchange(): return lax.all_to_all(pieces, axes, 0, 0, tiled=True)  28.2 us
    all_to_all x5, waiting for transfers between devices, exchange(): return lax.all_to_all(pieces, axes, 0, 0, tiled=True)  16.1 us
    pallas_call x10, Pallas kernels, kernel_call(): call(*ins, *[stay_in_hbm(a.array) for a in (*loads, *small, *carried)])  14.7 us
    ppermute x3, waiting for transfers between devices, swapped(): return lax.ppermute(blocks, 'seq', list(enumerate(partner)))  12.2 us
    ppermute x3, starting transfers between devices, swapped(): return lax.ppermute(blocks, 'seq', list(enumerate(partner)))  10.5 us
  transfers between devices with their start and end apart: 8, of which 6 were waited for; matrix products, arithmetic and copies ran while one was open for 2% of the time, Pallas kernels for 13%

profile of v2, /device:TPU:56, one launch (start us, length us, event | category | flops | bytes accessed | tf_op | source)
XLA Modules:
  0.0 85.0 jit_solution(16746829640269949620)
XLA Ops:
  0.0 1.3 %broadcast_in_dim.8 = bf16[8,4,1024]{2,1,0:T(4,128)(2,1)} broadcast(bf16[4,1024]{1,0:T(4,128)(2,1)} %param.16), dimensions={1,2} | broadcast | bytes 73728 | tf_op jit(solution)/shard_map/broadcast_in_dim | solution.py:494
  1.3 10.3 %all-to-all-start = ((bf16[8,4,1024]{2,1,0:T(4,128)(2,1)}), bf16[8,4,1024]{2,1,0:T(4,128)(2,1)S(1)}, u32[]{:S(2)}, u32[]{:S(2)}) async-start(bf16[8,4,1024]{2,1,0:T(4,128)(2,1)} %broadcast_in_dim.8), calls=%async_computation | async-start | bytes 131072 | tf_op jit(solution)/shard_map/all_to_all | solution.py:20
  11.6 1.3 %pack.1 = (bf16[1,1536,128]{2,1,0:T(8,128)(2,1)S(1)}, bf16[3,1024,128]{2,1,0:T(8,128)(2,1)S(1)}, f32[1,1024]{1,0:T(1,128)S(1)}) custom-call(bf16[1024,128]{1,0:T(8,128)(2,1)} %bitcast.10, bf16[64,1024]{1,0:T(8,128)(2,1)} %bitcast.11, bf16[3,1024,128]{2,1,0:T(8,128)(2,1)} %bitcast.9, f32[1,1024]{1,0:T(1,128)} %bitcast.12), custom_call_target="tpu_custom_call" | custom-call | flops 314572800 | bytes 1048576 | tf_op jit(solution)/shard_map/pack/pallas_call | solution.py:95
  13.0 3.5 %collective-permute-start = (bf16[1,1536,128]{2,1,0:T(8,128)(2,1)S(1)}, bf16[1,1536,128]{2,1,0:T(8,128)(2,1)}, u32[]{:S(2)}, u32[]{:S(2)}) collective-permute-start(bf16[1,1536,128]{2,1,0:T(8,128)(2,1)S(1)} %get-tuple-element.35.refs_0_), channel_id=1, source_target_pairs={{0,16},{8,24},{16,0},{24,8},{32,48},{40,56},{48,32},{56,40},{1,17}... | collective-permute-start | bytes 1179656 | tf_op jit(solution)/shard_map/ppermute | solution.py:24
  16.5 0.7 dynamic_slice.3
  17.3 0.9 %fusion = (f32[8,4,128]{2,1,0:T(4,128)S(1)}, f32[8,4,128]{2,1,0:T(4,128)S(1)}) fusion(f32[128]{0:T(128)} %constant.18.clone, f32[128]{0:T(128)} %constant.17.clone, f32[8,4]{1,0:T(8,128)S(1)} %add_convert_fusion), kind=kLoop, calls=%fused_computation.2 | loop fusion | flops 8192 | bytes 33920 | tf_op jit(solution)/shard_map/mul | solution.py:463
  18.2 1.8 %all-to-all-done.refs_0_.refs_1_ = bf16[8,4,1024]{2,1,0:T(4,128)(2,1)S(1)} async-done(((bf16[8,4,1024]{2,1,0:T(4,128)(2,1)}), bf16[8,4,1024]{2,1,0:T(4,128)(2,1)S(1)}, u32[]{:S(2)}, u32[]{:S(2)}) %all-to-all-start) | async-done | bytes 65568 | tf_op jit(solution)/shard_map/all_to_all | solution.py:20
  20.0 0.9 %project.1 = (bf16[8,32,128]{2,1,0:T(8,128)(2,1)}, bf16[32,128]{1,0:T(8,128)(2,1)S(1)}, bf16[32,128]{1,0:T(8,128)(2,1)S(1)}) custom-call(bf16[8,4,1024]{2,1,0:T(4,128)(2,1)S(1)} %all-to-all-done.refs_0_.refs_1_, f32[8,4,128]{2,1,0:T(4,128)S(1)} %get-tuple-element.42.refs_1_, f32[8,4,128]{2,1,0:T(4,128)S(1)} %get-tuple-element.41.refs_2_, ...), custom_call_target="tpu_custom_call" | custom-call | flops 314572800 | bytes 1048576 | tf_op jit(solution)/shard_map/project/pallas_call | solution.py:95
  21.0 4.3 %all-to-all-start.1 = ((bf16[8,32,128]{2,1,0:T(8,128)(2,1)}), bf16[8,32,128]{2,1,0:T(8,128)(2,1)S(1)}, u32[]{:S(2)}, u32[]{:S(2)}) async-start(bf16[8,32,128]{2,1,0:T(8,128)(2,1)} %get-tuple-element.25.refs_1_), calls=%async_computation.1 | async-start | bytes 131072 | tf_op jit(solution)/shard_map/all_to_all | solution.py:20
  25.3 2.5 %prepare.1 = (bf16[192,256]{1,0:T(8,128)(2,1)S(1)}, bf16[256,192]{1,0:T(8,128)(2,1)S(1)}, f32[192,192]{1,0:T(8,128)S(1)}, f32[192,256]{1,0:T(8,128)S(1)}, f32[32...) custom-call(s32[1]{0:T(128)} %bitcast.5.refs_0_, ...), custom_call_target="tpu_custom_call" | custom-call | flops 314572800 | bytes 1048576 | tf_op jit(solution)/shard_map/prepare/pallas_call | solution.py:95
  27.7 3.2 %all-to-all-done.1.refs_0_ = bf16[8,32,128]{2,1,0:T(8,128)(2,1)S(1)} async-done(((bf16[8,32,128]{2,1,0:T(8,128)(2,1)}), bf16[8,32,128]{2,1,0:T(8,128)(2,1)S(1)}, u32[]{:S(2)}, u32[]{:S(2)}) %all-to-all-start.1) | async-done | bytes 65568 | tf_op jit(solution)/shard_map/all_to_all | solution.py:20
  30.9 3.0 %cache.1.refs_2_ = bf16[8,64,128]{2,1,0:T(8,128)(2,1)} custom-call(bf16[8,32,128]{2,1,0:T(8,128)(2,1)S(1)} %all-to-all-done.1.refs_0_, bf16[192,256]{1,0:T(8,128)(2,1)S(1)} %get-tuple-element.28.refs_1_, bf16[256,192]{1,0:T(8,128)(2,1)S(1)} %get-tuple-element.29.refs_2_, f32[192,192]{1,0:T(8,128)S(1)} %get-tuple-element.30.refs_3_, ...), custom_call_target="tpu_custom_call" | custom-call | flops 1258291200 | bytes 4194304 | tf_op jit(solution)/shard_map/cache/pallas_call | solution.py:95
  33.9 3.4 %all-to-all-start.2 = ((bf16[8,64,128]{2,1,0:T(8,128)(2,1)}), bf16[8,64,128]{2,1,0:T(8,128)(2,1)S(1)}, u32[]{:S(2)}, u32[]{:S(2)}) async-start(bf16[8,64,128]{2,1,0:T(8,128)(2,1)} %cache.1.refs_2_), calls=%async_computation.2 | async-start | bytes 262144 | tf_op jit(solution)/shard_map/all_to_all | solution.py:20
  37.3 1.1 %join.2 = (bf16[2,1536,128]{2,1,0:T(8,128)(2,1)S(1)}, bf16[128,1024]{1,0:T(8,128)(2,1)S(1)}, f32[1,1024]{1,0:T(1,128)S(1)}) custom-call(bf16[1,1536,128]{2,1,0:T(8,128)(2,1)S(1)} %get-tuple-element.35.refs_0_, bf16[1,1536,128]{2,1,0:T(8,128)(2,1)} %collective-permute-done.refs_1_, bf16[8,64,128]{2,1,0:T(8,128)(2,1)} %cache.1.refs_2_, ...), custom_call_target="tpu_custom_call" | custom-call | flops 1258291200 | bytes 4194304 | tf_op jit(solution)/shard_map/join/pallas_call | solution.py:95
  38.4 5.1 %collective-permute-start.1 = (bf16[2,1536,128]{2,1,0:T(8,128)(2,1)S(1)}, bf16[2,1536,128]{2,1,0:T(8,128)(2,1)}, u32[]{:S(2)}, u32[]{:S(2)}) collective-permute-start(bf16[2,1536,128]{2,1,0:T(8,128)(2,1)S(1)} %get-tuple-element.39.refs_0_), channel_id=1, source_target_pairs={{0,48},{8,56},{16,32},{24,40},{32,16},{40,24},{48,0},{56,8},{1,49}... | collective-permute-start | bytes 2359304 | tf_op jit(solution)/shard_map/ppermute | solution.py:24
  43.5 1.2 %finish.1.refs_2_ = bf16[8,32,1024]{2,1,0:T(8,128)(2,1)} custom-call(bf16[8,64,128]{2,1,0:T(8,128)(2,1)S(1)} %all-to-all-done.2.refs_0_, f32[32,128]{1,0:T(8,128)S(1)} %get-tuple-element.33.refs_1_, f32[32,128]{1,0:T(8,128)S(1)} %get-tuple-element.34.refs_2_, bf16[128,1024]{1,0:T(8,128)(2,1)S(1)} %get-tuple-element.36.refs_3_), custom_call_target="tpu_custom_call" | custom-call | flops 9437184000 | bytes 31457280 | tf_op jit(solution)/shard_map/finish/pallas_call | solution.py:95
  44.7 5.1 %all-to-all-start.3 = ((bf16[8,32,1024]{2,1,0:T(8,128)(2,1)}), bf16[8,32,1024]{2,1,0:T(8,128)(2,1)S(1)}, u32[]{:S(2)}, u32[]{:S(2)}) async-start(bf16[8,32,1024]{2,1,0:T(8,128)(2,1)} %finish.1.refs_2_), calls=%async_computation.3 | async-start | bytes 1048576 | tf_op jit(solution)/shard_map/all_to_all | solution.py:20
  49.8 11.7 %collective-permute-done.1.refs_1_ = bf16[2,1536,128]{2,1,0:T(8,128)(2,1)} collective-permute-done((bf16[2,1536,128]{2,1,0:T(8,128)(2,1)S(1)}, bf16[2,1536,128]{2,1,0:T(8,128)(2,1)}, u32[]{:S(2)}, u32[]{:S(2)}) %collective-permute-start.1) | collective-permute-done | bytes 786464 | tf_op jit(solution)/shard_map/ppermute | solution.py:24
  61.4 1.1 %join.3.refs_1_ = bf16[4,1536,128]{2,1,0:T(8,128)(2,1)S(1)} custom-call(bf16[2,1536,128]{2,1,0:T(8,128)(2,1)S(1)} %get-tuple-element.39.refs_0_, bf16[2,1536,128]{2,1,0:T(8,128)(2,1)} %collective-permute-done.1.refs_1_, bf16[8,32,1024]{2,1,0:T(8,128)(2,1)} %finish.1.refs_2_), custom_call_target="tpu_custom_call" | custom-call | flops 1258291200 | bytes 4194304 | tf_op jit(solution)/shard_map/join/pallas_call | solution.py:95
  62.6 1.9 %collective-permute-start.2 = (bf16[4,1536,128]{2,1,0:T(8,128)(2,1)S(1)}, bf16[4,1536,128]{2,1,0:T(8,128)(2,1)}, u32[]{:S(2)}, u32[]{:S(2)}) collective-permute-start(bf16[4,1536,128]{2,1,0:T(8,128)(2,1)S(1)} %join.3.refs_1_), channel_id=1, source_target_pairs={{0,8},{8,0},{16,24},{24,16},{32,40},{40,32},{48,56},{56,48},{1,9},... | collective-permute-start | bytes 4718600 | tf_op jit(solution)/shard_map/ppermute | solution.py:24
  64.5 2.8 %all-to-all-done.3.refs_0_ = bf16[8,32,1024]{2,1,0:T(8,128)(2,1)S(1)} async-done(((bf16[8,32,1024]{2,1,0:T(8,128)(2,1)}), bf16[8,32,1024]{2,1,0:T(8,128)(2,1)S(1)}, u32[]{:S(2)}, u32[]{:S(2)}) %all-to-all-start.3) | async-done | bytes 524320 | tf_op jit(solution)/shard_map/all_to_all | solution.py:20
  68.0 2.8 %feed.1 = bf16[8,4,1024]{2,1,0:T(4,128)(2,1)} custom-call(bf16[32,1024]{1,0:T(8,128)(2,1)S(1)} %get-tuple-element.38.refs_0_, bf16[4,1536,128]{2,1,0:T(8,128)(2,1)S(1)} %join.3.refs_1_, bf16[4,1536,128]{2,1,0:T(8,128)(2,1)} %collective-permute-done.2.refs_2_), custom_call_target="tpu_custom_call" | custom-call | flops 1258291200 | bytes 4194304 | tf_op jit(solution)/shard_map/feed/pallas_call | solution.py:95
  70.9 5.1 %all-to-all-start.4 = ((bf16[8,4,1024]{2,1,0:T(4,128)(2,1)}), bf16[8,4,1024]{2,1,0:T(4,128)(2,1)S(1)}, u32[]{:S(2)}, u32[]{:S(2)}) async-start(bf16[8,4,1024]{2,1,0:T(4,128)(2,1)} %feed.1), calls=%async_computation.4 | async-start | bytes 131072 | tf_op jit(solution)/shard_map/all_to_all | solution.py:20
  76.0 8.4 %all-to-all-done.4.refs_1_ = bf16[8,4,1024]{2,1,0:T(4,128)(2,1)S(1)} async-done(((bf16[8,4,1024]{2,1,0:T(4,128)(2,1)}), bf16[8,4,1024]{2,1,0:T(4,128)(2,1)S(1)}, u32[]{:S(2)}, u32[]{:S(2)}) %all-to-all-start.4) | async-done | bytes 65568 | tf_op jit(solution)/shard_map/all_to_all | solution.py:20
  (8 shorter events, 1.4 us)
Async XLA Ops:
  1.3 18.7 %all-to-all-start = ((bf16[8,4,1024]{2,1,0:T(4,128)(2,1)}), bf16[8,4,1024]{2,1,0:T(4,128)(2,1)S(1)}, u32[]{:S(2)}, u32[]{:S(2)}) async-start(bf16[8,4,1024]{2,1,0:T(4,128)(2,1)} %broadcast_in_dim.8), calls=%async_computation | async-start | bytes 131072 | tf_op jit(solution)/shard_map/all_to_all | solution.py:20
  13.0 17.9 %copy-start = (bf16[24,256,128]{2,1,0:T(8,128)(2,1)S(1)}, bf16[24,256,128]{2,1,0:T(8,128)(2,1)}, u32[]{:S(2)}) copy-start(bf16[24,256,128]{2,1,0:T(8,128)(2,1)} %refs_5_.1) | copy-start | bytes 4718596
  13.0 24.3 %collective-permute-start = (bf16[1,1536,128]{2,1,0:T(8,128)(2,1)S(1)}, bf16[1,1536,128]{2,1,0:T(8,128)(2,1)}, u32[]{:S(2)}, u32[]{:S(2)}) collective-permute-start(bf16[1,1536,128]{2,1,0:T(8,128)(2,1)S(1)} %get-tuple-element.35.refs_0_), channel_id=1, source_target_pairs={{0,16},{8,24},{16,0},{24,8},{32,48},{40,56},{48,32},{56,40},{1,17}... | collective-permute-start | bytes 1179656 | tf_op jit(solution)/shard_map/ppermute | solution.py:24
  21.0 9.9 %all-to-all-start.1 = ((bf16[8,32,128]{2,1,0:T(8,128)(2,1)}), bf16[8,32,128]{2,1,0:T(8,128)(2,1)S(1)}, u32[]{:S(2)}, u32[]{:S(2)}) async-start(bf16[8,32,128]{2,1,0:T(8,128)(2,1)} %get-tuple-element.25.refs_1_), calls=%async_computation.1 | async-start | bytes 131072 | tf_op jit(solution)/shard_map/all_to_all | solution.py:20
  33.9 9.6 %all-to-all-start.2 = ((bf16[8,64,128]{2,1,0:T(8,128)(2,1)}), bf16[8,64,128]{2,1,0:T(8,128)(2,1)S(1)}, u32[]{:S(2)}, u32[]{:S(2)}) async-start(bf16[8,64,128]{2,1,0:T(8,128)(2,1)} %cache.1.refs_2_), calls=%async_computation.2 | async-start | bytes 262144 | tf_op jit(solution)/shard_map/all_to_all | solution.py:20
  38.4 23.1 %collective-permute-start.1 = (bf16[2,1536,128]{2,1,0:T(8,128)(2,1)S(1)}, bf16[2,1536,128]{2,1,0:T(8,128)(2,1)}, u32[]{:S(2)}, u32[]{:S(2)}) collective-permute-start(bf16[2,1536,128]{2,1,0:T(8,128)(2,1)S(1)} %get-tuple-element.39.refs_0_), channel_id=1, source_target_pairs={{0,48},{8,56},{16,32},{24,40},{32,16},{40,24},{48,0},{56,8},{1,49}... | collective-permute-start | bytes 2359304 | tf_op jit(solution)/shard_map/ppermute | solution.py:24
  44.7 22.6 %all-to-all-start.3 = ((bf16[8,32,1024]{2,1,0:T(8,128)(2,1)}), bf16[8,32,1024]{2,1,0:T(8,128)(2,1)S(1)}, u32[]{:S(2)}, u32[]{:S(2)}) async-start(bf16[8,32,1024]{2,1,0:T(8,128)(2,1)} %finish.1.refs_2_), calls=%async_computation.3 | async-start | bytes 1048576 | tf_op jit(solution)/shard_map/all_to_all | solution.py:20
  62.6 5.4 %collective-permute-start.2 = (bf16[4,1536,128]{2,1,0:T(8,128)(2,1)S(1)}, bf16[4,1536,128]{2,1,0:T(8,128)(2,1)}, u32[]{:S(2)}, u32[]{:S(2)}) collective-permute-start(bf16[4,1536,128]{2,1,0:T(8,128)(2,1)S(1)} %join.3.refs_1_), channel_id=1, source_target_pairs={{0,8},{8,0},{16,24},{24,16},{32,40},{40,32},{48,56},{56,48},{1,9},... | collective-permute-start | bytes 4718600 | tf_op jit(solution)/shard_map/ppermute | solution.py:24
  70.9 13.5 %all-to-all-start.4 = ((bf16[8,4,1024]{2,1,0:T(4,128)(2,1)}), bf16[8,4,1024]{2,1,0:T(4,128)(2,1)S(1)}, u32[]{:S(2)}, u32[]{:S(2)}) async-start(bf16[8,4,1024]{2,1,0:T(4,128)(2,1)} %feed.1), calls=%async_computation.4 | async-start | bytes 131072 | tf_op jit(solution)/shard_map/all_to_all | solution.py:20

commit v3 on v2

--- a/solution.py
+++ b/solution.py
@@ -263,7 +263,9 @@
         1.0,
         0.0,
     ).astype(jnp.bfloat16)
-    same_ref[...] = jnp.where((owner == owner_lane) & (row_in == lane_in), 0.0, FAR)
+    same_ref[...] = jnp.where(
+        (owner == owner_lane) & (row_in == lane_in), 0.0, FAR
+    ).astype(jnp.bfloat16)
 
     limit = jnp.where(owned, found & 511, 0)
     variate = (found >> (9 + 2 * step_row)) & 3
@@ -322,7 +324,7 @@
     scores = jnp.where(live, scores * scale + bias_mask, MASKED_SCORE)
     slot_top = jnp.max(scores, axis=1, keepdims=True)
     top_lane = jnp.transpose(jnp.broadcast_to(slot_top, (rows, LANES)))[0:1, :]
-    row_top = jnp.max(top_lane + same_ref[...], axis=1, keepdims=True)
+    row_top = jnp.max(top_lane + same_ref[...].astype(jnp.float32), axis=1, keepdims=True)
     weights = jnp.where(live, jnp.exp(scores - row_top), 0.0)
     total = jnp.sum(weights, axis=1, keepdims=True)
     arrive()
@@ -503,7 +505,7 @@
         loads=[gate_up.reshape(width, lanes), w_down.reshape(units, width)],
         carried=[w_qkv.transpose(1, 0, 2), attn_gain[None, :]],
     )()
-    ffn_next = swapped(ffn_weights, [2, 3, 0, 1, 6, 7, 4, 5])
+    ffn_next = swapped(ffn_weights, [2, 7, 0, 5, 6, 3, 4, 1])
 
     own_len = lax.dynamic_slice_in_dim(cache_len, seq_at * own_requests, own_requests, 0)
     cosine, sine = rotation_tables(own_len, steps)
@@ -517,13 +519,13 @@
     all_queries = exchange(queries, "seq")
 
     slot_rows = 2 * steps * slots
-    early = slots // 3
+    early = slots // 2
     pick, place, same, bias_mask, fresh, fresh_lse, held_values = kernel_call(
         lambda *refs: prepare_body(steps, slots, scale, *refs),
         [
             shape((slot_rows, requests * steps), bf16),
             shape((requests * steps, slot_rows), bf16),
-            shape((slot_rows, slot_rows), f32),
+            shape((slot_rows, slot_rows), bf16),
             shape((slot_rows, piece_len), f32),
             shape((rows, lanes), f32),
             shape((rows, lanes), f32),
@@ -550,7 +552,7 @@
     )
     partial = exchange(partial, "seq")
 
-    ffn_far = swapped(ffn_weights, [6, 7, 4, 5, 2, 3, 0, 1])
+    ffn_far = swapped(ffn_weights, [6, 3, 4, 1, 2, 7, 0, 5])
     mid_parts = kernel_call(
         finish_body,
         shape((tps, rows, width), bf16),

time: 86 us -> 82.7 us (0.962)
  starting transfers between devices: 38.7 us -> 37 us
  waiting for transfers between devices: 28.3 us -> 27.4 us
    ppermute x3, waiting for transfers between devices: 12.2 us -> 3.81 us  [swapped(): return lax.ppermute(blocks, 'seq', list(enumerate(partner)))]
    all_to_all x5, waiting for transfers between devices: 16.1 us -> 23.5 us  [exchange(): return lax.all_to_all(pieces, axes, 0, 0, tiled=True)]
    all_to_all x5, starting transfers between devices: 28.2 us -> 26.5 us  [exchange(): return lax.all_to_all(pieces, axes, 0, 0, tiled=True)]
  transfers between devices with their start and end apart: 8 -> 8, of which waited for: 6 -> 5; matrix products, arithmetic and copies ran while one was open for 2% -> 2% of each run, Pallas kernels for 13% -> 13%
where the time goes in v3:
time: 82.7 us; the launch traced here: 81.8 us
  starting transfers between devices  37 us (45%)
  waiting for transfers between devices  27.4 us (33%)
  Pallas kernels  14.4 us (17%)
  local copies, waits for them, and re-layouts  2.07 us (3%)
  other arithmetic  0.94 us (1%)
    all_to_all x5, starting transfers between devices, exchange(): return lax.all_to_all(pieces, axes, 0, 0, tiled=True)  26.5 us
    all_to_all x5, waiting for transfers between devices, exchange(): return lax.all_to_all(pieces, axes, 0, 0, tiled=True)  23.5 us
    pallas_call x10, Pallas kernels, kernel_call(): call(*ins, *[stay_in_hbm(a.array) for a in (*loads, *small, *carried)])  14.4 us
    ppermute x3, starting transfers between devices, swapped(): return lax.ppermute(blocks, 'seq', list(enumerate(partner)))  10.5 us
    ppermute x3, waiting for transfers between devices, swapped(): return lax.ppermute(blocks, 'seq', list(enumerate(partner)))  3.81 us
  transfers between devices with their start and end apart: 8, of which 5 were waited for; matrix products, arithmetic and copies ran while one was open for 2% of the time, Pallas kernels for 13%

profile of v3, /device:TPU:56, one launch (start us, length us, event | category | flops | bytes accessed | tf_op | source)
XLA Modules:
  0.0 81.8 jit_solution(8306461124020698481)
XLA Ops:
  0.0 1.3 %broadcast_in_dim.8 = bf16[8,4,1024]{2,1,0:T(4,128)(2,1)} broadcast(bf16[4,1024]{1,0:T(4,128)(2,1)} %param.16), dimensions={1,2} | broadcast | bytes 73728 | tf_op jit(solution)/shard_map/broadcast_in_dim | solution.py:496
  1.3 10.3 %all-to-all-start = ((bf16[8,4,1024]{2,1,0:T(4,128)(2,1)}), bf16[8,4,1024]{2,1,0:T(4,128)(2,1)S(1)}, u32[]{:S(2)}, u32[]{:S(2)}) async-start(bf16[8,4,1024]{2,1,0:T(4,128)(2,1)} %broadcast_in_dim.8), calls=%async_computation | async-start | bytes 131072 | tf_op jit(solution)/shard_map/all_to_all | solution.py:20
  11.6 1.3 %pack.1 = (bf16[1,1536,128]{2,1,0:T(8,128)(2,1)S(1)}, bf16[3,1024,128]{2,1,0:T(8,128)(2,1)S(1)}, f32[1,1024]{1,0:T(1,128)S(1)}) custom-call(bf16[1024,128]{1,0:T(8,128)(2,1)} %bitcast.10, bf16[64,1024]{1,0:T(8,128)(2,1)} %bitcast.11, bf16[3,1024,128]{2,1,0:T(8,128)(2,1)} %bitcast.9, f32[1,1024]{1,0:T(1,128)} %bitcast.12), custom_call_target="tpu_custom_call" | custom-call | flops 314572800 | bytes 1048576 | tf_op jit(solution)/shard_map/pack/pallas_call | solution.py:95
  13.0 3.5 %collective-permute-start = (bf16[1,1536,128]{2,1,0:T(8,128)(2,1)S(1)}, bf16[1,1536,128]{2,1,0:T(8,128)(2,1)}, u32[]{:S(2)}, u32[]{:S(2)}) collective-permute-start(bf16[1,1536,128]{2,1,0:T(8,128)(2,1)S(1)} %get-tuple-element.35.refs_0_), channel_id=1, source_target_pairs={{0,16},{8,56},{16,0},{24,40},{32,48},{40,24},{48,32},{56,8},{1,17}... | collective-permute-start | bytes 1179656 | tf_op jit(solution)/shard_map/ppermute | solution.py:24
  16.5 0.7 dynamic_slice.3
  17.3 0.9 %fusion = (f32[8,4,128]{2,1,0:T(4,128)S(1)}, f32[8,4,128]{2,1,0:T(4,128)S(1)}) fusion(f32[128]{0:T(128)} %constant.18.clone, f32[128]{0:T(128)} %constant.17.clone, f32[8,4]{1,0:T(8,128)S(1)} %add_convert_fusion), kind=kLoop, calls=%fused_computation.2 | loop fusion | flops 8192 | bytes 33920 | tf_op jit(solution)/shard_map/mul | solution.py:465
  18.2 1.8 %all-to-all-done.refs_0_.refs_1_ = bf16[8,4,1024]{2,1,0:T(4,128)(2,1)S(1)} async-done(((bf16[8,4,1024]{2,1,0:T(4,128)(2,1)}), bf16[8,4,1024]{2,1,0:T(4,128)(2,1)S(1)}, u32[]{:S(2)}, u32[]{:S(2)}) %all-to-all-start) | async-done | bytes 65568 | tf_op jit(solution)/shard_map/all_to_all | solution.py:20
  20.0 0.9 %project.1 = (bf16[8,32,128]{2,1,0:T(8,128)(2,1)}, bf16[32,128]{1,0:T(8,128)(2,1)S(1)}, bf16[32,128]{1,0:T(8,128)(2,1)S(1)}) custom-call(bf16[8,4,1024]{2,1,0:T(4,128)(2,1)S(1)} %all-to-all-done.refs_0_.refs_1_, f32[8,4,128]{2,1,0:T(4,128)S(1)} %get-tuple-element.42.refs_1_, f32[8,4,128]{2,1,0:T(4,128)S(1)} %get-tuple-element.41.refs_2_, ...), custom_call_target="tpu_custom_call" | custom-call | flops 314572800 | bytes 1048576 | tf_op jit(solution)/shard_map/project/pallas_call | solution.py:95
  21.0 4.3 %all-to-all-start.1 = ((bf16[8,32,128]{2,1,0:T(8,128)(2,1)}), bf16[8,32,128]{2,1,0:T(8,128)(2,1)S(1)}, u32[]{:S(2)}, u32[]{:S(2)}) async-start(bf16[8,32,128]{2,1,0:T(8,128)(2,1)} %get-tuple-element.25.refs_1_), calls=%async_computation.1 | async-start | bytes 131072 | tf_op jit(solution)/shard_map/all_to_all | solution.py:20
  25.3 2.5 %prepare.1 = (bf16[192,256]{1,0:T(8,128)(2,1)S(1)}, bf16[256,192]{1,0:T(8,128)(2,1)S(1)}, bf16[192,192]{1,0:T(8,128)(2,1)S(1)}, f32[192,256]{1,0:T(8,128)S(1)}, ...) custom-call(s32[1]{0:T(128)} %bitcast.5.refs_0_, ...), custom_call_target="tpu_custom_call" | custom-call | flops 314572800 | bytes 1048576 | tf_op jit(solution)/shard_map/prepare/pallas_call | solution.py:95
  27.7 3.2 %all-to-all-done.1.refs_0_ = bf16[8,32,128]{2,1,0:T(8,128)(2,1)S(1)} async-done(((bf16[8,32,128]{2,1,0:T(8,128)(2,1)}), bf16[8,32,128]{2,1,0:T(8,128)(2,1)S(1)}, u32[]{:S(2)}, u32[]{:S(2)}) %all-to-all-start.1) | async-done | bytes 65568 | tf_op jit(solution)/shard_map/all_to_all | solution.py:20
  30.9 2.6 %cache.1.refs_2_ = bf16[8,64,128]{2,1,0:T(8,128)(2,1)} custom-call(bf16[8,32,128]{2,1,0:T(8,128)(2,1)S(1)} %all-to-all-done.1.refs_0_, bf16[192,256]{1,0:T(8,128)(2,1)S(1)} %get-tuple-element.28.refs_1_, bf16[256,192]{1,0:T(8,128)(2,1)S(1)} %get-tuple-element.29.refs_2_, bf16[192,192]{1,0:T(8,128)(2,1)S(1)} %get-tuple-element.30.refs_3_, ...), custom_call_target="tpu_custom_call" | custom-call | flops 1258291200 | bytes 4194304 | tf_op jit(solution)/shard_map/cache/pallas_call | solution.py:95
  33.5 3.4 %all-to-all-start.2 = ((bf16[8,64,128]{2,1,0:T(8,128)(2,1)}), bf16[8,64,128]{2,1,0:T(8,128)(2,1)S(1)}, u32[]{:S(2)}, u32[]{:S(2)}) async-start(bf16[8,64,128]{2,1,0:T(8,128)(2,1)} %cache.1.refs_2_), calls=%async_computation.2 | async-start | bytes 262144 | tf_op jit(solution)/shard_map/all_to_all | solution.py:20
  36.9 1.1 %join.2 = (bf16[2,1536,128]{2,1,0:T(8,128)(2,1)S(1)}, bf16[128,1024]{1,0:T(8,128)(2,1)S(1)}, f32[1,1024]{1,0:T(1,128)S(1)}) custom-call(bf16[1,1536,128]{2,1,0:T(8,128)(2,1)S(1)} %get-tuple-element.35.refs_0_, bf16[1,1536,128]{2,1,0:T(8,128)(2,1)} %collective-permute-done.refs_1_, bf16[8,64,128]{2,1,0:T(8,128)(2,1)} %cache.1.refs_2_, ...), custom_call_target="tpu_custom_call" | custom-call | flops 1258291200 | bytes 4194304 | tf_op jit(solution)/shard_map/join/pallas_call | solution.py:95
  38.0 5.1 %collective-permute-start.1 = (bf16[2,1536,128]{2,1,0:T(8,128)(2,1)S(1)}, bf16[2,1536,128]{2,1,0:T(8,128)(2,1)}, u32[]{:S(2)}, u32[]{:S(2)}) collective-permute-start(bf16[2,1536,128]{2,1,0:T(8,128)(2,1)S(1)} %get-tuple-element.39.refs_0_), channel_id=1, source_target_pairs={{0,48},{8,24},{16,32},{24,8},{32,16},{40,56},{48,0},{56,40},{1,49}... | collective-permute-start | bytes 2359304 | tf_op jit(solution)/shard_map/ppermute | solution.py:24
  43.1 1.2 %finish.1.refs_2_ = bf16[8,32,1024]{2,1,0:T(8,128)(2,1)} custom-call(bf16[8,64,128]{2,1,0:T(8,128)(2,1)S(1)} %all-to-all-done.2.refs_0_, f32[32,128]{1,0:T(8,128)S(1)} %get-tuple-element.33.refs_1_, f32[32,128]{1,0:T(8,128)S(1)} %get-tuple-element.34.refs_2_, bf16[128,1024]{1,0:T(8,128)(2,1)S(1)} %get-tuple-element.36.refs_3_), custom_call_target="tpu_custom_call" | custom-call | flops 9437184000 | bytes 31457280 | tf_op jit(solution)/shard_map/finish/pallas_call | solution.py:95
  44.3 5.1 %all-to-all-start.3 = ((bf16[8,32,1024]{2,1,0:T(8,128)(2,1)}), bf16[8,32,1024]{2,1,0:T(8,128)(2,1)S(1)}, u32[]{:S(2)}, u32[]{:S(2)}) async-start(bf16[8,32,1024]{2,1,0:T(8,128)(2,1)} %finish.1.refs_2_), calls=%async_computation.3 | async-start | bytes 1048576 | tf_op jit(solution)/shard_map/all_to_all | solution.py:20
  49.4 3.8 %collective-permute-done.1.refs_1_ = bf16[2,1536,128]{2,1,0:T(8,128)(2,1)} collective-permute-done((bf16[2,1536,128]{2,1,0:T(8,128)(2,1)S(1)}, bf16[2,1536,128]{2,1,0:T(8,128)(2,1)}, u32[]{:S(2)}, u32[]{:S(2)}) %collective-permute-start.1) | collective-permute-done | bytes 786464 | tf_op jit(solution)/shard_map/ppermute | solution.py:24
  53.2 1.1 %join.3.refs_1_ = bf16[4,1536,128]{2,1,0:T(8,128)(2,1)S(1)} custom-call(bf16[2,1536,128]{2,1,0:T(8,128)(2,1)S(1)} %get-tuple-element.39.refs_0_, bf16[2,1536,128]{2,1,0:T(8,128)(2,1)} %collective-permute-done.1.refs_1_, bf16[8,32,1024]{2,1,0:T(8,128)(2,1)} %finish.1.refs_2_), custom_call_target="tpu_custom_call" | custom-call | flops 1258291200 | bytes 4194304 | tf_op jit(solution)/shard_map/join/pallas_call | solution.py:95
  54.3 1.9 %collective-permute-start.2 = (bf16[4,1536,128]{2,1,0:T(8,128)(2,1)S(1)}, bf16[4,1536,128]{2,1,0:T(8,128)(2,1)}, u32[]{:S(2)}, u32[]{:S(2)}) collective-permute-start(bf16[4,1536,128]{2,1,0:T(8,128)(2,1)S(1)} %join.3.refs_1_), channel_id=1, source_target_pairs={{0,8},{8,0},{16,24},{24,16},{32,40},{40,32},{48,56},{56,48},{1,9},... | collective-permute-start | bytes 4718600 | tf_op jit(solution)/shard_map/ppermute | solution.py:24
  56.3 10.3 %all-to-all-done.3.refs_0_ = bf16[8,32,1024]{2,1,0:T(8,128)(2,1)S(1)} async-done(((bf16[8,32,1024]{2,1,0:T(8,128)(2,1)}), bf16[8,32,1024]{2,1,0:T(8,128)(2,1)S(1)}, u32[]{:S(2)}, u32[]{:S(2)}) %all-to-all-start.3) | async-done | bytes 524320 | tf_op jit(solution)/shard_map/all_to_all | solution.py:20
  66.7 2.8 %feed.1 = bf16[8,4,1024]{2,1,0:T(4,128)(2,1)} custom-call(bf16[32,1024]{1,0:T(8,128)(2,1)S(1)} %get-tuple-element.38.refs_0_, bf16[4,1536,128]{2,1,0:T(8,128)(2,1)S(1)} %join.3.refs_1_, bf16[4,1536,128]{2,1,0:T(8,128)(2,1)} %collective-permute-done.2.refs_2_), custom_call_target="tpu_custom_call" | custom-call | flops 1258291200 | bytes 4194304 | tf_op jit(solution)/shard_map/feed/pallas_call | solution.py:95
  69.6 3.4 %all-to-all-start.4 = ((bf16[8,4,1024]{2,1,0:T(4,128)(2,1)}), bf16[8,4,1024]{2,1,0:T(4,128)(2,1)S(1)}, u32[]{:S(2)}, u32[]{:S(2)}) async-start(bf16[8,4,1024]{2,1,0:T(4,128)(2,1)} %feed.1), calls=%async_computation.4 | async-start | bytes 131072 | tf_op jit(solution)/shard_map/all_to_all | solution.py:20
  72.9 8.3 %all-to-all-done.4.refs_1_ = bf16[8,4,1024]{2,1,0:T(4,128)(2,1)S(1)} async-done(((bf16[8,4,1024]{2,1,0:T(4,128)(2,1)}), bf16[8,4,1024]{2,1,0:T(4,128)(2,1)S(1)}, u32[]{:S(2)}, u32[]{:S(2)}) %all-to-all-start.4) | async-done | bytes 65568 | tf_op jit(solution)/shard_map/all_to_all | solution.py:20
  (8 shorter events, 0.9 us)
Async XLA Ops:
  1.3 18.7 %all-to-all-start = ((bf16[8,4,1024]{2,1,0:T(4,128)(2,1)}), bf16[8,4,1024]{2,1,0:T(4,128)(2,1)S(1)}, u32[]{:S(2)}, u32[]{:S(2)}) async-start(bf16[8,4,1024]{2,1,0:T(4,128)(2,1)} %broadcast_in_dim.8), calls=%async_computation | async-start | bytes 131072 | tf_op jit(solution)/shard_map/all_to_all | solution.py:20
  13.0 17.9 %copy-start = (bf16[24,256,128]{2,1,0:T(8,128)(2,1)S(1)}, bf16[24,256,128]{2,1,0:T(8,128)(2,1)}, u32[]{:S(2)}) copy-start(bf16[24,256,128]{2,1,0:T(8,128)(2,1)} %refs_5_.1) | copy-start | bytes 4718596
  13.0 23.9 %collective-permute-start = (bf16[1,1536,128]{2,1,0:T(8,128)(2,1)S(1)}, bf16[1,1536,128]{2,1,0:T(8,128)(2,1)}, u32[]{:S(2)}, u32[]{:S(2)}) collective-permute-start(bf16[1,1536,128]{2,1,0:T(8,128)(2,1)S(1)} %get-tuple-element.35.refs_0_), channel_id=1, source_target_pairs={{0,16},{8,56},{16,0},{24,40},{32,48},{40,24},{48,32},{56,8},{1,17}... | collective-permute-start | bytes 1179656 | tf_op jit(solution)/shard_map/ppermute | solution.py:24
  21.0 9.9 %all-to-all-start.1 = ((bf16[8,32,128]{2,1,0:T(8,128)(2,1)}), bf16[8,32,128]{2,1,0:T(8,128)(2,1)S(1)}, u32[]{:S(2)}, u32[]{:S(2)}) async-start(bf16[8,32,128]{2,1,0:T(8,128)(2,1)} %get-tuple-element.25.refs_1_), calls=%async_computation.1 | async-start | bytes 131072 | tf_op jit(solution)/shard_map/all_to_all | solution.py:20
  33.5 9.6 %all-to-all-start.2 = ((bf16[8,64,128]{2,1,0:T(8,128)(2,1)}), bf16[8,64,128]{2,1,0:T(8,128)(2,1)S(1)}, u32[]{:S(2)}, u32[]{:S(2)}) async-start(bf16[8,64,128]{2,1,0:T(8,128)(2,1)} %cache.1.refs_2_), calls=%async_computation.2 | async-start | bytes 262144 | tf_op jit(solution)/shard_map/all_to_all | solution.py:20
  38.0 15.2 %collective-permute-start.1 = (bf16[2,1536,128]{2,1,0:T(8,128)(2,1)S(1)}, bf16[2,1536,128]{2,1,0:T(8,128)(2,1)}, u32[]{:S(2)}, u32[]{:S(2)}) collective-permute-start(bf16[2,1536,128]{2,1,0:T(8,128)(2,1)S(1)} %get-tuple-element.39.refs_0_), channel_id=1, source_target_pairs={{0,48},{8,24},{16,32},{24,8},{32,16},{40,56},{48,0},{56,40},{1,49}... | collective-permute-start | bytes 2359304 | tf_op jit(solution)/shard_map/ppermute | solution.py:24
  44.3 22.3 %all-to-all-start.3 = ((bf16[8,32,1024]{2,1,0:T(8,128)(2,1)}), bf16[8,32,1024]{2,1,0:T(8,128)(2,1)S(1)}, u32[]{:S(2)}, u32[]{:S(2)}) async-start(bf16[8,32,1024]{2,1,0:T(8,128)(2,1)} %finish.1.refs_2_), calls=%async_computation.3 | async-start | bytes 1048576 | tf_op jit(solution)/shard_map/all_to_all | solution.py:20
  54.3 12.4 %collective-permute-start.2 = (bf16[4,1536,128]{2,1,0:T(8,128)(2,1)S(1)}, bf16[4,1536,128]{2,1,0:T(8,128)(2,1)}, u32[]{:S(2)}, u32[]{:S(2)}) collective-permute-start(bf16[4,1536,128]{2,1,0:T(8,128)(2,1)S(1)} %join.3.refs_1_), channel_id=1, source_target_pairs={{0,8},{8,0},{16,24},{24,16},{32,40},{40,32},{48,56},{56,48},{1,9},... | collective-permute-start | bytes 4718600 | tf_op jit(solution)/shard_map/ppermute | solution.py:24
  69.6 11.7 %all-to-all-start.4 = ((bf16[8,4,1024]{2,1,0:T(4,128)(2,1)}), bf16[8,4,1024]{2,1,0:T(4,128)(2,1)S(1)}, u32[]{:S(2)}, u32[]{:S(2)}) async-start(bf16[8,4,1024]{2,1,0:T(4,128)(2,1)} %feed.1), calls=%async_computation.4 | async-start | bytes 131072 | tf_op jit(solution)/shard_map/all_to_all | solution.py:20

commit v4 on v3

--- a/solution.py
+++ b/solution.py
@@ -144,6 +144,51 @@
         carried=carried,
         scratch=[pltpu.SemaphoreType.DMA(())],
     )(first, stay_in_hbm(second), after)
+
+
+def extend_body(_, first_ref, far_ref, after_ref, out_ref, held_ref, last_ref, sems):
+    count = first_ref.shape[0]
+    kept = held_ref.shape[0]
+    far = [
+        pltpu.make_async_copy(far_ref.at[pl.ds(0, kept)], held_ref, sems.at[0]),
+        pltpu.make_async_copy(far_ref.at[pl.ds(kept, kept)], last_ref, sems.at[1]),
+    ]
+    out = [
+        pltpu.make_async_copy(first_ref, out_ref.at[pl.ds(0, count)], sems.at[2]),
+        pltpu.make_async_copy(held_ref, out_ref.at[pl.ds(count, kept)], sems.at[3]),
+        pltpu.make_async_copy(last_ref, out_ref.at[pl.ds(count + kept, kept)], sems.at[4]),
+    ]
+    for move in (*far, out[0]):
+        move.start()
+    for i in range(2):
+        far[i].wait()
+        out[i + 1].start()
+    for move in out:
+        move.wait()
+
+
+def extended(first, far, after):
+    count, kept = first.shape[0], far.shape[0] // 2
+    return pl.pallas_call(
+        lambda *refs: extend_body(None, *refs),
+        out_shape=[
+            jax.ShapeDtypeStruct((2 * count, *first.shape[1:]), first.dtype),
+            jax.ShapeDtypeStruct((kept, *first.shape[1:]), first.dtype),
+        ],
+        in_specs=in_vmem(1)
+        + [pl.BlockSpec(memory_space=pltpu.HBM), pl.BlockSpec(memory_space=pl.ANY)],
+        out_specs=[pl.BlockSpec(memory_space=pltpu.HBM), *in_vmem(1)],
+        scratch_shapes=[
+            pltpu.VMEM((kept, *first.shape[1:]), first.dtype),
+            pltpu.SemaphoreType.DMA((5,)),
+        ],
+        name="extend",
+        interpret=INTERPRET,
+        compiler_params=pltpu.CompilerParams(vmem_limit_bytes=8 << 20),
+        cost_estimate=pl.CostEstimate(
+            flops=300 * 4 << 20, bytes_accessed=4 << 20, transcendentals=0
+        ),
+    )(first, stay_in_hbm(far), after)
 
 
 def project_body(arrive, token_ref, cos_ref, sin_ref, gain_ref, w_ref, q_ref, k_ref, v_ref):
@@ -312,10 +357,17 @@
     row_head = iota((rows, LANES), 0) % group // steps
     head_match = row_head == iota((rows, LANES), 1) // HD
     picked = jnp.where(head_match, picked, 0.0)
+    doubled = jnp.concatenate([picked, picked], axis=1)
+    wide = doubled.shape
+    own_half = iota(wide, 0) // group % 2 == iota(wide, 1) // LANES
+    doubled = jnp.where(own_half, doubled, 0.0).astype(jnp.bfloat16)
     scores = jnp.concatenate(
         [
-            matmul_t(picked[group * s : group * (s + 1)].astype(jnp.bfloat16), k_ref[s])
-            for s in range(slots)
+            matmul_t(
+                doubled[group * s : group * (s + 2)],
+                jnp.concatenate([k_ref[s], k_ref[s + 1]], axis=1),
+            )
+            for s in range(0, slots, 2)
         ],
         axis=0,
     )
@@ -323,19 +375,35 @@
     live = bias_mask > 0.5 * MASKED_SCORE
     scores = jnp.where(live, scores * scale + bias_mask, MASKED_SCORE)
     slot_top = jnp.max(scores, axis=1, keepdims=True)
+    by_slot = jnp.where(pick_ref[...].astype(jnp.float32) > 0.5, slot_top, MASKED_SCORE)
+    tops = by_slot[:group]
+    for s in range(1, slots):
+        tops = jnp.maximum(tops, by_slot[group * s : group * (s + 1)])
+    tops = jnp.where(
+        iota(tops.shape, 0) == 0,
+        jnp.max(tops[:steps], axis=0, keepdims=True),
+        jnp.max(tops[steps:], axis=0, keepdims=True),
+    )
+    tops = jnp.transpose(tops)
     top_lane = jnp.transpose(jnp.broadcast_to(slot_top, (rows, LANES)))[0:1, :]
     row_top = jnp.max(top_lane + same_ref[...].astype(jnp.float32), axis=1, keepdims=True)
     weights = jnp.where(live, jnp.exp(scores - row_top), 0.0)
     total = jnp.sum(weights, axis=1, keepdims=True)
     arrive()
     values = [r.at[i] for r in (early_v_ref, late_v_ref) for i in range(r.shape[0])]
+    weights = weights.astype(jnp.bfloat16)
     mixed = jnp.concatenate(
         [
-            matmul(weights[group * s : group * (s + 1)].astype(jnp.bfloat16), values[s][...])
-            for s in range(slots)
+            matmul(
+                weights[group * s : group * (s + 2)],
+                jnp.concatenate([values[s][...], values[s + 1][...]], axis=1),
+            )
+            for s in range(0, slots, 2)
         ],
         axis=0,
     )
+    mixed = jnp.where(iota(mixed.shape, 0) // group % 2 == iota(mixed.shape, 1) // LANES, mixed, 0.0)
+    mixed = mixed[:, :LANES] + mixed[:, LANES:]
     both = jnp.concatenate(
         [jnp.where(head_match, mixed, 0.0), jnp.where(head_match, total, 0.0)], axis=1
     )
@@ -343,14 +411,8 @@
     place = place_ref[...]
     summed = matmul(place, high) + matmul(place, low)
     out_sum, total_sum = summed[:, :LANES], summed[:, LANES:]
-    lane_head = iota((1, rows), 1) % group // steps
-    placed = place.astype(jnp.float32) > 0.5
-    tops = [
-        jnp.max(jnp.where(placed & (lane_head == h), top_lane, MASKED_SCORE), axis=1, keepdims=True)
-        for h in range(2)
-    ]
     low_lanes = iota(out_sum.shape, 1) < HD
-    top = jnp.where(low_lanes, tops[0], tops[1])
+    top = jnp.where(low_lanes, tops[:, 0:1], tops[:, 1:2])
     some = total_sum > 0.0
     safe_total = jnp.where(some, total_sum, 1.0)
     averaged = jnp.where(some, out_sum / safe_total, 0.0).astype(jnp.bfloat16)
@@ -413,23 +475,20 @@
     normed_ref[...] = scaled_rows(mid, gain_ref[...])
 
 
-def feed_body(_, normed_ref, own_w_ref, near_hbm_ref, out_ref, near_w_ref, sems):
-    count = near_w_ref.shape[0]
-    moves = [
-        pltpu.make_async_copy(near_hbm_ref.at[i], near_w_ref.at[i], sems.at[i])
-        for i in range(count)
-    ]
-    for move in moves:
-        move.start()
+def feed_body(_, normed_ref, own_w_ref, near_w_ref, held_w_ref, far_ref, out_ref, last_w_ref, sem):
+    move = pltpu.make_async_copy(
+        far_ref.at[pl.ds(held_w_ref.shape[0], last_w_ref.shape[0])], last_w_ref, sem
+    )
+    move.start()
     own = out_ref.shape[1]
     normed = normed_ref[...]
     width = normed.shape[1]
-    blocks = [r.at[i] for r in (own_w_ref, near_w_ref) for i in range(count)]
+    refs = (own_w_ref, near_w_ref, held_w_ref, last_w_ref)
+    blocks = [r.at[i] for r in refs for i in range(r.shape[0])]
     halves = []
-    for s in range(0, 2 * count, 2):
-        if s >= count:
-            moves[s - count].wait()
-            moves[s - count + 1].wait()
+    for s in range(0, len(blocks), 2):
+        if s + 2 == len(blocks):
+            move.wait()
         halves.append(gated(normed, blocks[s : s + 2]))
     hidden = jnp.concatenate(halves, axis=1).astype(jnp.bfloat16)
     for c in range(0, width // LANES, 2):
@@ -560,9 +619,9 @@
         "finish",
         moved=30 << 20,
     )(partial, fresh, fresh_lse, out_weights)
-    ffn_weights = joined(ffn_weights, ffn_far, mid_parts)
+    ffn_all, ffn_held = extended(ffn_weights, ffn_far, mid_parts)
     mid_parts = exchange(mid_parts, "tp")
-    ffn_near = swapped(ffn_weights, [1, 0, 3, 2, 5, 4, 7, 6])
+    ffn_near = swapped(ffn_all, [1, 0, 3, 2, 5, 4, 7, 6])
     normed, mid = kernel_call(
         settle_body,
         [shape((rows, width), bf16), shape((tps, row_count, width), f32)],
@@ -573,14 +632,11 @@
     ffn_parts = kernel_call(
         feed_body,
         shape((tps, row_count, width), bf16),
-        in_vmem(2) + [pl.BlockSpec(memory_space=pltpu.HBM)],
+        in_vmem(4) + [pl.BlockSpec(memory_space=pltpu.HBM)],
         "feed",
         moved=4 << 20,
-        scratch=[
-            pltpu.VMEM(ffn_near.shape, bf16),
-            pltpu.SemaphoreType.DMA((ffn_near.shape[0],)),
-        ],
-    )(normed, ffn_weights, stay_in_hbm(ffn_near))
+        scratch=[pltpu.VMEM(ffn_held.shape, bf16), pltpu.SemaphoreType.DMA(())],
+    )(normed, ffn_weights, ffn_near, ffn_held, stay_in_hbm(ffn_far))
     ffn_parts = exchange(ffn_parts, "tp")
     return kernel_call(
         last_body, shape((row_count, width), bf16), in_smem(1) + in_vmem(2), "last", moved=1 << 17

time: 82.7 us -> 82.3 us (level)
  waiting for transfers between devices: 27.4 us -> 25.4 us
  local copies, waits for them, and re-layouts: 2.07 us -> 2.94 us
    pallas_call x0 -> x1, Pallas kernels: none -> 2.21 us  [extended(): pl.pallas_call(lambda *refs: extend_body(None, *refs), out_shape=[jax.Sha...]
    all_to_all x5, waiting for transfers between devices: 23.5 us -> 21.7 us  [exchange(): return lax.all_to_all(pieces, axes, 0, 0, tiled=True)]
    pallas_call x10 -> x9, Pallas kernels: 14.4 us -> 12.8 us  [kernel_call(): call(*ins, *[stay_in_hbm(a.array) for a in (*loads, *small, *carried)])]
    unnamed x2 -> x4, local copies, waits for them, and re-layouts: 0.01 us -> 0.88 us
  transfers between devices with their start and end apart: 8 -> 8, of which waited for: 5 -> 5; matrix products, arithmetic and copies ran while one was open for 2% -> 2% of each run, Pallas kernels for 13% -> 15%
where the time goes in v4:
time: 82.3 us; the launch traced here: 81.4 us
  starting transfers between devices  37 us (45%)
  waiting for transfers between devices  25.4 us (31%)
  Pallas kernels  15 us (18%)
  local copies, waits for them, and re-layouts  2.94 us (4%)
  other arithmetic  0.94 us (1%)
    all_to_all x5, starting transfers between devices, exchange(): return lax.all_to_all(pieces, axes, 0, 0, tiled=True)  26.5 us
    all_to_all x5, waiting for transfers between devices, exchange(): return lax.all_to_all(pieces, axes, 0, 0, tiled=True)  21.7 us
    pallas_call x9, Pallas kernels, kernel_call(): call(*ins, *[stay_in_hbm(a.array) for a in (*loads, *small, *carried)])  12.8 us
    ppermute x3, starting transfers between devices, swapped(): return lax.ppermute(blocks, 'seq', list(enumerate(partner)))  10.5 us
    ppermute x3, waiting for transfers between devices, swapped(): return lax.ppermute(blocks, 'seq', list(enumerate(partner)))  3.73 us
    pallas_call x1, Pallas kernels, extended(): pl.pallas_call(lambda *refs: extend_body(None, *refs), out_shape=[jax.Sha...  2.21 us
  transfers between devices with their start and end apart: 8, of which 5 were waited for; matrix products, arithmetic and copies ran while one was open for 2% of the time, Pallas kernels for 15%

profile of v4, /device:TPU:56, one launch (start us, length us, event | category | flops | bytes accessed | tf_op | source)
XLA Modules:
  0.0 81.4 jit_solution(16220875522605533885)
XLA Ops:
  0.0 1.3 %broadcast_in_dim.8 = bf16[8,4,1024]{2,1,0:T(4,128)(2,1)} broadcast(bf16[4,1024]{1,0:T(4,128)(2,1)} %param.16), dimensions={1,2} | broadcast | bytes 73728 | tf_op jit(solution)/shard_map/broadcast_in_dim | solution.py:555
  1.3 10.3 %all-to-all-start = ((bf16[8,4,1024]{2,1,0:T(4,128)(2,1)}), bf16[8,4,1024]{2,1,0:T(4,128)(2,1)S(1)}, u32[]{:S(2)}, u32[]{:S(2)}) async-start(bf16[8,4,1024]{2,1,0:T(4,128)(2,1)} %broadcast_in_dim.8), calls=%async_computation | async-start | bytes 131072 | tf_op jit(solution)/shard_map/all_to_all | solution.py:20
  11.6 1.3 %pack.1 = (bf16[1,1536,128]{2,1,0:T(8,128)(2,1)S(1)}, bf16[3,1024,128]{2,1,0:T(8,128)(2,1)S(1)}, f32[1,1024]{1,0:T(1,128)S(1)}) custom-call(bf16[1024,128]{1,0:T(8,128)(2,1)} %bitcast.10, bf16[64,1024]{1,0:T(8,128)(2,1)} %bitcast.11, bf16[3,1024,128]{2,1,0:T(8,128)(2,1)} %bitcast.9, f32[1,1024]{1,0:T(1,128)} %bitcast.12), custom_call_target="tpu_custom_call" | custom-call | flops 314572800 | bytes 1048576 | tf_op jit(solution)/shard_map/pack/pallas_call | solution.py:95
  13.0 3.5 %collective-permute-start = (bf16[1,1536,128]{2,1,0:T(8,128)(2,1)S(1)}, bf16[1,1536,128]{2,1,0:T(8,128)(2,1)}, u32[]{:S(2)}, u32[]{:S(2)}) collective-permute-start(bf16[1,1536,128]{2,1,0:T(8,128)(2,1)S(1)} %get-tuple-element.37.refs_0_), channel_id=1, source_target_pairs={{0,16},{8,56},{16,0},{24,40},{32,48},{40,24},{48,32},{56,8},{1,17}... | collective-permute-start | bytes 1179656 | tf_op jit(solution)/shard_map/ppermute | solution.py:24
  17.3 0.9 %fusion = (f32[8,4,128]{2,1,0:T(4,128)S(1)}, f32[8,4,128]{2,1,0:T(4,128)S(1)}) fusion(f32[128]{0:T(128)} %constant.18.clone, f32[128]{0:T(128)} %constant.17.clone, f32[8,4]{1,0:T(8,128)S(1)} %add_convert_fusion), kind=kLoop, calls=%fused_computation.2 | loop fusion | flops 8192 | bytes 33920 | tf_op jit(solution)/shard_map/mul | solution.py:524
  18.2 1.8 %all-to-all-done.refs_0_.refs_1_ = bf16[8,4,1024]{2,1,0:T(4,128)(2,1)S(1)} async-done(((bf16[8,4,1024]{2,1,0:T(4,128)(2,1)}), bf16[8,4,1024]{2,1,0:T(4,128)(2,1)S(1)}, u32[]{:S(2)}, u32[]{:S(2)}) %all-to-all-start) | async-done | bytes 65568 | tf_op jit(solution)/shard_map/all_to_all | solution.py:20
  20.0 0.9 %project.1 = (bf16[8,32,128]{2,1,0:T(8,128)(2,1)}, bf16[32,128]{1,0:T(8,128)(2,1)S(1)}, bf16[32,128]{1,0:T(8,128)(2,1)S(1)}) custom-call(bf16[8,4,1024]{2,1,0:T(4,128)(2,1)S(1)} %all-to-all-done.refs_0_.refs_1_, f32[8,4,128]{2,1,0:T(4,128)S(1)} %get-tuple-element.46.refs_1_, f32[8,4,128]{2,1,0:T(4,128)S(1)} %get-tuple-element.45.refs_2_, ...), custom_call_target="tpu_custom_call" | custom-call | flops 314572800 | bytes 1048576 | tf_op jit(solution)/shard_map/project/pallas_call | solution.py:95
  21.0 4.3 %all-to-all-start.1 = ((bf16[8,32,128]{2,1,0:T(8,128)(2,1)}), bf16[8,32,128]{2,1,0:T(8,128)(2,1)S(1)}, u32[]{:S(2)}, u32[]{:S(2)}) async-start(bf16[8,32,128]{2,1,0:T(8,128)(2,1)} %get-tuple-element.27.refs_1_), calls=%async_computation.1 | async-start | bytes 131072 | tf_op jit(solution)/shard_map/all_to_all | solution.py:20
  25.3 2.5 %prepare.1 = (bf16[192,256]{1,0:T(8,128)(2,1)S(1)}, bf16[256,192]{1,0:T(8,128)(2,1)S(1)}, bf16[192,192]{1,0:T(8,128)(2,1)S(1)}, f32[192,256]{1,0:T(8,128)S(1)}, ...) custom-call(s32[1]{0:T(128)} %bitcast.5.refs_0_, ...), custom_call_target="tpu_custom_call" | custom-call | flops 314572800 | bytes 1048576 | tf_op jit(solution)/shard_map/prepare/pallas_call | solution.py:95
  27.7 3.2 %all-to-all-done.1.refs_0_ = bf16[8,32,128]{2,1,0:T(8,128)(2,1)S(1)} async-done(((bf16[8,32,128]{2,1,0:T(8,128)(2,1)}), bf16[8,32,128]{2,1,0:T(8,128)(2,1)S(1)}, u32[]{:S(2)}, u32[]{:S(2)}) %all-to-all-start.1) | async-done | bytes 65568 | tf_op jit(solution)/shard_map/all_to_all | solution.py:20
  30.9 2.6 %cache.1.refs_2_ = bf16[8,64,128]{2,1,0:T(8,128)(2,1)} custom-call(bf16[8,32,128]{2,1,0:T(8,128)(2,1)S(1)} %all-to-all-done.1.refs_0_, bf16[192,256]{1,0:T(8,128)(2,1)S(1)} %get-tuple-element.30.refs_1_, bf16[256,192]{1,0:T(8,128)(2,1)S(1)} %get-tuple-element.31.refs_2_, bf16[192,192]{1,0:T(8,128)(2,1)S(1)} %get-tuple-element.32.refs_3_, ...), custom_call_target="tpu_custom_call" | custom-call | flops 1258291200 | bytes 4194304 | tf_op jit(solution)/shard_map/cache/pallas_call | solution.py:95
  33.5 3.4 %all-to-all-start.2 = ((bf16[8,64,128]{2,1,0:T(8,128)(2,1)}), bf16[8,64,128]{2,1,0:T(8,128)(2,1)S(1)}, u32[]{:S(2)}, u32[]{:S(2)}) async-start(bf16[8,64,128]{2,1,0:T(8,128)(2,1)} %cache.1.refs_2_), calls=%async_computation.2 | async-start | bytes 262144 | tf_op jit(solution)/shard_map/all_to_all | solution.py:20
  36.9 1.1 %join.1 = (bf16[2,1536,128]{2,1,0:T(8,128)(2,1)S(1)}, bf16[128,1024]{1,0:T(8,128)(2,1)S(1)}, f32[1,1024]{1,0:T(1,128)S(1)}) custom-call(bf16[1,1536,128]{2,1,0:T(8,128)(2,1)S(1)} %get-tuple-element.37.refs_0_, bf16[1,1536,128]{2,1,0:T(8,128)(2,1)} %collective-permute-done.refs_1_, bf16[8,64,128]{2,1,0:T(8,128)(2,1)} %cache.1.refs_2_, ...), custom_call_target="tpu_custom_call" | custom-call | flops 1258291200 | bytes 4194304 | tf_op jit(solution)/shard_map/join/pallas_call | solution.py:95
  38.0 5.1 %collective-permute-start.1 = (bf16[2,1536,128]{2,1,0:T(8,128)(2,1)S(1)}, bf16[2,1536,128]{2,1,0:T(8,128)(2,1)S(1)}, u32[]{:S(2)}, u32[]{:S(2)}) collective-permute-start(bf16[2,1536,128]{2,1,0:T(8,128)(2,1)S(1)} %get-tuple-element.41.refs_0_.refs_1_), channel_id=1, source_target_pairs={{0,48},{8,24},{16,32},{24,8},{32,16},{40,56},{48,0},{56,40},{1,49}... | collective-permute-start | bytes 2359304 | tf_op jit(solution)/shard_map/ppermute | solution.py:24
  43.1 1.2 %finish.1.refs_2_ = bf16[8,32,1024]{2,1,0:T(8,128)(2,1)} custom-call(bf16[8,64,128]{2,1,0:T(8,128)(2,1)S(1)} %all-to-all-done.2.refs_0_, f32[32,128]{1,0:T(8,128)S(1)} %get-tuple-element.35.refs_1_, f32[32,128]{1,0:T(8,128)S(1)} %get-tuple-element.36.refs_2_, bf16[128,1024]{1,0:T(8,128)(2,1)S(1)} %get-tuple-element.38.refs_3_), custom_call_target="tpu_custom_call" | custom-call | flops 9437184000 | bytes 31457280 | tf_op jit(solution)/shard_map/finish/pallas_call | solution.py:95
  44.3 5.1 %all-to-all-start.3 = ((bf16[8,32,1024]{2,1,0:T(8,128)(2,1)}), bf16[8,32,1024]{2,1,0:T(8,128)(2,1)S(1)}, u32[]{:S(2)}, u32[]{:S(2)}) async-start(bf16[8,32,1024]{2,1,0:T(8,128)(2,1)} %finish.1.refs_2_), calls=%async_computation.3 | async-start | bytes 1048576 | tf_op jit(solution)/shard_map/all_to_all | solution.py:20
  49.4 3.7 %collective-permute-done.1.refs_1_.refs_4_ = bf16[2,1536,128]{2,1,0:T(8,128)(2,1)S(1)} collective-permute-done((bf16[2,1536,128]{2,1,0:T(8,128)(2,1)S(1)}, bf16[2,1536,128]{2,1,0:T(8,128)(2,1)S(1)}, u32[]{:S(2)}, u32[]{:S(2)}) %collective-permute-start.1) | collective-permute-done | bytes 786464 | tf_op jit(solution)/shard_map/ppermute | solution.py:24
  53.1 0.9 %copy-done.1 = bf16[2,1536,128]{2,1,0:T(8,128)(2,1)} copy-done((bf16[2,1536,128]{2,1,0:T(8,128)(2,1)}, bf16[2,1536,128]{2,1,0:T(8,128)(2,1)S(1)}, u32[]{:S(2)}) %copy-start.1) | copy-done | bytes 786456
  54.0 2.2 %extend.1 = (bf16[4,1536,128]{2,1,0:T(8,128)(2,1)}, bf16[1,1536,128]{2,1,0:T(8,128)(2,1)S(1)}) custom-call(bf16[2,1536,128]{2,1,0:T(8,128)(2,1)S(1)} %get-tuple-element.41.refs_0_.refs_1_, bf16[2,1536,128]{2,1,0:T(8,128)(2,1)} %copy-done.1, bf16[8,32,1024]{2,1,0:T(8,128)(2,1)} %finish.1.refs_2_), custom_call_target="tpu_custom_call" | custom-call | flops 1258291200 | bytes 4194304 | tf_op jit(solution)/shard_map/extend/pallas_call | solution.py:172
  56.2 1.9 %collective-permute-start.2 = (bf16[4,1536,128]{2,1,0:T(8,128)(2,1)}, bf16[4,1536,128]{2,1,0:T(8,128)(2,1)S(1)}, u32[]{:S(2)}, u32[]{:S(2)}) collective-permute-start(bf16[4,1536,128]{2,1,0:T(8,128)(2,1)} %get-tuple-element.42), channel_id=1, source_target_pairs={{0,8},{8,0},{16,24},{24,16},{32,40},{40,32},{48,56},{56,48},{1,9},... | collective-permute-start | bytes 4718600 | tf_op jit(solution)/shard_map/ppermute | solution.py:24
  58.1 8.4 %all-to-all-done.3.refs_0_ = bf16[8,32,1024]{2,1,0:T(8,128)(2,1)S(1)} async-done(((bf16[8,32,1024]{2,1,0:T(8,128)(2,1)}), bf16[8,32,1024]{2,1,0:T(8,128)(2,1)S(1)}, u32[]{:S(2)}, u32[]{:S(2)}) %all-to-all-start.3) | async-done | bytes 524320 | tf_op jit(solution)/shard_map/all_to_all | solution.py:20
  66.7 2.4 %feed.1 = bf16[8,4,1024]{2,1,0:T(4,128)(2,1)} custom-call(bf16[32,1024]{1,0:T(8,128)(2,1)S(1)} %get-tuple-element.40.refs_0_, bf16[2,1536,128]{2,1,0:T(8,128)(2,1)S(1)} %get-tuple-element.41.refs_0_.refs_1_, bf16[4,1536,128]{2,1,0:T(8,128)(2,1)S(1)} %collective-permute-done.2.refs_2_, bf16[1,1536,128]{2,1,0:T(8,128)(2,1)S(1)} %get-tuple-element.43.refs_3_, ...), custom_call_target="tpu_custom_call" | custom-call | flops 1258291200 | bytes 4194304 | tf_op jit(solution)/shard_map/feed/pallas_call | solution.py:95
  69.2 3.4 %all-to-all-start.4 = ((bf16[8,4,1024]{2,1,0:T(4,128)(2,1)}), bf16[8,4,1024]{2,1,0:T(4,128)(2,1)S(1)}, u32[]{:S(2)}, u32[]{:S(2)}) async-start(bf16[8,4,1024]{2,1,0:T(4,128)(2,1)} %feed.1), calls=%async_computation.4 | async-start | bytes 131072 | tf_op jit(solution)/shard_map/all_to_all | solution.py:20
  72.5 8.3 %all-to-all-done.4.refs_1_ = bf16[8,4,1024]{2,1,0:T(4,128)(2,1)S(1)} async-done(((bf16[8,4,1024]{2,1,0:T(4,128)(2,1)}), bf16[8,4,1024]{2,1,0:T(4,128)(2,1)S(1)}, u32[]{:S(2)}, u32[]{:S(2)}) %all-to-all-start.4) | async-done | bytes 65568 | tf_op jit(solution)/shard_map/all_to_all | solution.py:20
  (10 shorter events, 1.6 us)
Async XLA Ops:
  1.3 18.7 %all-to-all-start = ((bf16[8,4,1024]{2,1,0:T(4,128)(2,1)}), bf16[8,4,1024]{2,1,0:T(4,128)(2,1)S(1)}, u32[]{:S(2)}, u32[]{:S(2)}) async-start(bf16[8,4,1024]{2,1,0:T(4,128)(2,1)} %broadcast_in_dim.8), calls=%async_computation | async-start | bytes 131072 | tf_op jit(solution)/shard_map/all_to_all | solution.py:20
  13.0 17.9 %copy-start = (bf16[24,256,128]{2,1,0:T(8,128)(2,1)S(1)}, bf16[24,256,128]{2,1,0:T(8,128)(2,1)}, u32[]{:S(2)}) copy-start(bf16[24,256,128]{2,1,0:T(8,128)(2,1)} %refs_5_.1) | copy-start | bytes 4718596
  13.0 23.9 %collective-permute-start = (bf16[1,1536,128]{2,1,0:T(8,128)(2,1)S(1)}, bf16[1,1536,128]{2,1,0:T(8,128)(2,1)}, u32[]{:S(2)}, u32[]{:S(2)}) collective-permute-start(bf16[1,1536,128]{2,1,0:T(8,128)(2,1)S(1)} %get-tuple-element.37.refs_0_), channel_id=1, source_target_pairs={{0,16},{8,56},{16,0},{24,40},{32,48},{40,24},{48,32},{56,8},{1,17}... | collective-permute-start | bytes 1179656 | tf_op jit(solution)/shard_map/ppermute | solution.py:24
  21.0 9.9 %all-to-all-start.1 = ((bf16[8,32,128]{2,1,0:T(8,128)(2,1)}), bf16[8,32,128]{2,1,0:T(8,128)(2,1)S(1)}, u32[]{:S(2)}, u32[]{:S(2)}) async-start(bf16[8,32,128]{2,1,0:T(8,128)(2,1)} %get-tuple-element.27.refs_1_), calls=%async_computation.1 | async-start | bytes 131072 | tf_op jit(solution)/shard_map/all_to_all | solution.py:20
  33.5 9.6 %all-to-all-start.2 = ((bf16[8,64,128]{2,1,0:T(8,128)(2,1)}), bf16[8,64,128]{2,1,0:T(8,128)(2,1)S(1)}, u32[]{:S(2)}, u32[]{:S(2)}) async-start(bf16[8,64,128]{2,1,0:T(8,128)(2,1)} %cache.1.refs_2_), calls=%async_computation.2 | async-start | bytes 262144 | tf_op jit(solution)/shard_map/all_to_all | solution.py:20
  38.0 15.1 %collective-permute-start.1 = (bf16[2,1536,128]{2,1,0:T(8,128)(2,1)S(1)}, bf16[2,1536,128]{2,1,0:T(8,128)(2,1)S(1)}, u32[]{:S(2)}, u32[]{:S(2)}) collective-permute-start(bf16[2,1536,128]{2,1,0:T(8,128)(2,1)S(1)} %get-tuple-element.41.refs_0_.refs_1_), channel_id=1, source_target_pairs={{0,48},{8,24},{16,32},{24,8},{32,16},{40,56},{48,0},{56,40},{1,49}... | collective-permute-start | bytes 2359304 | tf_op jit(solution)/shard_map/ppermute | solution.py:24
  44.3 22.3 %all-to-all-start.3 = ((bf16[8,32,1024]{2,1,0:T(8,128)(2,1)}), bf16[8,32,1024]{2,1,0:T(8,128)(2,1)S(1)}, u32[]{:S(2)}, u32[]{:S(2)}) async-start(bf16[8,32,1024]{2,1,0:T(8,128)(2,1)} %finish.1.refs_2_), calls=%async_computation.3 | async-start | bytes 1048576 | tf_op jit(solution)/shard_map/all_to_all | solution.py:20
  53.1 0.9 %copy-start.1 = (bf16[2,1536,128]{2,1,0:T(8,128)(2,1)}, bf16[2,1536,128]{2,1,0:T(8,128)(2,1)S(1)}, u32[]{:S(2)}) copy-start(bf16[2,1536,128]{2,1,0:T(8,128)(2,1)S(1)} %collective-permute-done.1.refs_1_.refs_4_) | copy-start | bytes 2359300
  56.2 10.5 %collective-permute-start.2 = (bf16[4,1536,128]{2,1,0:T(8,128)(2,1)}, bf16[4,1536,128]{2,1,0:T(8,128)(2,1)S(1)}, u32[]{:S(2)}, u32[]{:S(2)}) collective-permute-start(bf16[4,1536,128]{2,1,0:T(8,128)(2,1)} %get-tuple-element.42), channel_id=1, source_target_pairs={{0,8},{8,0},{16,24},{24,16},{32,40},{40,32},{48,56},{56,48},{1,9},... | collective-permute-start | bytes 4718600 | tf_op jit(solution)/shard_map/ppermute | solution.py:24
  69.2 11.7 %all-to-all-start.4 = ((bf16[8,4,1024]{2,1,0:T(4,128)(2,1)}), bf16[8,4,1024]{2,1,0:T(4,128)(2,1)S(1)}, u32[]{:S(2)}, u32[]{:S(2)}) async-start(bf16[8,4,1024]{2,1,0:T(4,128)(2,1)} %feed.1), calls=%async_computation.4 | async-start | bytes 131072 | tf_op jit(solution)/shard_map/all_to_all | solution.py:20

commit v5 on v4

--- a/solution.py
+++ b/solution.py
@@ -47,7 +47,7 @@
 
 
 def kernel_call(
-    body, out_shape, in_specs, name, moved, loads=(), small=(), carried=(), scratch=()
+    body, out_shape, in_specs, name, moved, loads=(), small=(), carried=(), scratch=(), spread=False
 ):
     loads, small, carried = (
         [a if isinstance(a, Part) else Part(a) for a in arrays] for arrays in (loads, small, carried)
@@ -81,11 +81,14 @@
         for move in moves[count:]:
             move.wait()
 
+    places = in_vmem(outs + more)
+    if spread:
+        places[0] = pl.BlockSpec(memory_space=pltpu.HBM)
     call = pl.pallas_call(
         run,
         out_shape=shapes if many or more else shapes[0],
         in_specs=list(in_specs) + [pl.BlockSpec(memory_space=pltpu.HBM)] * (count + more),
-        out_specs=in_vmem(outs + more) if many or more else in_vmem(1)[0],
+        out_specs=places if many or more else places[0],
         scratch_shapes=held + [pltpu.SemaphoreType.DMA(())] * (count + more) + list(scratch),
         name=name,
         interpret=INTERPRET,
@@ -191,7 +194,18 @@
     )(first, stay_in_hbm(far), after)
 
 
-def project_body(arrive, token_ref, cos_ref, sin_ref, gain_ref, w_ref, q_ref, k_ref, v_ref):
+def repeats(block_ref, out_ref, sems):
+    moves = [
+        pltpu.make_async_copy(block_ref, out_ref.at[i], sems.at[i]) for i in range(out_ref.shape[0])
+    ]
+    for move in moves:
+        move.start()
+    return moves
+
+
+def project_body(
+    _, token_ref, cos_ref, sin_ref, gain_ref, w_ref, q_ref, own_q_ref, k_ref, v_ref, sems
+):
     normed = scaled_rows(stacked(token_ref), gain_ref[...])
     cosine, sine = stacked(cos_ref), stacked(sin_ref)
     first_half = iota(cosine.shape, 1) % HD < HD // 2
@@ -204,15 +218,16 @@
         )
         return (part * cosine + partner * sine).astype(jnp.bfloat16)
 
-    queries = rotate(matmul(normed, w_ref[0]))
-    for i in range(q_ref.shape[0]):
-        q_ref[i] = queries
+    own_q_ref[...] = rotate(matmul(normed, w_ref[0]))
+    moves = repeats(own_q_ref, q_ref, sems)
     k_ref[...] = rotate(matmul(normed, w_ref[1]))
     v_ref[...] = matmul(normed, w_ref[2]).astype(jnp.bfloat16)
+    for move in moves:
+        move.wait()
 
 
 def fresh_part(steps, scale, packed, q_ref, k_ref, v_ref, bias_ref, out_ref, lse_ref):
-    queries = q_ref[0]
+    queries = q_ref[...]
     rows = queries.shape[0]
     packed = jnp.concatenate(
         [jnp.broadcast_to(packed[i : i + 1, :rows], (steps, rows)) for i in range(packed.shape[0])],
@@ -275,7 +290,7 @@
     columns = jnp.transpose(columns.astype(jnp.float32)).astype(jnp.int32)
     packed_variate, length = columns[:, 0:1], columns[:, 1:2]
     packed_ref[...] = jnp.broadcast_to(packed_variate, (requests, LANES))
-    own = requests // (requests * steps // q_ref.shape[1])
+    own = requests // (requests * steps // q_ref.shape[0])
     packed = packed_ref[pl.ds(pl.multiple_of(seq_ref[0] * own, own), own), :]
     fresh_part(steps, scale, packed, q_ref, k_ref, v_ref, bias_ref, fresh_ref, fresh_lse_ref)
 
@@ -409,7 +424,10 @@
     )
     high, low = two_terms(both)
     place = place_ref[...]
-    summed = matmul(place, high) + matmul(place, low)
+    half = place.shape[0] // 2
+    summed = jnp.concatenate(
+        [matmul(p, high) + matmul(p, low) for p in (place[:half], place[half:])], axis=0
+    )
     out_sum, total_sum = summed[:, :LANES], summed[:, LANES:]
     low_lanes = iota(out_sum.shape, 1) < HD
     top = jnp.where(low_lanes, tops[:, 0:1], tops[:, 1:2])
@@ -431,7 +449,7 @@
         out_ref[d, span:] = coded[span * d : span * (d + 1)]
 
 
-def finish_body(arrive, part_ref, fresh_ref, fresh_lse_ref, w_ref, out_ref):
+def finish_body(_, part_ref, fresh_ref, fresh_lse_ref, w_ref, out_ref, sum_ref, sems):
     devices = part_ref.shape[0]
     span = part_ref.shape[1] // 2
     source, lane = iota((LANES, LANES), 0), iota((LANES, LANES), 1)
@@ -449,9 +467,9 @@
         total = total + weight
         mixed = mixed + weight * part_ref[d, :span].astype(jnp.float32)
     attended = (mixed / total).astype(jnp.bfloat16)
-    partial = matmul(attended, w_ref[...]).astype(jnp.bfloat16)
-    for d in range(out_ref.shape[0]):
-        out_ref[d] = partial
+    sum_ref[...] = matmul(attended, w_ref[...]).astype(jnp.bfloat16)
+    for move in repeats(sum_ref, out_ref, sems):
+        move.wait()
 
 
 def gated(normed, blocks):
@@ -568,12 +586,14 @@
 
     own_len = lax.dynamic_slice_in_dim(cache_len, seq_at * own_requests, own_requests, 0)
     cosine, sine = rotation_tables(own_len, steps)
-    queries, keys_new, values_new = kernel_call(
+    queries, own_queries, keys_new, values_new = kernel_call(
         project_body,
-        [shape((seqs, rows, lanes), bf16), shape((rows, lanes), bf16), shape((rows, lanes), bf16)],
+        [shape((seqs, rows, lanes), bf16)] + [shape((rows, lanes), bf16)] * 3,
         in_vmem(5),
         "project",
         moved=1 << 20,
+        scratch=[pltpu.SemaphoreType.DMA((seqs,))],
+        spread=True,
     )(row_tokens, cosine, sine, qkv_gain, qkv_weights)
     all_queries = exchange(queries, "seq")
 
@@ -596,7 +616,7 @@
         small=[variate_bias],
         carried=[Part(cache_values, 0, early)],
         scratch=[pltpu.VMEM((requests, lanes), jnp.int32)],
-    )(seq_at.astype(jnp.int32).reshape(1), queries, keys_new, values_new)
+    )(seq_at.astype(jnp.int32).reshape(1), own_queries, keys_new, values_new)
 
     partial = kernel_call(
         lambda *refs: cache_body(steps, scale, *refs),
@@ -618,6 +638,8 @@
         in_vmem(4),
         "finish",
         moved=30 << 20,
+        scratch=[pltpu.VMEM((rows, width), bf16), pltpu.SemaphoreType.DMA((tps,))],
+        spread=True,
     )(partial, fresh, fresh_lse, out_weights)
     ffn_all, ffn_held = extended(ffn_weights, ffn_far, mid_parts)
     mid_parts = exchange(mid_parts, "tp")

time: 82.3 us -> 82.4 us (level)
  waiting for transfers between devices: 25.4 us -> 26.3 us
    all_to_all x5, waiting for transfers between devices: 21.7 us -> 22.6 us  [exchange(): return lax.all_to_all(pieces, axes, 0, 0, tiled=True)]
  transfers between devices with their start and end apart: 8 -> 8, of which waited for: 5 -> 5; matrix products, arithmetic and copies ran while one was open for 2% -> 2% of each run, Pallas kernels for 15% -> 14%
where the time goes in v5:
time: 82.4 us; the launch traced here: 81.6 us
  starting transfers between devices  37 us (45%)
  waiting for transfers between devices  26.3 us (32%)
  Pallas kernels  14.3 us (17%)
  local copies, waits for them, and re-layouts  2.94 us (4%)
  other arithmetic  0.94 us (1%)
    all_to_all x5, starting transfers between devices, exchange(): return lax.all_to_all(pieces, axes, 0, 0, tiled=True)  26.5 us
    all_to_all x5, waiting for transfers between devices, exchange(): return lax.all_to_all(pieces, axes, 0, 0, tiled=True)  22.6 us
    pallas_call x9, Pallas kernels, kernel_call(): call(*ins, *[stay_in_hbm(a.array) for a in (*loads, *small, *carried)])  12 us
    ppermute x3, starting transfers between devices, swapped(): return lax.ppermute(blocks, 'seq', list(enumerate(partner)))  10.5 us
    ppermute x3, waiting for transfers between devices, swapped(): return lax.ppermute(blocks, 'seq', list(enumerate(partner)))  3.66 us
    pallas_call x1, Pallas kernels, extended(): pl.pallas_call(lambda *refs: extend_body(None, *refs), out_shape=[jax.Sha...  2.21 us
  transfers between devices with their start and end apart: 8, of which 5 were waited for; matrix products, arithmetic and copies ran while one was open for 2% of the time, Pallas kernels for 14%

profile of v5, /device:TPU:56, one launch (start us, length us, event | category | flops | bytes accessed | tf_op | source)
XLA Modules:
  0.0 81.6 jit_solution(10346484156539043926)
XLA Ops:
  0.0 1.3 %broadcast_in_dim.8 = bf16[8,4,1024]{2,1,0:T(4,128)(2,1)} broadcast(bf16[4,1024]{1,0:T(4,128)(2,1)} %param.16), dimensions={1,2} | broadcast | bytes 73728 | tf_op jit(solution)/shard_map/broadcast_in_dim | solution.py:573
  1.3 10.3 %all-to-all-start = ((bf16[8,4,1024]{2,1,0:T(4,128)(2,1)}), bf16[8,4,1024]{2,1,0:T(4,128)(2,1)S(1)}, u32[]{:S(2)}, u32[]{:S(2)}) async-start(bf16[8,4,1024]{2,1,0:T(4,128)(2,1)} %broadcast_in_dim.8), calls=%async_computation | async-start | bytes 131072 | tf_op jit(solution)/shard_map/all_to_all | solution.py:20
  11.6 1.3 %pack.1 = (bf16[1,1536,128]{2,1,0:T(8,128)(2,1)S(1)}, bf16[3,1024,128]{2,1,0:T(8,128)(2,1)S(1)}, f32[1,1024]{1,0:T(1,128)S(1)}) custom-call(bf16[1024,128]{1,0:T(8,128)(2,1)} %bitcast.10, bf16[64,1024]{1,0:T(8,128)(2,1)} %bitcast.11, bf16[3,1024,128]{2,1,0:T(8,128)(2,1)} %bitcast.9, f32[1,1024]{1,0:T(1,128)} %bitcast.12), custom_call_target="tpu_custom_call" | custom-call | flops 314572800 | bytes 1048576 | tf_op jit(solution)/shard_map/pack/pallas_call | solution.py:98
  13.0 3.5 %collective-permute-start = (bf16[1,1536,128]{2,1,0:T(8,128)(2,1)S(1)}, bf16[1,1536,128]{2,1,0:T(8,128)(2,1)}, u32[]{:S(2)}, u32[]{:S(2)}) collective-permute-start(bf16[1,1536,128]{2,1,0:T(8,128)(2,1)S(1)} %get-tuple-element.39.refs_0_), channel_id=1, source_target_pairs={{0,16},{8,56},{16,0},{24,40},{32,48},{40,24},{48,32},{56,8},{1,17}... | collective-permute-start | bytes 1179656 | tf_op jit(solution)/shard_map/ppermute | solution.py:24
  17.3 0.9 %fusion = (f32[8,4,128]{2,1,0:T(4,128)S(1)}, f32[8,4,128]{2,1,0:T(4,128)S(1)}) fusion(f32[128]{0:T(128)} %constant.18.clone, f32[128]{0:T(128)} %constant.17.clone, f32[8,4]{1,0:T(8,128)S(1)} %add_convert_fusion), kind=kLoop, calls=%fused_computation.2 | loop fusion | flops 8192 | bytes 33920 | tf_op jit(solution)/shard_map/mul | solution.py:542
  18.2 1.8 %all-to-all-done.refs_0_.refs_1_ = bf16[8,4,1024]{2,1,0:T(4,128)(2,1)S(1)} async-done(((bf16[8,4,1024]{2,1,0:T(4,128)(2,1)}), bf16[8,4,1024]{2,1,0:T(4,128)(2,1)S(1)}, u32[]{:S(2)}, u32[]{:S(2)}) %all-to-all-start) | async-done | bytes 65568 | tf_op jit(solution)/shard_map/all_to_all | solution.py:20
  20.0 1.0 %project.1 = (bf16[8,32,128]{2,1,0:T(8,128)(2,1)}, bf16[32,128]{1,0:T(8,128)(2,1)S(1)}, bf16[32,128]{1,0:T(8,128)(2,1)S(1)}, bf16[32,128]{1,0:T(8,128)(2,1)S(1)}) custom-call(bf16[8,4,1024]{2,1,0:T(4,128)(2,1)S(1)} %all-to-all-done.refs_0_.refs_1_, f32[8,4,128]{2,1,0:T(4,128)S(1)} %get-tuple-element.48.refs_1_, f32[8,4,128]{2,1,0:T(4,128)S(1)} %get-tuple-element.47.refs_2_, ...), custom_call_target="tpu_custom_call" | custom-call | flops 314572800 | bytes 1048576 | tf_op jit(solution)/shard_map/project/pallas_call | solution.py:98
  21.0 4.3 %all-to-all-start.1 = ((bf16[8,32,128]{2,1,0:T(8,128)(2,1)}), bf16[8,32,128]{2,1,0:T(8,128)(2,1)S(1)}, u32[]{:S(2)}, u32[]{:S(2)}) async-start(bf16[8,32,128]{2,1,0:T(8,128)(2,1)} %get-tuple-element.28), calls=%async_computation.1 | async-start | bytes 131072 | tf_op jit(solution)/shard_map/all_to_all | solution.py:20
  25.4 1.6 %prepare.1 = (bf16[192,256]{1,0:T(8,128)(2,1)S(1)}, bf16[256,192]{1,0:T(8,128)(2,1)S(1)}, bf16[192,192]{1,0:T(8,128)(2,1)S(1)}, f32[192,256]{1,0:T(8,128)S(1)}, ...) custom-call(s32[1]{0:T(128)} %bitcast.5.refs_0_, ...), custom_call_target="tpu_custom_call" | custom-call | flops 314572800 | bytes 1048576 | tf_op jit(solution)/shard_map/prepare/pallas_call | solution.py:98
  27.0 4.0 %all-to-all-done.1.refs_0_ = bf16[8,32,128]{2,1,0:T(8,128)(2,1)S(1)} async-done(((bf16[8,32,128]{2,1,0:T(8,128)(2,1)}), bf16[8,32,128]{2,1,0:T(8,128)(2,1)S(1)}, u32[]{:S(2)}, u32[]{:S(2)}) %all-to-all-start.1) | async-done | bytes 65568 | tf_op jit(solution)/shard_map/all_to_all | solution.py:20
  31.0 2.6 %cache.1.refs_2_ = bf16[8,64,128]{2,1,0:T(8,128)(2,1)} custom-call(bf16[8,32,128]{2,1,0:T(8,128)(2,1)S(1)} %all-to-all-done.1.refs_0_, bf16[192,256]{1,0:T(8,128)(2,1)S(1)} %get-tuple-element.32.refs_1_, bf16[256,192]{1,0:T(8,128)(2,1)S(1)} %get-tuple-element.33.refs_2_, bf16[192,192]{1,0:T(8,128)(2,1)S(1)} %get-tuple-element.34.refs_3_, ...), custom_call_target="tpu_custom_call" | custom-call | flops 1258291200 | bytes 4194304 | tf_op jit(solution)/shard_map/cache/pallas_call | solution.py:98
  33.6 3.4 %all-to-all-start.2 = ((bf16[8,64,128]{2,1,0:T(8,128)(2,1)}), bf16[8,64,128]{2,1,0:T(8,128)(2,1)S(1)}, u32[]{:S(2)}, u32[]{:S(2)}) async-start(bf16[8,64,128]{2,1,0:T(8,128)(2,1)} %cache.1.refs_2_), calls=%async_computation.2 | async-start | bytes 262144 | tf_op jit(solution)/shard_map/all_to_all | solution.py:20
  37.0 1.1 %join.1 = (bf16[2,1536,128]{2,1,0:T(8,128)(2,1)S(1)}, bf16[128,1024]{1,0:T(8,128)(2,1)S(1)}, f32[1,1024]{1,0:T(1,128)S(1)}) custom-call(bf16[1,1536,128]{2,1,0:T(8,128)(2,1)S(1)} %get-tuple-element.39.refs_0_, bf16[1,1536,128]{2,1,0:T(8,128)(2,1)} %collective-permute-done.refs_1_, bf16[8,64,128]{2,1,0:T(8,128)(2,1)} %cache.1.refs_2_, ...), custom_call_target="tpu_custom_call" | custom-call | flops 1258291200 | bytes 4194304 | tf_op jit(solution)/shard_map/join/pallas_call | solution.py:98
  38.1 5.1 %collective-permute-start.1 = (bf16[2,1536,128]{2,1,0:T(8,128)(2,1)S(1)}, bf16[2,1536,128]{2,1,0:T(8,128)(2,1)S(1)}, u32[]{:S(2)}, u32[]{:S(2)}) collective-permute-start(bf16[2,1536,128]{2,1,0:T(8,128)(2,1)S(1)} %get-tuple-element.43.refs_0_.refs_1_), channel_id=1, source_target_pairs={{0,48},{8,24},{16,32},{24,8},{32,16},{40,56},{48,0},{56,40},{1,49}... | collective-permute-start | bytes 2359304 | tf_op jit(solution)/shard_map/ppermute | solution.py:24
  43.2 1.2 %finish.1.refs_2_ = bf16[8,32,1024]{2,1,0:T(8,128)(2,1)} custom-call(bf16[8,64,128]{2,1,0:T(8,128)(2,1)S(1)} %all-to-all-done.2.refs_0_, f32[32,128]{1,0:T(8,128)S(1)} %get-tuple-element.37.refs_1_, f32[32,128]{1,0:T(8,128)S(1)} %get-tuple-element.38.refs_2_, bf16[128,1024]{1,0:T(8,128)(2,1)S(1)} %get-tuple-element.40.refs_3_), custom_call_target="tpu_custom_call" | custom-call | flops 9437184000 | bytes 31457280 | tf_op jit(solution)/shard_map/finish/pallas_call | solution.py:98
  44.4 5.1 %all-to-all-start.3 = ((bf16[8,32,1024]{2,1,0:T(8,128)(2,1)}), bf16[8,32,1024]{2,1,0:T(8,128)(2,1)S(1)}, u32[]{:S(2)}, u32[]{:S(2)}) async-start(bf16[8,32,1024]{2,1,0:T(8,128)(2,1)} %finish.1.refs_2_), calls=%async_computation.3 | async-start | bytes 1048576 | tf_op jit(solution)/shard_map/all_to_all | solution.py:20
  49.5 3.7 %collective-permute-done.1.refs_1_.refs_4_ = bf16[2,1536,128]{2,1,0:T(8,128)(2,1)S(1)} collective-permute-done((bf16[2,1536,128]{2,1,0:T(8,128)(2,1)S(1)}, bf16[2,1536,128]{2,1,0:T(8,128)(2,1)S(1)}, u32[]{:S(2)}, u32[]{:S(2)}) %collective-permute-start.1) | collective-permute-done | bytes 786464 | tf_op jit(solution)/shard_map/ppermute | solution.py:24
  53.2 0.9 %copy-done.1 = bf16[2,1536,128]{2,1,0:T(8,128)(2,1)} copy-done((bf16[2,1536,128]{2,1,0:T(8,128)(2,1)}, bf16[2,1536,128]{2,1,0:T(8,128)(2,1)S(1)}, u32[]{:S(2)}) %copy-start.1) | copy-done | bytes 786456
  54.1 2.2 %extend.1 = (bf16[4,1536,128]{2,1,0:T(8,128)(2,1)}, bf16[1,1536,128]{2,1,0:T(8,128)(2,1)S(1)}) custom-call(bf16[2,1536,128]{2,1,0:T(8,128)(2,1)S(1)} %get-tuple-element.43.refs_0_.refs_1_, bf16[2,1536,128]{2,1,0:T(8,128)(2,1)} %copy-done.1, bf16[8,32,1024]{2,1,0:T(8,128)(2,1)} %finish.1.refs_2_), custom_call_target="tpu_custom_call" | custom-call | flops 1258291200 | bytes 4194304 | tf_op jit(solution)/shard_map/extend/pallas_call | solution.py:175
  56.3 1.9 %collective-permute-start.2 = (bf16[4,1536,128]{2,1,0:T(8,128)(2,1)}, bf16[4,1536,128]{2,1,0:T(8,128)(2,1)S(1)}, u32[]{:S(2)}, u32[]{:S(2)}) collective-permute-start(bf16[4,1536,128]{2,1,0:T(8,128)(2,1)} %get-tuple-element.44), channel_id=1, source_target_pairs={{0,8},{8,0},{16,24},{24,16},{32,40},{40,32},{48,56},{56,48},{1,9},... | collective-permute-start | bytes 4718600 | tf_op jit(solution)/shard_map/ppermute | solution.py:24
  58.2 8.5 %all-to-all-done.3.refs_0_ = bf16[8,32,1024]{2,1,0:T(8,128)(2,1)S(1)} async-done(((bf16[8,32,1024]{2,1,0:T(8,128)(2,1)}), bf16[8,32,1024]{2,1,0:T(8,128)(2,1)S(1)}, u32[]{:S(2)}, u32[]{:S(2)}) %all-to-all-start.3) | async-done | bytes 524320 | tf_op jit(solution)/shard_map/all_to_all | solution.py:20
  66.9 2.4 %feed.1 = bf16[8,4,1024]{2,1,0:T(4,128)(2,1)} custom-call(bf16[32,1024]{1,0:T(8,128)(2,1)S(1)} %get-tuple-element.42.refs_0_, bf16[2,1536,128]{2,1,0:T(8,128)(2,1)S(1)} %get-tuple-element.43.refs_0_.refs_1_, bf16[4,1536,128]{2,1,0:T(8,128)(2,1)S(1)} %collective-permute-done.2.refs_2_, bf16[1,1536,128]{2,1,0:T(8,128)(2,1)S(1)} %get-tuple-element.45.refs_3_, ...), custom_call_target="tpu_custom_call" | custom-call | flops 1258291200 | bytes 4194304 | tf_op jit(solution)/shard_map/feed/pallas_call | solution.py:98
  69.3 3.4 %all-to-all-start.4 = ((bf16[8,4,1024]{2,1,0:T(4,128)(2,1)}), bf16[8,4,1024]{2,1,0:T(4,128)(2,1)S(1)}, u32[]{:S(2)}, u32[]{:S(2)}) async-start(bf16[8,4,1024]{2,1,0:T(4,128)(2,1)} %feed.1), calls=%async_computation.4 | async-start | bytes 131072 | tf_op jit(solution)/shard_map/all_to_all | solution.py:20
  72.7 8.3 %all-to-all-done.4.refs_1_ = bf16[8,4,1024]{2,1,0:T(4,128)(2,1)S(1)} async-done(((bf16[8,4,1024]{2,1,0:T(4,128)(2,1)}), bf16[8,4,1024]{2,1,0:T(4,128)(2,1)S(1)}, u32[]{:S(2)}, u32[]{:S(2)}) %all-to-all-start.4) | async-done | bytes 65568 | tf_op jit(solution)/shard_map/all_to_all | solution.py:20
  (10 shorter events, 1.6 us)
Async XLA Ops:
  1.3 18.7 %all-to-all-start = ((bf16[8,4,1024]{2,1,0:T(4,128)(2,1)}), bf16[8,4,1024]{2,1,0:T(4,128)(2,1)S(1)}, u32[]{:S(2)}, u32[]{:S(2)}) async-start(bf16[8,4,1024]{2,1,0:T(4,128)(2,1)} %broadcast_in_dim.8), calls=%async_computation | async-start | bytes 131072 | tf_op jit(solution)/shard_map/all_to_all | solution.py:20
  13.0 18.0 %copy-start = (bf16[24,256,128]{2,1,0:T(8,128)(2,1)S(1)}, bf16[24,256,128]{2,1,0:T(8,128)(2,1)}, u32[]{:S(2)}) copy-start(bf16[24,256,128]{2,1,0:T(8,128)(2,1)} %refs_5_.1) | copy-start | bytes 4718596
  13.0 24.0 %collective-permute-start = (bf16[1,1536,128]{2,1,0:T(8,128)(2,1)S(1)}, bf16[1,1536,128]{2,1,0:T(8,128)(2,1)}, u32[]{:S(2)}, u32[]{:S(2)}) collective-permute-start(bf16[1,1536,128]{2,1,0:T(8,128)(2,1)S(1)} %get-tuple-element.39.refs_0_), channel_id=1, source_target_pairs={{0,16},{8,56},{16,0},{24,40},{32,48},{40,24},{48,32},{56,8},{1,17}... | collective-permute-start | bytes 1179656 | tf_op jit(solution)/shard_map/ppermute | solution.py:24
  21.0 9.9 %all-to-all-start.1 = ((bf16[8,32,128]{2,1,0:T(8,128)(2,1)}), bf16[8,32,128]{2,1,0:T(8,128)(2,1)S(1)}, u32[]{:S(2)}, u32[]{:S(2)}) async-start(bf16[8,32,128]{2,1,0:T(8,128)(2,1)} %get-tuple-element.28), calls=%async_computation.1 | async-start | bytes 131072 | tf_op jit(solution)/shard_map/all_to_all | solution.py:20
  33.6 9.6 %all-to-all-start.2 = ((bf16[8,64,128]{2,1,0:T(8,128)(2,1)}), bf16[8,64,128]{2,1,0:T(8,128)(2,1)S(1)}, u32[]{:S(2)}, u32[]{:S(2)}) async-start(bf16[8,64,128]{2,1,0:T(8,128)(2,1)} %cache.1.refs_2_), calls=%async_computation.2 | async-start | bytes 262144 | tf_op jit(solution)/shard_map/all_to_all | solution.py:20
  38.1 15.1 %collective-permute-start.1 = (bf16[2,1536,128]{2,1,0:T(8,128)(2,1)S(1)}, bf16[2,1536,128]{2,1,0:T(8,128)(2,1)S(1)}, u32[]{:S(2)}, u32[]{:S(2)}) collective-permute-start(bf16[2,1536,128]{2,1,0:T(8,128)(2,1)S(1)} %get-tuple-element.43.refs_0_.refs_1_), channel_id=1, source_target_pairs={{0,48},{8,24},{16,32},{24,8},{32,16},{40,56},{48,0},{56,40},{1,49}... | collective-permute-start | bytes 2359304 | tf_op jit(solution)/shard_map/ppermute | solution.py:24
  44.4 22.3 %all-to-all-start.3 = ((bf16[8,32,1024]{2,1,0:T(8,128)(2,1)}), bf16[8,32,1024]{2,1,0:T(8,128)(2,1)S(1)}, u32[]{:S(2)}, u32[]{:S(2)}) async-start(bf16[8,32,1024]{2,1,0:T(8,128)(2,1)} %finish.1.refs_2_), calls=%async_computation.3 | async-start | bytes 1048576 | tf_op jit(solution)/shard_map/all_to_all | solution.py:20
  53.2 0.9 %copy-start.1 = (bf16[2,1536,128]{2,1,0:T(8,128)(2,1)}, bf16[2,1536,128]{2,1,0:T(8,128)(2,1)S(1)}, u32[]{:S(2)}) copy-start(bf16[2,1536,128]{2,1,0:T(8,128)(2,1)S(1)} %collective-permute-done.1.refs_1_.refs_4_) | copy-start | bytes 2359300
  56.3 10.6 %collective-permute-start.2 = (bf16[4,1536,128]{2,1,0:T(8,128)(2,1)}, bf16[4,1536,128]{2,1,0:T(8,128)(2,1)S(1)}, u32[]{:S(2)}, u32[]{:S(2)}) collective-permute-start(bf16[4,1536,128]{2,1,0:T(8,128)(2,1)} %get-tuple-element.44), channel_id=1, source_target_pairs={{0,8},{8,0},{16,24},{24,16},{32,40},{40,32},{48,56},{56,48},{1,9},... | collective-permute-start | bytes 4718600 | tf_op jit(solution)/shard_map/ppermute | solution.py:24
  69.3 11.7 %all-to-all-start.4 = ((bf16[8,4,1024]{2,1,0:T(4,128)(2,1)}), bf16[8,4,1024]{2,1,0:T(4,128)(2,1)S(1)}, u32[]{:S(2)}, u32[]{:S(2)}) async-start(bf16[8,4,1024]{2,1,0:T(4,128)(2,1)} %feed.1), calls=%async_computation.4 | async-start | bytes 131072 | tf_op jit(solution)/shard_map/all_to_all | solution.py:20

commit v6 on v4

--- a/solution.py
+++ b/solution.py
@@ -409,7 +409,10 @@
     )
     high, low = two_terms(both)
     place = place_ref[...]
-    summed = matmul(place, high) + matmul(place, low)
+    half = place.shape[0] // 2
+    summed = jnp.concatenate(
+        [matmul(p, high) + matmul(p, low) for p in (place[:half], place[half:])], axis=0
+    )
     out_sum, total_sum = summed[:, :LANES], summed[:, LANES:]
     low_lanes = iota(out_sum.shape, 1) < HD
     top = jnp.where(low_lanes, tops[:, 0:1], tops[:, 1:2])

time: 82.3 us -> 82.3 us (level)
  no operation moved by 1% of the time
where the time goes in v6:
time: 82.3 us; the launch traced here: 81.4 us
  starting transfers between devices  37 us (45%)
  waiting for transfers between devices  25.4 us (31%)
  Pallas kernels  15 us (18%)
  local copies, waits for them, and re-layouts  2.94 us (4%)
  other arithmetic  0.94 us (1%)
    all_to_all x5, starting transfers between devices, exchange(): return lax.all_to_all(pieces, axes, 0, 0, tiled=True)  26.5 us
    all_to_all x5, waiting for transfers between devices, exchange(): return lax.all_to_all(pieces, axes, 0, 0, tiled=True)  21.7 us
    pallas_call x9, Pallas kernels, kernel_call(): call(*ins, *[stay_in_hbm(a.array) for a in (*loads, *small, *carried)])  12.8 us
    ppermute x3, starting transfers between devices, swapped(): return lax.ppermute(blocks, 'seq', list(enumerate(partner)))  10.5 us
    ppermute x3, waiting for transfers between devices, swapped(): return lax.ppermute(blocks, 'seq', list(enumerate(partner)))  3.73 us
    pallas_call x1, Pallas kernels, extended(): pl.pallas_call(lambda *refs: extend_body(None, *refs), out_shape=[jax.Sha...  2.21 us
  transfers between devices with their start and end apart: 8, of which 5 were waited for; matrix products, arithmetic and copies ran while one was open for 2% of the time, Pallas kernels for 15%

profile of v6, /device:TPU:56, one launch (start us, length us, event | category | flops | bytes accessed | tf_op | source)
XLA Modules:
  0.0 81.4 jit_solution(7007665469088956244)
XLA Ops:
  0.0 1.3 %broadcast_in_dim.8 = bf16[8,4,1024]{2,1,0:T(4,128)(2,1)} broadcast(bf16[4,1024]{1,0:T(4,128)(2,1)} %param.16), dimensions={1,2} | broadcast | bytes 73728 | tf_op jit(solution)/shard_map/broadcast_in_dim | solution.py:558
  1.3 10.3 %all-to-all-start = ((bf16[8,4,1024]{2,1,0:T(4,128)(2,1)}), bf16[8,4,1024]{2,1,0:T(4,128)(2,1)S(1)}, u32[]{:S(2)}, u32[]{:S(2)}) async-start(bf16[8,4,1024]{2,1,0:T(4,128)(2,1)} %broadcast_in_dim.8), calls=%async_computation | async-start | bytes 131072 | tf_op jit(solution)/shard_map/all_to_all | solution.py:20
  11.6 1.3 %pack.1 = (bf16[1,1536,128]{2,1,0:T(8,128)(2,1)S(1)}, bf16[3,1024,128]{2,1,0:T(8,128)(2,1)S(1)}, f32[1,1024]{1,0:T(1,128)S(1)}) custom-call(bf16[1024,128]{1,0:T(8,128)(2,1)} %bitcast.10, bf16[64,1024]{1,0:T(8,128)(2,1)} %bitcast.11, bf16[3,1024,128]{2,1,0:T(8,128)(2,1)} %bitcast.9, f32[1,1024]{1,0:T(1,128)} %bitcast.12), custom_call_target="tpu_custom_call" | custom-call | flops 314572800 | bytes 1048576 | tf_op jit(solution)/shard_map/pack/pallas_call | solution.py:95
  13.0 3.5 %collective-permute-start = (bf16[1,1536,128]{2,1,0:T(8,128)(2,1)S(1)}, bf16[1,1536,128]{2,1,0:T(8,128)(2,1)}, u32[]{:S(2)}, u32[]{:S(2)}) collective-permute-start(bf16[1,1536,128]{2,1,0:T(8,128)(2,1)S(1)} %get-tuple-element.37.refs_0_), channel_id=1, source_target_pairs={{0,16},{8,56},{16,0},{24,40},{32,48},{40,24},{48,32},{56,8},{1,17}... | collective-permute-start | bytes 1179656 | tf_op jit(solution)/shard_map/ppermute | solution.py:24
  17.3 0.9 %fusion = (f32[8,4,128]{2,1,0:T(4,128)S(1)}, f32[8,4,128]{2,1,0:T(4,128)S(1)}) fusion(f32[128]{0:T(128)} %constant.18.clone, f32[128]{0:T(128)} %constant.17.clone, f32[8,4]{1,0:T(8,128)S(1)} %add_convert_fusion), kind=kLoop, calls=%fused_computation.2 | loop fusion | flops 8192 | bytes 33920 | tf_op jit(solution)/shard_map/mul | solution.py:527
  18.2 1.8 %all-to-all-done.refs_0_.refs_1_ = bf16[8,4,1024]{2,1,0:T(4,128)(2,1)S(1)} async-done(((bf16[8,4,1024]{2,1,0:T(4,128)(2,1)}), bf16[8,4,1024]{2,1,0:T(4,128)(2,1)S(1)}, u32[]{:S(2)}, u32[]{:S(2)}) %all-to-all-start) | async-done | bytes 65568 | tf_op jit(solution)/shard_map/all_to_all | solution.py:20
  20.0 0.9 %project.1 = (bf16[8,32,128]{2,1,0:T(8,128)(2,1)}, bf16[32,128]{1,0:T(8,128)(2,1)S(1)}, bf16[32,128]{1,0:T(8,128)(2,1)S(1)}) custom-call(bf16[8,4,1024]{2,1,0:T(4,128)(2,1)S(1)} %all-to-all-done.refs_0_.refs_1_, f32[8,4,128]{2,1,0:T(4,128)S(1)} %get-tuple-element.46.refs_1_, f32[8,4,128]{2,1,0:T(4,128)S(1)} %get-tuple-element.45.refs_2_, ...), custom_call_target="tpu_custom_call" | custom-call | flops 314572800 | bytes 1048576 | tf_op jit(solution)/shard_map/project/pallas_call | solution.py:95
  21.0 4.3 %all-to-all-start.1 = ((bf16[8,32,128]{2,1,0:T(8,128)(2,1)}), bf16[8,32,128]{2,1,0:T(8,128)(2,1)S(1)}, u32[]{:S(2)}, u32[]{:S(2)}) async-start(bf16[8,32,128]{2,1,0:T(8,128)(2,1)} %get-tuple-element.27.refs_1_), calls=%async_computation.1 | async-start | bytes 131072 | tf_op jit(solution)/shard_map/all_to_all | solution.py:20
  25.3 2.5 %prepare.1 = (bf16[192,256]{1,0:T(8,128)(2,1)S(1)}, bf16[256,192]{1,0:T(8,128)(2,1)S(1)}, bf16[192,192]{1,0:T(8,128)(2,1)S(1)}, f32[192,256]{1,0:T(8,128)S(1)}, ...) custom-call(s32[1]{0:T(128)} %bitcast.5.refs_0_, ...), custom_call_target="tpu_custom_call" | custom-call | flops 314572800 | bytes 1048576 | tf_op jit(solution)/shard_map/prepare/pallas_call | solution.py:95
  27.7 3.2 %all-to-all-done.1.refs_0_ = bf16[8,32,128]{2,1,0:T(8,128)(2,1)S(1)} async-done(((bf16[8,32,128]{2,1,0:T(8,128)(2,1)}), bf16[8,32,128]{2,1,0:T(8,128)(2,1)S(1)}, u32[]{:S(2)}, u32[]{:S(2)}) %all-to-all-start.1) | async-done | bytes 65568 | tf_op jit(solution)/shard_map/all_to_all | solution.py:20
  30.9 2.6 %cache.1.refs_2_ = bf16[8,64,128]{2,1,0:T(8,128)(2,1)} custom-call(bf16[8,32,128]{2,1,0:T(8,128)(2,1)S(1)} %all-to-all-done.1.refs_0_, bf16[192,256]{1,0:T(8,128)(2,1)S(1)} %get-tuple-element.30.refs_1_, bf16[256,192]{1,0:T(8,128)(2,1)S(1)} %get-tuple-element.31.refs_2_, bf16[192,192]{1,0:T(8,128)(2,1)S(1)} %get-tuple-element.32.refs_3_, ...), custom_call_target="tpu_custom_call" | custom-call | flops 1258291200 | bytes 4194304 | tf_op jit(solution)/shard_map/cache/pallas_call | solution.py:95
  33.5 3.4 %all-to-all-start.2 = ((bf16[8,64,128]{2,1,0:T(8,128)(2,1)}), bf16[8,64,128]{2,1,0:T(8,128)(2,1)S(1)}, u32[]{:S(2)}, u32[]{:S(2)}) async-start(bf16[8,64,128]{2,1,0:T(8,128)(2,1)} %cache.1.refs_2_), calls=%async_computation.2 | async-start | bytes 262144 | tf_op jit(solution)/shard_map/all_to_all | solution.py:20
  36.9 1.1 %join.1 = (bf16[2,1536,128]{2,1,0:T(8,128)(2,1)S(1)}, bf16[128,1024]{1,0:T(8,128)(2,1)S(1)}, f32[1,1024]{1,0:T(1,128)S(1)}) custom-call(bf16[1,1536,128]{2,1,0:T(8,128)(2,1)S(1)} %get-tuple-element.37.refs_0_, bf16[1,1536,128]{2,1,0:T(8,128)(2,1)} %collective-permute-done.refs_1_, bf16[8,64,128]{2,1,0:T(8,128)(2,1)} %cache.1.refs_2_, ...), custom_call_target="tpu_custom_call" | custom-call | flops 1258291200 | bytes 4194304 | tf_op jit(solution)/shard_map/join/pallas_call | solution.py:95
  38.0 5.1 %collective-permute-start.1 = (bf16[2,1536,128]{2,1,0:T(8,128)(2,1)S(1)}, bf16[2,1536,128]{2,1,0:T(8,128)(2,1)S(1)}, u32[]{:S(2)}, u32[]{:S(2)}) collective-permute-start(bf16[2,1536,128]{2,1,0:T(8,128)(2,1)S(1)} %get-tuple-element.41.refs_0_.refs_1_), channel_id=1, source_target_pairs={{0,48},{8,24},{16,32},{24,8},{32,16},{40,56},{48,0},{56,40},{1,49}... | collective-permute-start | bytes 2359304 | tf_op jit(solution)/shard_map/ppermute | solution.py:24
  43.1 1.2 %finish.1.refs_2_ = bf16[8,32,1024]{2,1,0:T(8,128)(2,1)} custom-call(bf16[8,64,128]{2,1,0:T(8,128)(2,1)S(1)} %all-to-all-done.2.refs_0_, f32[32,128]{1,0:T(8,128)S(1)} %get-tuple-element.35.refs_1_, f32[32,128]{1,0:T(8,128)S(1)} %get-tuple-element.36.refs_2_, bf16[128,1024]{1,0:T(8,128)(2,1)S(1)} %get-tuple-element.38.refs_3_), custom_call_target="tpu_custom_call" | custom-call | flops 9437184000 | bytes 31457280 | tf_op jit(solution)/shard_map/finish/pallas_call | solution.py:95
  44.3 5.1 %all-to-all-start.3 = ((bf16[8,32,1024]{2,1,0:T(8,128)(2,1)}), bf16[8,32,1024]{2,1,0:T(8,128)(2,1)S(1)}, u32[]{:S(2)}, u32[]{:S(2)}) async-start(bf16[8,32,1024]{2,1,0:T(8,128)(2,1)} %finish.1.refs_2_), calls=%async_computation.3 | async-start | bytes 1048576 | tf_op jit(solution)/shard_map/all_to_all | solution.py:20
  49.4 3.7 %collective-permute-done.1.refs_1_.refs_4_ = bf16[2,1536,128]{2,1,0:T(8,128)(2,1)S(1)} collective-permute-done((bf16[2,1536,128]{2,1,0:T(8,128)(2,1)S(1)}, bf16[2,1536,128]{2,1,0:T(8,128)(2,1)S(1)}, u32[]{:S(2)}, u32[]{:S(2)}) %collective-permute-start.1) | collective-permute-done | bytes 786464 | tf_op jit(solution)/shard_map/ppermute | solution.py:24
  53.1 0.9 %copy-done.1 = bf16[2,1536,128]{2,1,0:T(8,128)(2,1)} copy-done((bf16[2,1536,128]{2,1,0:T(8,128)(2,1)}, bf16[2,1536,128]{2,1,0:T(8,128)(2,1)S(1)}, u32[]{:S(2)}) %copy-start.1) | copy-done | bytes 786456
  54.0 2.2 %extend.1 = (bf16[4,1536,128]{2,1,0:T(8,128)(2,1)}, bf16[1,1536,128]{2,1,0:T(8,128)(2,1)S(1)}) custom-call(bf16[2,1536,128]{2,1,0:T(8,128)(2,1)S(1)} %get-tuple-element.41.refs_0_.refs_1_, bf16[2,1536,128]{2,1,0:T(8,128)(2,1)} %copy-done.1, bf16[8,32,1024]{2,1,0:T(8,128)(2,1)} %finish.1.refs_2_), custom_call_target="tpu_custom_call" | custom-call | flops 1258291200 | bytes 4194304 | tf_op jit(solution)/shard_map/extend/pallas_call | solution.py:172
  56.2 1.9 %collective-permute-start.2 = (bf16[4,1536,128]{2,1,0:T(8,128)(2,1)}, bf16[4,1536,128]{2,1,0:T(8,128)(2,1)S(1)}, u32[]{:S(2)}, u32[]{:S(2)}) collective-permute-start(bf16[4,1536,128]{2,1,0:T(8,128)(2,1)} %get-tuple-element.42), channel_id=1, source_target_pairs={{0,8},{8,0},{16,24},{24,16},{32,40},{40,32},{48,56},{56,48},{1,9},... | collective-permute-start | bytes 4718600 | tf_op jit(solution)/shard_map/ppermute | solution.py:24
  58.1 8.4 %all-to-all-done.3.refs_0_ = bf16[8,32,1024]{2,1,0:T(8,128)(2,1)S(1)} async-done(((bf16[8,32,1024]{2,1,0:T(8,128)(2,1)}), bf16[8,32,1024]{2,1,0:T(8,128)(2,1)S(1)}, u32[]{:S(2)}, u32[]{:S(2)}) %all-to-all-start.3) | async-done | bytes 524320 | tf_op jit(solution)/shard_map/all_to_all | solution.py:20
  66.7 2.4 %feed.1 = bf16[8,4,1024]{2,1,0:T(4,128)(2,1)} custom-call(bf16[32,1024]{1,0:T(8,128)(2,1)S(1)} %get-tuple-element.40.refs_0_, bf16[2,1536,128]{2,1,0:T(8,128)(2,1)S(1)} %get-tuple-element.41.refs_0_.refs_1_, bf16[4,1536,128]{2,1,0:T(8,128)(2,1)S(1)} %collective-permute-done.2.refs_2_, bf16[1,1536,128]{2,1,0:T(8,128)(2,1)S(1)} %get-tuple-element.43.refs_3_, ...), custom_call_target="tpu_custom_call" | custom-call | flops 1258291200 | bytes 4194304 | tf_op jit(solution)/shard_map/feed/pallas_call | solution.py:95
  69.1 3.4 %all-to-all-start.4 = ((bf16[8,4,1024]{2,1,0:T(4,128)(2,1)}), bf16[8,4,1024]{2,1,0:T(4,128)(2,1)S(1)}, u32[]{:S(2)}, u32[]{:S(2)}) async-start(bf16[8,4,1024]{2,1,0:T(4,128)(2,1)} %feed.1), calls=%async_computation.4 | async-start | bytes 131072 | tf_op jit(solution)/shard_map/all_to_all | solution.py:20
  72.5 8.3 %all-to-all-done.4.refs_1_ = bf16[8,4,1024]{2,1,0:T(4,128)(2,1)S(1)} async-done(((bf16[8,4,1024]{2,1,0:T(4,128)(2,1)}), bf16[8,4,1024]{2,1,0:T(4,128)(2,1)S(1)}, u32[]{:S(2)}, u32[]{:S(2)}) %all-to-all-start.4) | async-done | bytes 65568 | tf_op jit(solution)/shard_map/all_to_all | solution.py:20
  (10 shorter events, 1.6 us)
Async XLA Ops:
  1.3 18.7 %all-to-all-start = ((bf16[8,4,1024]{2,1,0:T(4,128)(2,1)}), bf16[8,4,1024]{2,1,0:T(4,128)(2,1)S(1)}, u32[]{:S(2)}, u32[]{:S(2)}) async-start(bf16[8,4,1024]{2,1,0:T(4,128)(2,1)} %broadcast_in_dim.8), calls=%async_computation | async-start | bytes 131072 | tf_op jit(solution)/shard_map/all_to_all | solution.py:20
  13.0 17.9 %copy-start = (bf16[24,256,128]{2,1,0:T(8,128)(2,1)S(1)}, bf16[24,256,128]{2,1,0:T(8,128)(2,1)}, u32[]{:S(2)}) copy-start(bf16[24,256,128]{2,1,0:T(8,128)(2,1)} %refs_5_.1) | copy-start | bytes 4718596
  13.0 23.9 %collective-permute-start = (bf16[1,1536,128]{2,1,0:T(8,128)(2,1)S(1)}, bf16[1,1536,128]{2,1,0:T(8,128)(2,1)}, u32[]{:S(2)}, u32[]{:S(2)}) collective-permute-start(bf16[1,1536,128]{2,1,0:T(8,128)(2,1)S(1)} %get-tuple-element.37.refs_0_), channel_id=1, source_target_pairs={{0,16},{8,56},{16,0},{24,40},{32,48},{40,24},{48,32},{56,8},{1,17}... | collective-permute-start | bytes 1179656 | tf_op jit(solution)/shard_map/ppermute | solution.py:24
  21.0 9.9 %all-to-all-start.1 = ((bf16[8,32,128]{2,1,0:T(8,128)(2,1)}), bf16[8,32,128]{2,1,0:T(8,128)(2,1)S(1)}, u32[]{:S(2)}, u32[]{:S(2)}) async-start(bf16[8,32,128]{2,1,0:T(8,128)(2,1)} %get-tuple-element.27.refs_1_), calls=%async_computation.1 | async-start | bytes 131072 | tf_op jit(solution)/shard_map/all_to_all | solution.py:20
  33.5 9.6 %all-to-all-start.2 = ((bf16[8,64,128]{2,1,0:T(8,128)(2,1)}), bf16[8,64,128]{2,1,0:T(8,128)(2,1)S(1)}, u32[]{:S(2)}, u32[]{:S(2)}) async-start(bf16[8,64,128]{2,1,0:T(8,128)(2,1)} %cache.1.refs_2_), calls=%async_computation.2 | async-start | bytes 262144 | tf_op jit(solution)/shard_map/all_to_all | solution.py:20
  38.0 15.1 %collective-permute-start.1 = (bf16[2,1536,128]{2,1,0:T(8,128)(2,1)S(1)}, bf16[2,1536,128]{2,1,0:T(8,128)(2,1)S(1)}, u32[]{:S(2)}, u32[]{:S(2)}) collective-permute-start(bf16[2,1536,128]{2,1,0:T(8,128)(2,1)S(1)} %get-tuple-element.41.refs_0_.refs_1_), channel_id=1, source_target_pairs={{0,48},{8,24},{16,32},{24,8},{32,16},{40,56},{48,0},{56,40},{1,49}... | collective-permute-start | bytes 2359304 | tf_op jit(solution)/shard_map/ppermute | solution.py:24
  44.3 22.3 %all-to-all-start.3 = ((bf16[8,32,1024]{2,1,0:T(8,128)(2,1)}), bf16[8,32,1024]{2,1,0:T(8,128)(2,1)S(1)}, u32[]{:S(2)}, u32[]{:S(2)}) async-start(bf16[8,32,1024]{2,1,0:T(8,128)(2,1)} %finish.1.refs_2_), calls=%async_computation.3 | async-start | bytes 1048576 | tf_op jit(solution)/shard_map/all_to_all | solution.py:20
  53.1 0.9 %copy-start.1 = (bf16[2,1536,128]{2,1,0:T(8,128)(2,1)}, bf16[2,1536,128]{2,1,0:T(8,128)(2,1)S(1)}, u32[]{:S(2)}) copy-start(bf16[2,1536,128]{2,1,0:T(8,128)(2,1)S(1)} %collective-permute-done.1.refs_1_.refs_4_) | copy-start | bytes 2359300
  56.2 10.5 %collective-permute-start.2 = (bf16[4,1536,128]{2,1,0:T(8,128)(2,1)}, bf16[4,1536,128]{2,1,0:T(8,128)(2,1)S(1)}, u32[]{:S(2)}, u32[]{:S(2)}) collective-permute-start(bf16[4,1536,128]{2,1,0:T(8,128)(2,1)} %get-tuple-element.42), channel_id=1, source_target_pairs={{0,8},{8,0},{16,24},{24,16},{32,40},{40,32},{48,56},{56,48},{1,9},... | collective-permute-start | bytes 4718600 | tf_op jit(solution)/shard_map/ppermute | solution.py:24
  69.1 11.7 %all-to-all-start.4 = ((bf16[8,4,1024]{2,1,0:T(4,128)(2,1)}), bf16[8,4,1024]{2,1,0:T(4,128)(2,1)S(1)}, u32[]{:S(2)}, u32[]{:S(2)}) async-start(bf16[8,4,1024]{2,1,0:T(4,128)(2,1)} %feed.1), calls=%async_computation.4 | async-start | bytes 131072 | tf_op jit(solution)/shard_map/all_to_all | solution.py:20
